TPU v7x, 32 devices: a whole 2x2x4 slice. The times are simulated.
32 devices in a mesh: fsdp: 4 (over y, core), dp: 8 (over z, x).
Axes of the slice: x: 2, y: 2, z: 4, core: 2. Of those that a mesh axis runs over, the one named last changes fastest.
Arguments:
- tokens: bfloat16 [8, 2048, 768], P('fsdp', 'dp'), may hold values from -6 to 6
- segments: int32 [8, 2048], P('fsdp'), may hold values from 0 to 2, never falling along the last dimension, each value on 1 to 2000 neighbouring positions
- ln1_gain: bfloat16 [768], P('fsdp'), may hold values from 0.5 to 1.5
- ln1_bias: bfloat16 [768], P('fsdp'), may hold values from -1.75 to 1.75
- w_query: bfloat16 [768, 768], P('fsdp'), may hold values from -0.21875 to 0.21875
- w_key: bfloat16 [768, 768], P('fsdp'), may hold values from -0.21875 to 0.21875
- w_value: bfloat16 [768, 768], P('fsdp'), may hold values from -0.21875 to 0.21875
- shift_taps: bfloat16 [64, 768], P(None, 'fsdp'), may hold values from -0.75 to 0.75
- ssm_rate: bfloat16 [12, 32], P('fsdp'), may hold values from 0.0009994507 to 0.099609375
- ssm_freq: bfloat16 [12, 32], P('fsdp'), may hold values from -0.29882812 to 0.29882812
- ssm_coef: bfloat16 [2, 12, 32], P(None, 'fsdp'), may hold values from -0.01171875 to 0.01171875
- ssm_skip: bfloat16 [12], P('fsdp'), may hold values from -0.625 to 0.625
- w_out: bfloat16 [768, 768], P('fsdp'), may hold values from -0.21875 to 0.21875
- ln2_gain: bfloat16 [768], P('fsdp'), may hold values from 0.5 to 1.5
- ln2_bias: bfloat16 [768], P('fsdp'), may hold values from -1.75 to 1.75
- w_up: bfloat16 [768, 3072], P('fsdp'), may hold values from -0.21875 to 0.21875
- w_down: bfloat16 [3072, 768], P('fsdp'), may hold values from -0.109375 to 0.109375
- cotangent: bfloat16 [8, 2048, 768], P('fsdp', 'dp'), may hold values from -6 to 6
Outputs:
- output: bfloat16 [8, 2048, 768], P('fsdp', 'dp')
- input_grad: bfloat16 [8, 2048, 768], P('fsdp', 'dp')
- ln1_gain_grad: float32 [768], P('fsdp')
- ln1_bias_grad: float32 [768], P('fsdp')
- w_query_grad: float32 [768, 768], P('fsdp')
- w_key_grad: float32 [768, 768], P('fsdp')
- w_value_grad: float32 [768, 768], P('fsdp')
- shift_taps_grad: float32 [64, 768], P(None, 'fsdp')
- ssm_rate_grad: float32 [12, 32], P('fsdp')
- ssm_freq_grad: float32 [12, 32], P('fsdp')
- ssm_coef_grad: float32 [2, 12, 32], P(None, 'fsdp')
- ssm_skip_grad: float32 [12], P('fsdp')
- w_out_grad: float32 [768, 768], P('fsdp')
- ln2_gain_grad: float32 [768], P('fsdp')
- ln2_bias_grad: float32 [768], P('fsdp')
- w_up_grad: float32 [768, 3072], P('fsdp')
- w_down_grad: float32 [3072, 768], P('fsdp')
Inputs may be any that keep to these rules, and one draw needn't show every extreme that they name: `segments`: along each row the document numbers never fall; each document has 1 to 2000 tokens and some document in each row exactly 2000.
All inputs are finite; a program needn't handle non-finite values.
Results may differ from a plain program's by a relative error of at most 0.014.
Values may be sent and summed in bfloat16 or wider, within the bound.
No kernel may reach another device: no remote copies, remote signals or barrier semaphores. Data moves between devices by JAX's collectives and lax.ppermute only.
A program may use at most 256 MiB of HBM per device.

v0:
```python
import functools

import jax
import jax.numpy as jnp
import numpy as np
from jax import lax
from jax.experimental import pallas as pl
from jax.experimental.pallas import tpu as pltpu
from jax.sharding import PartitionSpec as P

SHIFT = 64
HOPS = 8
TILE = 256
HALO = 64
EPS = 1e-05
BF = jnp.bfloat16
F32 = jnp.float32
VMEM_BYTES = 56 * 1024 * 1024


def vmem():
    return pl.BlockSpec(memory_space=pltpu.VMEM)


def smem():
    return pl.BlockSpec(memory_space=pltpu.SMEM)


def hbm():
    return pl.BlockSpec(memory_space=pl.ANY)


def params():
    return pltpu.CompilerParams(vmem_limit_bytes=VMEM_BYTES)


SCALE = 1000


def cost(micros, moved):
    return pl.CostEstimate(
        flops=int(micros * 1.0e9) // SCALE, bytes_accessed=int(moved) // (8 * SCALE), transcendentals=0
    )


def mm(left, right):
    return lax.dot_general(left, right, (((1,), (0,)), ((), ())), preferred_element_type=F32)


def mm_nt(left, right):
    return lax.dot_general(left, right, (((1,), (1,)), ((), ())), preferred_element_type=F32)


def tn(left, right):
    return lax.dot_general(left, right, (((0,), (0,)), ((), ())), preferred_element_type=F32)


def cut_lanes(width, rows):
    tiles = [(base, 128, rows, False) for base in range(0, width - 127, 128)]
    if width % 128:
        assert width % 128 == 64
        tiles.append((width - 64, 64, rows // 2, True))
    return tiles


def fill_ext_t(ext, source, halo, width, lead):
    rows = source.shape[0] * TILE
    first = HALO if lead else 0
    for index, (base, size, span, packed) in enumerate(cut_lanes(width, rows)):
        halo_at = 0 if lead else span
        blocks = span // TILE
        sides = [(0, 0)] + ([(64, span)] if packed else [])
        for lane, token in sides:
            lanes = slice(lane, lane + size)
            for block in range(blocks):
                part = source[token // TILE + block, base : base + size, :].astype(F32).T
                ext[index, first + block * TILE : first + (block + 1) * TILE, lanes] = part
            if lead and token:
                part = source[token // TILE - 1, base : base + size, TILE - 128 :].astype(F32).T[128 - HALO :]
            else:
                part = halo[:, base : base + size].astype(F32)
            ext[index, halo_at : halo_at + HALO, lanes] = part


def fill_ext(ext, source, halo, width):
    rows = source.shape[0]
    for index, (base, size, span, packed) in enumerate(cut_lanes(width, rows)):
        features = slice(base, base + size)
        if packed:
            ext[index, 0 : span + HALO, 0:size] = source[0 : span + HALO, features]
            ext[index, 0:span, size : 2 * size] = source[span:rows, features]
            ext[index, span : span + HALO, size : 2 * size] = halo[:, features]
        else:
            ext[index, 0:span, :] = source[:, features]
            ext[index, span : span + HALO, :] = halo[:, features]


def fill_segments(seg_b, seg_p, column):
    total = column.shape[0]
    seg_b[...] = jnp.broadcast_to(column[...], seg_b.shape)
    if seg_p is not None:
        half = seg_p.shape[0]
        seg_p[:, 0:64] = seg_b[0:half, 0:64]
        seg_p[:, 64:128] = seg_b[total - half : total, 64:128]


def windows(source, index, start, way):
    for fine in range(8):
        if way < 0:
            window = source[index, pl.ds(start + HALO - 56 - fine, 120), :]
        else:
            window = source[index, pl.ds(start + fine, 120), :]
        for coarse in range(SHIFT // 8):
            at = 56 - 8 * coarse if way < 0 else 8 * coarse
            yield 8 * coarse + fine, window[at : at + 64]


def seg_windows(seg_b, start, way):
    for fine in range(8):
        if way < 0:
            window = seg_b[pl.ds(start + HALO - 56 - fine, 120), :]
        else:
            window = seg_b[pl.ds(start + HALO + fine, 120), :]
        for coarse in range(SHIFT // 8):
            at = 56 - 8 * coarse if way < 0 else 8 * coarse
            yield window[at : at + 64]


def filtered(source, index, start, taps_ref, seg, way, clear):
    def plain():
        total = jnp.zeros((64, 128), F32)
        for lag, part in windows(source, index, start, way):
            total = total + part * taps_ref[index, lag : lag + 1, :]
        return total

    def masked():
        total = jnp.zeros((64, 128), F32)
        now = seg[pl.ds(start + HALO, 64), :]
        pairs = zip(windows(source, index, start, way), seg_windows(seg, start, way))
        for (lag, part), there in pairs:
            total = total + jnp.where(there == now, part * taps_ref[index, lag : lag + 1, :], 0.0)
        return total

    return lax.cond(clear, plain, masked)


def all_same(seg_s, start, first, last, packed, span):
    same = seg_s[start + first] == seg_s[start + last]
    if packed:
        same = jnp.logical_and(same, seg_s[span + start + first] == seg_s[span + start + last])
    return same


def shift_fwd_kernel(seg_s, k_ref, halo_ref, taps_ref, segcol_ref, out_ref, ext, seg_b, seg_p):
    width = k_ref.shape[1]
    rows = k_ref.shape[0] * TILE
    fill_ext_t(ext, k_ref, halo_ref, width, True)
    fill_segments(seg_b, seg_p, segcol_ref)
    for index, (base, size, span, packed) in enumerate(cut_lanes(width, rows)):

        def body(tile, carry):
            start = pl.multiple_of(tile * 64, 64)
            clear = all_same(seg_s, start, 1, HALO + 63, packed, span)
            total = filtered(ext, index, start, taps_ref, seg_p if packed else seg_b, -1, clear)
            out_ref[pl.ds(start, 64), base : base + size] = total[:, 0:size].astype(BF)
            if packed:
                out_ref[pl.ds(start + span, 64), base : base + size] = total[:, size:].astype(BF)
            return carry

        lax.fori_loop(0, span // 64, body, 0)


def lane_taps(taps):
    tiles = []
    for base, size, _, packed in cut_lanes(taps.shape[1], 0):
        part = taps[:, base : base + size]
        tiles.append(jnp.concatenate([part, part], axis=1) if packed else part)
    return jnp.stack(tiles)


def shift_fwd(seg_full, k_own, k_halo, taps):
    count, width, _ = k_own.shape
    rows = count * TILE
    tiles = len(cut_lanes(width, rows))
    return pl.pallas_call(
        shift_fwd_kernel,
        out_shape=jax.ShapeDtypeStruct((rows, width), BF),
        in_specs=[smem(), vmem(), vmem(), vmem(), vmem()],
        out_specs=vmem(),
        scratch_shapes=[
            pltpu.VMEM((tiles, HALO + rows, 128), F32),
            pltpu.VMEM((2 * HALO + rows, 128), jnp.int32),
            pltpu.VMEM((2 * HALO + rows // 2, 128), jnp.int32),
        ],
        compiler_params=params(),
        cost_estimate=cost(10, 2 << 20),
        name="shift_fwd",
    )(seg_full, k_own, k_halo, taps, seg_full[:, None])


def shift_bwd_kernel(
    seg_s, k_ref, halo_ref, g_ref, ghalo_ref, taps_ref, segcol_ref, tg_ref, out_ref,
    ext, gext, seg_b, seg_p, acc, gk_rows,
):
    width = k_ref.shape[1]
    rows = k_ref.shape[0] * TILE
    fill_ext_t(ext, k_ref, halo_ref, width, True)
    fill_ext(gext, g_ref, ghalo_ref, width)
    fill_segments(seg_b, seg_p, segcol_ref)
    acc[...] = jnp.zeros_like(acc)

    def fold(part):
        total = part[0:8]
        for piece in range(1, 8):
            total = total + part[8 * piece : 8 * piece + 8]
        return total

    for index, (base, size, span, packed) in enumerate(cut_lanes(width, rows)):
        seg = seg_p if packed else seg_b

        def body(tile, carry):
            start = pl.multiple_of(tile * 64, 64)
            clear = all_same(seg_s, start, HALO, HALO + 126, packed, span)
            gk_rows[index, pl.ds(start, 64), :] = filtered(gext, index, start, taps_ref, seg, 1, clear)
            grad = gext[index, pl.ds(start, 64), :]
            clear = all_same(seg_s, start, 1, HALO + 63, packed, span)

            @pl.when(clear)
            def _():
                for lag, part in windows(ext, index, start, -1):
                    acc[index, lag] += fold(part * grad)

            @pl.when(jnp.logical_not(clear))
            def _():
                now = seg[pl.ds(start + HALO, 64), :]
                pairs = zip(windows(ext, index, start, -1), seg_windows(seg, start, -1))
                for (lag, part), there in pairs:
                    acc[index, lag] += fold(jnp.where(there == now, part * grad, 0.0))

            return carry

        lax.fori_loop(0, span // 64, body, 0)
        line = jnp.sum(acc[index], axis=1)
        if packed:
            line = line[:, 0:size] + line[:, size:]
        tg_ref[:, base : base + size] = line
        blocks = span // TILE
        for block in range(rows // TILE):
            at = (block % blocks) * TILE
            part = gk_rows[index, at : at + TILE, :].T
            lane = (block // blocks) * size
            out_ref[block, base : base + size, :] = part[lane : lane + size].astype(BF)


def shift_bwd(seg_full, k_own, k_halo, grad, grad_halo, taps):
    count, width, _ = k_own.shape
    rows = count * TILE
    tiles = len(cut_lanes(width, rows))
    return pl.pallas_call(
        shift_bwd_kernel,
        out_shape=(
            jax.ShapeDtypeStruct((SHIFT, width), F32),
            jax.ShapeDtypeStruct(k_own.shape, BF),
        ),
        in_specs=[smem()] + [vmem()] * 6,
        out_specs=(vmem(),) * 2,
        scratch_shapes=[
            pltpu.VMEM((tiles, HALO + rows, 128), F32),
            pltpu.VMEM((tiles, HALO + rows, 128), F32),
            pltpu.VMEM((2 * HALO + rows, 128), jnp.int32),
            pltpu.VMEM((2 * HALO + rows // 2, 128), jnp.int32),
            pltpu.VMEM((tiles, SHIFT, 8, 128), F32),
            pltpu.VMEM((tiles, rows, 128), F32),
        ],
        compiler_params=params(),
        cost_estimate=cost(20, 4 << 20),
        name="shift_bwd",
    )(seg_full, k_own, k_halo, grad, grad_halo, taps, seg_full[:, None])


def build_bands(bands, row):
    length = row.shape[1]
    skewed = pltpu.roll(jnp.broadcast_to(row, (8, length)), 0, 1, stride=1, stride_axis=0)
    for step in range(16):
        bands[step] = pltpu.roll(skewed, 8 * step, 1) if step else skewed


def band_parts(distance, first, count):
    parts = []
    for row in range(first, first + count, 128):
        high = min(128, first + count - row)
        lane = TILE * (1 + distance) - (row // 128) * 128
        parts.append((slice((row % 128) // 8, (row % 128 + high) // 8), slice(lane, lane + TILE), high))
    return parts


def read_band(bands, parts):
    pieces = [bands[steps, :, lanes].reshape(high, TILE) for steps, lanes, high in parts]
    return pieces[0] if len(pieces) == 1 else jnp.concatenate(pieces, axis=0)


def alike(seg_b, rows, seg_line):
    now = seg_b[rows, :]
    return jnp.concatenate([now, now], axis=1) == seg_line


def head_rows(dest, source, heads, size):
    for head in range(heads):
        dest[head] = source[:, head * size : (head + 1) * size]


def head_turn(dest, source, heads, size, base=0):
    for head in range(heads):
        for block in range(source.shape[0]):
            part = source[block, base + head * size : base + (head + 1) * size, :].astype(F32)
            dest[head, block * TILE : (block + 1) * TILE, :] = part.T.astype(dest.dtype)


STRIP = 64


def mix_fwd_kernel(v_base, q_ref, k_ref, v_ref, row_ref, segq_ref, segk_ref, y_ref, kh, bands, seg_b):
    heads = row_ref.shape[0]
    size = k_ref.shape[1] // heads
    query_blocks, key_blocks = q_ref.shape[0], v_ref.shape[0]
    offset = key_blocks - query_blocks
    head_rows(kh, k_ref, heads, size)
    seg_b[...] = jnp.broadcast_to(segk_ref[...], seg_b.shape)

    def head_body(head, carry):
        build_bands(bands, row_ref[head])
        own = pl.ds(pl.multiple_of(head * size, size), size)
        own_v = pl.ds(pl.multiple_of(v_base + head * size, size), size)
        for row in range(query_blocks):
            query = q_ref[row, own, :]
            total = jnp.zeros((size, TILE), F32)
            for col in range(max(0, row + offset - HOPS), row + offset + 1):
                for first in range(0, TILE, STRIP):
                    kern = read_band(bands, band_parts(row + offset - col, first, STRIP))
                    rows = slice(col * TILE + first, col * TILE + first + STRIP)
                    weight = mm(kh[head, rows, :], query) * kern
                    weight = jnp.where(alike(seg_b, rows, segq_ref[row]), weight, 0.0).astype(BF)
                    total = total + mm(v_ref[col, own_v, first : first + STRIP], weight)
            y_ref[row, own, :] = total.astype(BF)
        return carry

    lax.fori_loop(0, heads, head_body, 0)


def mix_fwd(q, k_win, v_win, kern_asc, seg_q, seg_k):
    blocks = q.shape[0]
    wide, width = k_win.shape
    shape = (blocks, width, TILE)
    heads, _, length = kern_asc.shape
    size = width // heads
    return pl.pallas_call(
        functools.partial(mix_fwd_kernel, v_win.shape[1] - width),
        out_shape=jax.ShapeDtypeStruct(shape, BF),
        in_specs=[vmem()] * 6,
        out_specs=vmem(),
        scratch_shapes=[
            pltpu.VMEM((heads, wide, size), BF),
            pltpu.VMEM((16, 8, length), F32),
            pltpu.VMEM((wide, 128), jnp.int32),
        ],
        compiler_params=params(),
        cost_estimate=cost(20, 4 << 20),
        name="mix_fwd",
    )(q, k_win, v_win, kern_asc, seg_q.reshape(blocks, 1, TILE), seg_k[:, None])


def mix_bwd_kernel(
    v_base, q_ref, k_ref, v_ref, g_ref, row_ref, segq_ref, segk_ref, gq_ref, gk_ref, gv_ref, gkern_ref,
    qh, kh, vh, gh, kt, gqt, gkacc, gvacc, bands, gbands, seg_b,
):
    heads, length = row_ref.shape[0], row_ref.shape[2]
    size = k_ref.shape[1] // heads
    query_blocks, key_blocks = q_ref.shape[0], v_ref.shape[0]
    offset = key_blocks - query_blocks
    head_turn(qh, q_ref, heads, size)
    head_rows(kh, k_ref, heads, size)
    head_turn(vh, v_ref, heads, size, v_base)
    head_turn(gh, g_ref, heads, size)
    for head in range(heads):
        for block in range(key_blocks):
            part = kh[head, block * TILE : (block + 1) * TILE, :].astype(F32)
            kt[block, head * size : (head + 1) * size, :] = part.T.astype(BF)
    seg_b[...] = jnp.broadcast_to(segk_ref[...], seg_b.shape)
    gqt[...] = jnp.zeros_like(gqt)

    def head_body(head, carry):
        build_bands(bands, row_ref[head])
        gbands[...] = jnp.zeros_like(gbands)
        own = pl.ds(pl.multiple_of(head * size, size), size)
        for col in range(key_blocks):
            rows = slice(col * TILE, (col + 1) * TILE)
            gk = jnp.zeros((TILE, size), F32)
            gv = jnp.zeros((TILE, size), F32)
            for row in range(max(0, col - offset), min(query_blocks, col - offset + HOPS + 1)):
                parts = band_parts(row + offset - col, 0, TILE)
                kern = read_band(bands, parts)
                score = mm(kh[head, rows, :], q_ref[row, own, :])
                grad = mm(vh[head, rows, :], g_ref[row, own, :])
                live = alike(seg_b, rows, segq_ref[row])
                grad = jnp.where(live, grad, 0.0)
                weight = jnp.where(live, score * kern, 0.0).astype(BF)
                gscore = (grad * kern).astype(BF)
                both = grad * score
                at = 0
                for steps, lanes, high in parts:
                    gbands[steps, :, lanes] += both[at : at + high].reshape(high // 8, 8, TILE)
                    at += high
                queries = slice(row * TILE, (row + 1) * TILE)
                gk = gk + mm(gscore, qh[head, queries, :])
                gv = gv + mm(weight, gh[head, queries, :])
                gqt[row, own, :] += mm(kt[col, own, :], gscore)
            gkacc[head, rows, :] = gk
            gvacc[head, rows, :] = gv
        total = gbands[0]
        for step in range(1, 16):
            total = total + pltpu.roll(gbands[step], length - 8 * step, 1)
        line = total[0:1]
        for sub in range(1, 8):
            line = line + pltpu.roll(total, length - sub, 1)[sub : sub + 1]
        gkern_ref[head] = line
        return carry

    lax.fori_loop(0, heads, head_body, 0)
    gq_ref[:, 0 : heads * size, :] = gqt[...].astype(BF)
    for head in range(heads):
        gk_ref[:, head * size : (head + 1) * size] = gkacc[head]
        for block in range(key_blocks):
            part = gvacc[head, block * TILE : (block + 1) * TILE, :].T
            gv_ref[block, v_base + head * size : v_base + (head + 1) * size, :] = part.astype(gv_ref.dtype)


def mix_bwd_merged(v_base, *refs):
    mix_bwd_kernel(v_base, *refs[:7], refs[7], refs[8], refs[7], *refs[9:])


def mix_bwd(q, k_win, v_win, grad, kern_asc, seg_q, seg_k):
    blocks = q.shape[0]
    wide, width = k_win.shape
    heads, _, length = kern_asc.shape
    size = width // heads
    rows = blocks * TILE
    shape = (blocks, width, TILE)
    v_base = v_win.shape[1] - width
    outs = [
        jax.ShapeDtypeStruct((blocks, v_win.shape[1], TILE), BF),
        jax.ShapeDtypeStruct((wide, width), F32),
        jax.ShapeDtypeStruct((heads, 1, length), F32),
    ]
    if not v_base:
        outs.insert(2, jax.ShapeDtypeStruct(v_win.shape, F32))
    return pl.pallas_call(
        functools.partial(mix_bwd_merged if v_base else mix_bwd_kernel, v_base),
        out_shape=tuple(outs),
        in_specs=[vmem()] * 7,
        out_specs=(vmem(),) * len(outs),
        scratch_shapes=[
            pltpu.VMEM((heads, rows, size), BF),
            pltpu.VMEM((heads, wide, size), BF),
            pltpu.VMEM((heads, wide, size), BF),
            pltpu.VMEM((heads, rows, size), BF),
            pltpu.VMEM((wide // TILE, width, TILE), BF),
            pltpu.VMEM(shape, F32),
            pltpu.VMEM((heads, wide, size), F32),
            pltpu.VMEM((heads, wide, size), F32),
            pltpu.VMEM((16, 8, length), F32),
            pltpu.VMEM((16, 8, length), F32),
            pltpu.VMEM((wide, 128), jnp.int32),
        ],
        compiler_params=params(),
        cost_estimate=cost(40, 8 << 20),
        name="mix_bwd",
    )(q, k_win, v_win, grad, kern_asc, seg_q.reshape(blocks, 1, TILE), seg_k[:, None])


def load_pieces(me, pieces, full, sem, base):
    rows = pieces[0].shape[0]
    copies = []
    for mask, piece in enumerate(pieces):
        place = pl.ds(pl.multiple_of((me ^ mask) * rows, 64), rows)
        copies.append(pltpu.make_async_copy(piece, full.at[place], sem.at[base + mask]))
    for copy in copies:
        copy.start()

    def wait():
        for copy in copies:
            copy.wait()

    return wait


def normal_stats(value):
    center = value - jnp.mean(value, axis=-1, keepdims=True)
    scale = lax.rsqrt(jnp.mean(center * center, axis=-1, keepdims=True) + EPS)
    return center * scale, scale


def normal_grad(grad, hat, scale, gain):
    lead = grad * gain
    first = jnp.mean(lead, axis=-1, keepdims=True)
    second = jnp.mean(lead * hat, axis=-1, keepdims=True)
    return scale * (lead - first - hat * second)


def to_blocks(dest, turned, seqs, groups, base=0):
    share = turned.shape[0] // groups
    for seq in range(seqs):
        for group in range(groups):
            dest[seq * groups + group, base : base + share, :] = turned[
                group * share : (group + 1) * share, seq * TILE : (seq + 1) * TILE
            ]


def from_blocks(dest, blocks, seqs, groups, base=0):
    share = dest.shape[1] // groups
    for seq in range(seqs):
        whole = jnp.concatenate(
            [blocks[seq * groups + group, base : base + share, :] for group in range(groups)], axis=0
        )
        dest[seq * TILE : (seq + 1) * TILE, :] = whole.astype(F32).T.astype(BF)


def turn(value):
    return value.astype(F32).T.astype(BF)


def key_kernel(me_ref, x_ref, n0, n1, n2, n3, w0, w1, w2, w3, act_ref, out_ref, norm_ref, full, sem):
    wait = load_pieces(me_ref[0], (w0, w1, w2, w3), full, sem, 0)
    width = full.shape[0]
    groups = width // out_ref.shape[1]
    seqs = x_ref.shape[0] // TILE
    share = n0.shape[1]
    for owner in range(width // share):
        mask = me_ref[0] ^ owner
        low = jnp.where(mask == 0, n0[...].astype(F32), n1[...].astype(F32))
        high = jnp.where(mask == 2, n2[...].astype(F32), n3[...].astype(F32))
        norm_ref[:, owner * share : (owner + 1) * share] = jnp.where(mask < 2, low, high)
    hat, _ = normal_stats(x_ref[...].astype(F32))
    act_ref[...] = (hat * norm_ref[0:1, :] + norm_ref[1:2, :]).astype(BF)
    wait()
    to_blocks(out_ref, mm(act_ref[...], full[...]).T.astype(BF), seqs, groups)


def key_call(me, x, norms, pieces, blocks):
    tokens, width = x.shape
    return pl.pallas_call(
        key_kernel,
        out_shape=(
            jax.ShapeDtypeStruct((tokens, width), BF),
            jax.ShapeDtypeStruct(blocks, BF),
            jax.ShapeDtypeStruct((2, width), F32),
        ),
        in_specs=[smem()] + [vmem()] * 5 + [hbm()] * 4,
        out_specs=(vmem(),) * 3,
        scratch_shapes=[pltpu.VMEM((width, width), BF), pltpu.SemaphoreType.DMA((4,))],
        compiler_params=params(),
        cost_estimate=cost(0.1, 1 << 16),
        name="key_call",
    )(me, x, *norms, *pieces)


def query_value_kernel(me_ref, act_ref, q0, q1, q2, q3, v0, v1, v2, v3, *rest):
    outs, (qfull, vfull, turned, sem) = rest[:-4], rest[-4:]
    wait_q = load_pieces(me_ref[0], (q0, q1, q2, q3), qfull, sem, 0)
    wait_v = load_pieces(me_ref[0], (v0, v1, v2, v3), vfull, sem, 4)
    share = outs[0].shape[0] // 2
    wait_q()
    turned[0] = mm(act_ref[...], qfull[...]).T.astype(BF)
    wait_v()
    turned[1] = mm(act_ref[...], vfull[...]).T.astype(BF)
    groups = qfull.shape[0] // share
    for mask, out in enumerate(outs):
        there = me_ref[1] ^ mask
        features = pl.ds(pl.multiple_of(lax.rem(there, groups) * share, 64), share)
        tokens = pl.ds(pl.multiple_of(lax.div(there, groups) * TILE, TILE), TILE)
        out[0:share, :] = turned[0, features, tokens]
        out[share : 2 * share, :] = turned[1, features, tokens]


def query_value_call(me, act, q_pieces, v_pieces, blocks):
    width = act.shape[1]
    return pl.pallas_call(
        query_value_kernel,
        out_shape=(jax.ShapeDtypeStruct((2 * blocks[1], blocks[2]), BF),) * blocks[0],
        in_specs=[smem(), vmem()] + [hbm()] * 8,
        out_specs=(vmem(),) * blocks[0],
        scratch_shapes=[
            pltpu.VMEM((width, width), BF),
            pltpu.VMEM((width, width), BF),
            pltpu.VMEM((2, width, act.shape[0]), BF),
            pltpu.SemaphoreType.DMA((8,)),
        ],
        compiler_params=params(),
        cost_estimate=cost(0.1, 1 << 16),
        name="query_value_call",
    )(me, act, *q_pieces, *v_pieces)


GELU_A = 0.7978845608028654
GELU_B = 0.044715


def middle_kernel(
    me_ref, y_ref, x_ref, gain_ref, bias_ref, cot_ref, o0, o1, o2, o3, u0, u1, u2, u3, d0, d1, d2, d3,
    resid_ref, act_ref, hidden_ref, gz_ref, gr_ref, gy_ref, gln_ref,
    ofull, ufull, dfull, mixed, hat, gb, sem,
):
    me = me_ref[0]
    wait_o = load_pieces(me, (o0, o1, o2, o3), ofull, sem, 0)
    wait_u = load_pieces(me, (u0, u1, u2, u3), ufull, sem, 4)
    wait_d = load_pieces(me, (d0, d1, d2, d3), dfull, sem, 8)
    tokens, width = x_ref.shape
    groups = width // y_ref.shape[1]
    seqs = tokens // TILE
    chunk = width
    chunks = ufull.shape[1] // chunk
    from_blocks(mixed, y_ref, seqs, groups)
    wait_o()
    resid_ref[...] = x_ref[...].astype(F32) + mm(mixed[...], ofull[...])
    normed, scale = normal_stats(resid_ref[...])
    hat[...] = normed
    act_ref[...] = (normed * gain_ref[...] + bias_ref[...]).astype(BF)
    gb[...] = jnp.zeros_like(gb)
    wait_u()
    wait_d()

    def body(step, carry):
        rows = pl.ds(pl.multiple_of(lax.rem(step, seqs) * TILE, TILE), TILE)
        cols = pl.ds(pl.multiple_of(lax.div(step, seqs) * chunk, chunk), chunk)
        z = mm(act_ref[rows, :], ufull[:, cols])
        dh = mm_nt(cot_ref[rows, :], dfull[cols, :])
        square = z * z
        t = jnp.tanh(GELU_A * z * (1.0 + GELU_B * square))
        half = 0.5 * (1.0 + t)
        hidden_ref[rows, cols] = (z * half).astype(BF)
        slope = half + 0.5 * z * (1.0 - t * t) * (GELU_A * (1.0 + 3.0 * GELU_B * square))
        gz = (slope * dh).astype(BF)
        gz_ref[rows, cols] = gz
        gb[rows, :] += mm_nt(gz, ufull[:, cols])
        return carry

    lax.fori_loop(0, seqs * chunks, body, 0)
    gln_ref[0:1, :] = jnp.sum(gb[...] * hat[...], axis=0, keepdims=True)
    gln_ref[1:2, :] = jnp.sum(gb[...], axis=0, keepdims=True)
    gr_ref[...] = cot_ref[...].astype(F32) + normal_grad(gb[...], hat[...], scale, gain_ref[...])
    to_blocks(gy_ref, mm_nt(ofull[...], gr_ref[...].astype(BF)).astype(BF), seqs, groups)


def middle_call(me, y, x, gain, bias, cot, o_pieces, u_pieces, d_pieces):
    tokens, width = x.shape
    hidden = u_pieces[0].shape[1]
    return pl.pallas_call(
        middle_kernel,
        out_shape=(
            jax.ShapeDtypeStruct((tokens, width), F32),
            jax.ShapeDtypeStruct((tokens, width), BF),
            jax.ShapeDtypeStruct((tokens, hidden), BF),
            jax.ShapeDtypeStruct((tokens, hidden), BF),
            jax.ShapeDtypeStruct((tokens, width), F32),
            jax.ShapeDtypeStruct(y.shape, BF),
            jax.ShapeDtypeStruct((2, width), F32),
        ),
        in_specs=[smem()] + [vmem()] * 5 + [hbm()] * 12,
        out_specs=(vmem(),) * 7,
        scratch_shapes=[
            pltpu.VMEM((width, width), BF),
            pltpu.VMEM((width, hidden), BF),
            pltpu.VMEM((hidden, width), BF),
            pltpu.VMEM((tokens, width), BF),
            pltpu.VMEM((tokens, width), F32),
            pltpu.VMEM((tokens, width), F32),
            pltpu.SemaphoreType.DMA((12,)),
        ],
        compiler_params=params(),
        cost_estimate=cost(15, 24 << 20),
        name="middle_call",
    )(me, y, x, gain, bias, cot, *o_pieces, *u_pieces, *d_pieces)


def down_grads_kernel(me_ref, hidden_ref, cot_ref, keep_ref, send_ref):
    me = me_ref[0]
    wide = keep_ref.shape[1]
    for slot in range(2):
        for dest, mask in ((keep_ref, 2 * slot), (send_ref, 2 * slot + 1)):
            part = hidden_ref[:, pl.ds(pl.multiple_of((me ^ mask) * wide, wide), wide)]
            dest[slot] = mm(turn(part), cot_ref[...]).astype(dest.dtype)


def down_grads_call(me, hidden, cot, shards_count):
    width = cot.shape[1]
    wide = hidden.shape[1] // shards_count
    return pl.pallas_call(
        down_grads_kernel,
        out_shape=(
            jax.ShapeDtypeStruct((2, wide, width), BF),
            jax.ShapeDtypeStruct((2, wide, width), BF),
        ),
        in_specs=[smem()] + [vmem()] * 2,
        out_specs=(vmem(),) * 2,
        compiler_params=params(),
        cost_estimate=cost(6, 16 << 20),
        name="down_grads_call",
    )(me, hidden, cot)


def up_grads_kernel(
    me_ref, y_ref, resid_ref, act_ref, hidden_ref, gz_ref, gr_ref, d0, d1, d2, d3,
    out_ref, keep_ref, send_ref, dfull, act_t, low, sem,
):
    me = me_ref[0]
    wait_d = load_pieces(me, (d0, d1, d2, d3), dfull, sem, 0)
    tokens, width = resid_ref.shape
    hidden = hidden_ref.shape[1]
    groups = width // y_ref.shape[1]
    share = width // groups
    seqs = tokens // TILE
    act_t[...] = turn(act_ref[...])
    low[...] = gr_ref[...].astype(BF)
    blocks = hidden // width
    for slot in range(2):
        for dest, mask in ((keep_ref, 2 * slot), (send_ref, 2 * slot + 1)):
            owner = me ^ mask
            part = act_t[pl.ds(pl.multiple_of(owner * share, share), share), :]
            for block in range(blocks):
                value = mm(part, gz_ref[:, block * width : (block + 1) * width])
                dest[slot, block * share : (block + 1) * share, :] = value.astype(dest.dtype)
            value = mm(y_ref[owner], low[0:TILE, :])
            for seq in range(1, seqs):
                value = value + mm(y_ref[seq * groups + owner], low[seq * TILE : (seq + 1) * TILE, :])
            dest[slot, blocks * share : (blocks + 1) * share, :] = value.astype(dest.dtype)
    wait_d()
    out_ref[...] = (resid_ref[...] + mm(hidden_ref[...], dfull[...])).astype(BF)


def up_grads_call(me, y, resid, act, hidden, gz, gr, d_pieces):
    tokens, width = resid.shape
    wide = hidden.shape[1]
    groups = width // y.shape[1]
    rows = (wide // width + 1) * (width // groups)
    return pl.pallas_call(
        up_grads_kernel,
        out_shape=(
            jax.ShapeDtypeStruct((tokens, width), BF),
            jax.ShapeDtypeStruct((2, rows, width), BF),
            jax.ShapeDtypeStruct((2, rows, width), BF),
        ),
        in_specs=[smem()] + [vmem()] * 6 + [hbm()] * 4,
        out_specs=(vmem(),) * 3,
        scratch_shapes=[
            pltpu.VMEM((wide, width), BF),
            pltpu.VMEM((width, tokens), BF),
            pltpu.VMEM((tokens, width), BF),
            pltpu.SemaphoreType.DMA((4,)),
        ],
        compiler_params=params(),
        cost_estimate=cost(10, 24 << 20),
        name="up_grads_call",
    )(me, y, resid, act, hidden, gz, gr, *d_pieces)


def input_grads(me, act_t, grad, share, base, keep_ref, send_ref):
    for slot in range(2):
        for dest, mask in ((keep_ref, 2 * slot), (send_ref, 2 * slot + 1)):
            part = act_t[pl.ds(pl.multiple_of((me ^ mask) * share, share), share), :]
            dest[slot, base : base + share, :] = mm(part, grad).astype(dest.dtype)


def qv_grads_kernel(
    me_ref, gqv_ref, act_ref, q0, q1, q2, q3, v0, v1, v2, v3,
    keep_ref, send_ref, ga_ref, qfull, vfull, act_t, rows, sem,
):
    me = me_ref[0]
    wait_q = load_pieces(me, (q0, q1, q2, q3), qfull, sem, 0)
    wait_v = load_pieces(me, (v0, v1, v2, v3), vfull, sem, 4)
    tokens, width = act_ref.shape
    share = gqv_ref.shape[1] // 2
    groups = width // share
    seqs = tokens // TILE
    act_t[...] = turn(act_ref[...])
    from_blocks(rows, gqv_ref, seqs, groups)
    input_grads(me, act_t, rows[...], share, 0, keep_ref, send_ref)
    wait_q()
    ga_ref[...] = mm_nt(rows[...], qfull[...])
    from_blocks(rows, gqv_ref, seqs, groups, share)
    input_grads(me, act_t, rows[...], share, share, keep_ref, send_ref)
    wait_v()
    ga_ref[...] += mm_nt(rows[...], vfull[...])


def qv_grads_call(me, gqv, act, q_pieces, v_pieces):
    tokens, width = act.shape
    share = gqv.shape[1] // 2
    return pl.pallas_call(
        qv_grads_kernel,
        out_shape=(
            jax.ShapeDtypeStruct((2, 2 * share, width), BF),
            jax.ShapeDtypeStruct((2, 2 * share, width), BF),
            jax.ShapeDtypeStruct((tokens, width), F32),
        ),
        in_specs=[smem()] + [vmem()] * 2 + [hbm()] * 8,
        out_specs=(vmem(),) * 3,
        scratch_shapes=[
            pltpu.VMEM((width, width), BF),
            pltpu.VMEM((width, width), BF),
            pltpu.VMEM((width, tokens), BF),
            pltpu.VMEM((tokens, width), BF),
            pltpu.SemaphoreType.DMA((8,)),
        ],
        compiler_params=params(),
        cost_estimate=cost(8, 12 << 20),
        name="qv_grads_call",
    )(me, gqv, act, *q_pieces, *v_pieces)


def last_kernel(
    me_ref, gk_ref, act_ref, ga_ref, x_ref, gr_ref, norm_ref, extra_ref, k0, k1, k2, k3,
    keep_ref, send_ref, gx_ref, kfull, act_t, rows, sem,
):
    me = me_ref[0]
    wait_k = load_pieces(me, (k0, k1, k2, k3), kfull, sem, 0)
    tokens, width = act_ref.shape
    share = gk_ref.shape[1]
    act_t[...] = turn(act_ref[...])
    from_blocks(rows, gk_ref, tokens // TILE, width // share)
    input_grads(me, act_t, rows[...], share, 0, keep_ref, send_ref)
    wait_k()
    ga = ga_ref[...] + mm_nt(rows[...], kfull[...])
    hat, scale = normal_stats(x_ref[...].astype(F32))
    gain = jnp.sum(ga * hat, axis=0, keepdims=True)
    bias = jnp.sum(ga, axis=0, keepdims=True)
    lines = jnp.concatenate([gain, bias, jnp.zeros((6, width), F32)], axis=0).astype(BF)
    for slot in range(2):
        for dest, mask in ((keep_ref, 2 * slot), (send_ref, 2 * slot + 1)):
            dest[slot, share : share + 8, :] = lines
            dest[slot, share + 8 :, :] = extra_ref[mask]
    gx_ref[...] = (gr_ref[...] + normal_grad(ga, hat, scale, norm_ref[0:1, :])).astype(BF)


def last_call(me, gk, act, ga, x, gr, norm, extra, k_pieces):
    tokens, width = act.shape
    rows = gk.shape[1] + 8 + extra.shape[1]
    return pl.pallas_call(
        last_kernel,
        out_shape=(
            jax.ShapeDtypeStruct((2, rows, width), BF),
            jax.ShapeDtypeStruct((2, rows, width), BF),
            jax.ShapeDtypeStruct((tokens, width), BF),
        ),
        in_specs=[smem()] + [vmem()] * 7 + [hbm()] * 4,
        out_specs=(vmem(),) * 3,
        scratch_shapes=[
            pltpu.VMEM((width, width), BF),
            pltpu.VMEM((width, tokens), BF),
            pltpu.VMEM((tokens, width), BF),
            pltpu.SemaphoreType.DMA((4,)),
        ],
        compiler_params=params(),
        cost_estimate=cost(6, 8 << 20),
        name="last_call",
    )(me, gk, act, ga, x, gr, norm, extra, *k_pieces)


def xor_permute(value, axis, mask):
    count = lax.axis_size(axis)
    return lax.ppermute(value, axis, [(source, source ^ mask) for source in range(count)])


def collect_kernel(me_ref, *refs):
    parts, out = refs[:-1], refs[-1]
    for mask, part in enumerate(parts):
        out[me_ref[1] ^ mask] = part[...]


def swap_parts(me, parts, label, order):
    came = [order(parts[0])] + [xor_permute(part, "dp", mask) for mask, part in enumerate(parts) if mask]
    shape = (len(parts),) + parts[0].shape
    return pl.pallas_call(
        collect_kernel,
        out_shape=jax.ShapeDtypeStruct(shape, BF),
        in_specs=[smem()] + [vmem()] * len(parts),
        out_specs=vmem(),
        compiler_params=params(),
        cost_estimate=cost(0.5, 2 << 20),
        name=label,
    )(me, *came)


def gather_pieces(shard):
    across = xor_permute(shard, "fsdp", 2)
    beside = xor_permute(shard, "fsdp", 1)
    both = xor_permute(across, "fsdp", 1)
    return (shard, beside, across, both)


class Order:
    def __init__(self):
        self.last = None

    def __call__(self, value):
        if self.last is None:
            return value
        return lax.optimization_barrier((value, self.last))[0]

    def mark(self, value):
        self.last = value
        return value


def join_halves(own, other, bit):
    first = jnp.where(bit == 0, own, other)
    second = jnp.where(bit == 0, other, own)
    return jnp.concatenate([first, second], axis=0)


DP_MASKS = (1, 2, 4)


class Reduction:
    def __init__(self, order, keep, send, direct=False, near_first=False):
        self.order = order
        self.keep = keep
        self.move = send
        self.me = lax.axis_index("dp")
        self.steps = [self.core]
        self.near_first = near_first and lax.axis_size("dp") == 8
        if direct or lax.axis_size("dp") != 8:
            self.cuts = []
            self.steps += [self.high, self.scatter_all, self.gather_all]
        else:
            self.cuts = list(DP_MASKS)
            scatters = [functools.partial(self.scatter, mask) for mask in DP_MASKS]
            self.steps += scatters[:1] + [self.high] + scatters[1:] if near_first else [self.high] + scatters
            self.steps += [functools.partial(self.gather, mask) for mask in DP_MASKS[::-1]]

    def next(self):
        if self.steps:
            self.steps.pop(0)()
            self.order.mark(self.move)

    def add(self, came):
        return (self.order(self.keep).astype(F32) + came.astype(F32)).astype(BF)

    def core(self):
        came = xor_permute(self.move, "fsdp", 1)
        total = self.add(came)
        if self.near_first:
            self.cut(total, 1)
        else:
            self.keep, self.move = total[0], total[1]

    def high(self):
        self.cut(self.add(xor_permute(self.move, "fsdp", 2)))

    def cut(self, total, axis=0):
        self.move = total
        if self.cuts:
            bit = (self.me // self.cuts.pop(0)) % 2
            rows = total.shape[axis] // 2
            halves = total.reshape(total.shape[:axis] + (2, rows) + total.shape[axis + 1 :])
            self.keep = lax.dynamic_index_in_dim(halves, bit, axis, keepdims=False)
            self.move = lax.dynamic_index_in_dim(halves, 1 - bit, axis, keepdims=False)

    def scatter(self, mask):
        total = self.add(xor_permute(self.move, "dp", mask))
        if total.ndim == 3:
            self.keep, self.move = total[0], total[1]
        else:
            self.cut(total)

    def gather(self, mask):
        other = xor_permute(self.move, "dp", mask)
        self.move = join_halves(self.order(self.move), other, (self.me // mask) % 2)

    def scatter_all(self):
        rows, cols = self.move.shape
        count = lax.axis_size("dp")
        parts = lax.all_to_all(self.move.reshape(count, rows // count, cols), "dp", 0, 0)
        self.move = jnp.sum(self.order(parts).astype(F32), axis=0).astype(BF)

    def gather_all(self):
        rows, cols = self.move.shape
        count = lax.axis_size("dp")
        spread = jnp.broadcast_to(self.move[None], (count, rows, cols))
        self.move = lax.all_to_all(spread, "dp", 0, 0).reshape(count * rows, cols)

    def result(self):
        while self.steps:
            self.next()
        return self.move.astype(F32)


def kernel_rows(rate, freq, coef, skip, lags, reach):
    lag = lags.astype(F32)
    inside = (lags >= 0) & (lags < reach)
    clipped = jnp.where(inside, lag, 0.0)
    decay = jnp.exp(-rate[:, :, None] * clipped)
    angle = freq[:, :, None] * clipped
    wave = coef[0][:, :, None] * jnp.cos(angle) - coef[1][:, :, None] * jnp.sin(angle)
    first = (lags == 0).astype(F32)
    return jnp.where(inside, jnp.sum(decay * wave, axis=1) + skip[:, None] * first, 0.0)


def shards(
    tokens, segments, ln1_gain, ln1_bias, w_query, w_key, w_value, shift_taps, ssm_rate, ssm_freq,
    ssm_coef, ssm_skip, w_out, ln2_gain, ln2_bias, w_up, w_down, cotangent,
):
    seqs, rows, width = tokens.shape
    fsdp = lax.axis_size("fsdp")
    dp = lax.axis_size("dp")
    run = HOPS
    place = lax.axis_index("fsdp")
    me = lax.axis_index("dp")
    chunk, inner = me // run, me % run
    group_count = run // seqs
    share = width // group_count
    seq, group = inner // group_count, inner % group_count
    span = run * rows
    multi = dp > run
    groups = [list(range(base, base + run)) for base in range(0, dp, run)] if multi else None
    reach = HOPS * rows + rows
    assert dp % run == 0 and rows == TILE and fsdp == 4 and group_count == fsdp
    blocks = (run, share, rows)

    def exchange(value):
        return lax.all_to_all(value, "dp", 0, 0, axis_index_groups=groups)

    def from_prev(value):
        if not multi:
            return jnp.zeros_like(value)
        return lax.ppermute(value, "dp", [(src, src + run) for src in range(dp - run)])

    def from_next(value):
        return lax.ppermute(value, "dp", [(src + run, src) for src in range(dp - run)])

    key_w = gather_pieces(w_key)
    norm_one = gather_pieces(jnp.stack([ln1_gain, ln1_bias]))
    w_query, w_value, w_out, _ = lax.optimization_barrier((w_query, w_value, w_out, key_w[2]))
    query_w = gather_pieces(w_query)
    value_w = gather_pieces(w_value)
    out_w = gather_pieces(w_out)
    w_up, w_down, _ = lax.optimization_barrier((w_up, w_down, value_w[2]))
    up_w = gather_pieces(w_up)
    down_w = gather_pieces(w_down)
    small_parts = (shift_taps, ssm_rate, ssm_freq, ssm_coef, ssm_skip, ln2_gain, ln2_bias)
    flat = jnp.concatenate([part.reshape(-1) for part in small_parts])
    padded = -(-flat.shape[0] // 1024) * 1024
    flat = jnp.pad(flat, (0, padded - flat.shape[0])).reshape(padded // 128, 128)
    flat, _ = lax.optimization_barrier((flat, key_w[2]))
    in_order = jnp.stack(gather_pieces(flat)).reshape(fsdp, padded)
    small = in_order[jnp.arange(fsdp) ^ place]
    pieces, at = [], 0
    for part in small_parts:
        pieces.append(small[:, at : at + part.size])
        at += part.size
    gain_two, bias_two = (pieces[index].reshape(1, width).astype(F32) for index in (5, 6))

    def mine(piece, shape):
        return lax.dynamic_index_in_dim(piece, group, 0, keepdims=False).reshape(shape).astype(F32)

    taps = mine(pieces[0], shift_taps.shape)
    rate = mine(pieces[1], ssm_rate.shape)
    freq = mine(pieces[2], ssm_freq.shape)
    coef = mine(pieces[3], ssm_coef.shape)
    skip = mine(pieces[4], ssm_skip.shape)

    lags = jnp.arange(reach + TILE) - TILE
    kern, kern_pull = jax.vjp(lambda *leaves: kernel_rows(*leaves, lags, reach), rate, freq, coef, skip)
    kern = kern[:, None, :]

    segments, _ = lax.optimization_barrier((segments, key_w[3]))
    seg_row = lax.dynamic_index_in_dim(segments, seq, 0, keepdims=False)
    seg_wide = jnp.concatenate(
        [jnp.full((span,), -1, jnp.int32), seg_row, jnp.full((HALO,), -2, jnp.int32)]
    )
    seg_full = lax.dynamic_slice_in_dim(seg_wide, chunk * span + span - HALO, span + 2 * HALO, 0)
    seg_q = seg_full[HALO : HALO + span]
    seg_k = lax.dynamic_slice_in_dim(seg_wide, chunk * span, 2 * span, 0) if multi else seg_q

    taps_tiles = lane_taps(taps)

    which = jnp.stack([place, inner]).astype(jnp.int32)
    x = tokens.reshape(seqs * rows, width)
    cot = cotangent.reshape(seqs * rows, width)
    act_one, k_mine, norm = key_call(which, x, norm_one, key_w, blocks)
    k_own = exchange(k_mine)
    qv_parts = query_value_call(which, act_one, query_w, value_w, blocks)
    k_halo = from_prev(k_own[-1, :, rows - HALO :].T)
    ks_own = shift_fwd(seg_full, k_own, k_halo, taps_tiles)
    forward = Order()
    forward.mark((ks_own, up_w[2], out_w[3]))
    qv_own = swap_parts(which, qv_parts, "collect_qv", forward)
    if multi:
        ks_win = jnp.concatenate([from_prev(ks_own), ks_own], axis=0)
        v_own = qv_own[:, share:]
        v_win = jnp.concatenate([from_prev(v_own), v_own], axis=0)
    else:
        ks_win, v_win = ks_own, qv_own
    y_own = mix_fwd(qv_own, ks_win, v_win, kern, seg_q, seg_k)
    forward.mark(down_w[2])
    y_mine = exchange(forward(y_own))
    resid, act_two, hidden, gz, gr, gy_mine, gln_two = middle_call(
        which, y_mine, x, gain_two, bias_two, cot, out_w, up_w, down_w
    )
    gy_own = exchange(gy_mine)
    order = Order()
    down_sum = Reduction(order, *down_grads_call(which, hidden, cot, fsdp), near_first=True)
    order.mark(down_sum.move)
    down_sum.next()
    output, *up_parts = up_grads_call(which, y_mine, resid, order(act_two), hidden, gz, gr, down_w)
    up_sum = Reduction(order, *up_parts)

    up_sum.move, gy_own = lax.optimization_barrier((up_sum.move, gy_own))
    up_sum.next()
    gy_own = order(gy_own)
    if multi:
        gq_own, gks_win, gv_win, gkern = mix_bwd(qv_own, ks_win, v_win, gy_own, kern, seg_q, seg_k)
        gks_own = gks_win[span:] + from_next(gks_win[:span].astype(BF)).astype(F32)
        gv_own = (gv_win[run:] + from_next(gv_win[:run].astype(BF)).astype(F32)).astype(BF)
        gqv_own = jnp.concatenate([gq_own, gv_own], axis=1)
        gks_halo = from_next(gks_own[:HALO].astype(BF)).astype(F32)
    else:
        gqv_own, gks_own, gkern = mix_bwd(qv_own, ks_win, v_win, gy_own, kern, seg_q, seg_k)
        gks_halo = jnp.zeros((HALO, share), F32)
    order.mark(gkern)
    gqv_mine = exchange(gqv_own)
    down_sum.next()
    up_sum.next()
    gks_own = order(gks_own)
    taps_grad, gk_own = shift_bwd(seg_full, k_own, k_halo, gks_own, gks_halo, taps_tiles)
    order.mark(taps_grad)
    down_sum.next()
    up_sum.next()
    rate_grad, freq_grad, coef_grad, skip_grad = kern_pull(order(gkern)[:, 0, :])

    ssm_line = jnp.concatenate([grad.reshape(-1) for grad in (rate_grad, freq_grad, coef_grad, skip_grad)])
    ssm_line = jnp.pad(ssm_line, (0, width - ssm_line.shape[0]))[None]
    by_group = jnp.concatenate([taps_grad.reshape(-1, width), ssm_line])
    slots = (jnp.arange(fsdp) ^ place) == group
    by_group = jnp.where(slots[:, None, None], by_group[None], 0.0)
    extra = jnp.concatenate([jnp.broadcast_to(gln_two, (fsdp, 2, width)), by_group], axis=1).astype(BF)
    extra = jnp.pad(extra, ((0, 0), (0, 56 - extra.shape[1]), (0, 0)))
    order.mark(extra)
    down_sum.next()
    gk_own, gqv_mine = lax.optimization_barrier((gk_own, order(gqv_mine)))
    gk_mine = exchange(gk_own)
    *qv_grads, ga = qv_grads_call(which, gqv_mine, act_one, query_w, value_w)
    qv_sum = Reduction(order, *qv_grads)
    order.mark(qv_sum.move)
    qv_sum.next()
    up_sum.next()
    keep_c, send_c, input_grad = last_call(which, order(gk_mine), act_one, ga, x, gr, norm, extra, key_w)
    key_sum = Reduction(order, keep_c, send_c, direct=True)
    order.mark(send_c)

    shard = width // fsdp
    chains = {"k": key_sum, "q": qv_sum, "u": up_sum, "d": down_sum}
    for name in "dkuqdkuqdukqduqkq":
        chains[name].next()
    key_rows, query_value, up_out, down_grad = (
        chain.result() for chain in (key_sum, qv_sum, up_sum, down_sum)
    )
    key_grad = key_rows[:shard]
    up_grad = up_out[:-shard]
    up_grad = up_grad.reshape(-1, shard, width).transpose(1, 0, 2).reshape(w_up.shape)
    out_grad = up_out[-shard:]
    query_grad, value_grad = query_value[:shard], query_value[shard:]
    norms = jnp.concatenate([key_rows[shard : shard + 2], key_rows[shard + 8 : shard + 10]])
    norms = lax.dynamic_slice_in_dim(norms, place * shard, shard, 1)
    owned = jnp.concatenate([norms.reshape(-1), key_rows[shard + 10 :].reshape(-1)])
    shapes = [ln1_gain.shape, ln1_bias.shape, ln2_gain.shape, ln2_bias.shape, shift_taps.shape]
    shapes += [ssm_rate.shape, ssm_freq.shape, ssm_coef.shape, ssm_skip.shape]
    little, at = [], 0
    for shape in shapes:
        count = int(np.prod(shape))
        little.append(owned[at : at + count].reshape(shape))
        at += count
    return (
        output.reshape(seqs, rows, width),
        input_grad.reshape(seqs, rows, width),
        little[0],
        little[1],
        query_grad,
        key_grad,
        value_grad,
        little[4],
        little[5],
        little[6],
        little[7],
        little[8],
        out_grad,
        little[2],
        little[3],
        up_grad,
        down_grad,
    )


def solution(mesh):
    return jax.shard_map(
        shards,
        mesh=mesh,
        in_specs=(
            P("fsdp", "dp", None),
            P("fsdp", None),
            P("fsdp"),
            P("fsdp"),
            P("fsdp", None),
            P("fsdp", None),
            P("fsdp", None),
            P(None, "fsdp"),
            P("fsdp", None),
            P("fsdp", None),
            P(None, "fsdp", None),
            P("fsdp"),
            P("fsdp", None),
            P("fsdp"),
            P("fsdp"),
            P("fsdp", None),
            P("fsdp", None),
            P("fsdp", "dp", None),
        ),
        out_specs=(
            P("fsdp", "dp", None),
            P("fsdp", "dp", None),
            P("fsdp"),
            P("fsdp"),
            P("fsdp", None),
            P("fsdp", None),
            P("fsdp", None),
            P(None, "fsdp"),
            P("fsdp", None),
            P("fsdp", None),
            P(None, "fsdp", None),
            P("fsdp"),
            P("fsdp", None),
            P("fsdp"),
            P("fsdp"),
            P("fsdp", None),
            P("fsdp", None),
        ),
        check_vma=False,
    )
```

profile of v0, /device:TPU:0, one launch (start us, length us, event | category | flops | bytes accessed | tf_op | source)
XLA Modules:
  0.0 431.3 jit_solution(8275065684161525658)
XLA Ops:
  2.1 3.0 collective-permute-start.1
  8.8 2.1 concatenate.51
  10.9 3.8 collective-permute-done.4.w2.k2
  15.1 3.6 collective-permute-done.13
  21.5 1.8 collective-permute-start.7
  23.9 6.1 %collective-permute-done.10.v2 = bf16[192,768]{1,0:T(8,128)(2,1)S(1)} collective-permute-done((bf16[192,768]{1,0:T(8,128)(2,1)}, bf16[192,768]{1,0:T(8,128)(2,1)S(1)}, u32[]{:S(2)}, u32[]{:S(2)}) %collective-permute-start.10) | collective-permute-done | bytes 294944 | tf_op jit(solution)/shard_map/ppermute | solution.py:869
  30.8 1.8 collective-permute-start.15
  32.6 4.2 fusion.13
  36.8 4.3 key_call.1
  41.2 6.4 %all-to-all-start = ((bf16[8,192,256]{2,1,0:T(8,128)(2,1)}), bf16[8,192,256]{2,1,0:T(8,128)(2,1)S(1)}, u32[]{:S(2)}, u32[]{:S(2)}) async-start(bf16[8,192,256]{2,1,0:T(8,128)(2,1)} %get-tuple-element.102), calls=%async_computation | async-start | bytes 1572864 | tf_op jit(solution)/shard_map/all_to_all | solution.py:1029
  53.0 5.7 %query_value_call.1 = (bf16[384,256]{1,0:T(8,128)(2,1)}, bf16[384,256]{1,0:T(8,128)(2,1)}, bf16[384,256]{1,0:T(8,128)(2,1)}, bf16[384,256]{1,0:T(8,128)(2,1)}, b...) custom-call(s32[2]{0:T(128)} %pad_add_fusion.1.me_ref, ...), custom_call_target="tpu_custom_call" | custom-call | flops 100000 | bytes 8 | tf_op jit(solution)/shard_map/query_value_call/pallas_call | solution.py:586
  58.7 2.1 collective-permute-start.18
  63.1 3.9 collective-permute-done.18.refs_1_
  67.0 2.9 collective-permute-start.21
  69.9 1.8 collective-permute-start.22
  71.7 3.4 collective-permute-done.20.refs_3_
  75.1 2.3 collective-permute-start.23
  77.4 4.6 %collective-permute-start.24 = (bf16[384,256]{1,0:T(8,128)(2,1)}, bf16[384,256]{1,0:T(8,128)(2,1)S(1)}, u32[]{:S(2)}, u32[]{:S(2)}) collective-permute-start(bf16[384,256]{1,0:T(8,128)(2,1)} %get-tuple-element.113), channel_id=1, source_target_pairs={{0,7},{1,6},{2,5},{3,4},{4,3},{5,2},{6,1},{7,0},{8,15},{9,14},{10,... | collective-permute-start | bytes 589832 | tf_op jit(solution)/shard_map/ppermute | solution.py:869
  86.0 12.0 %shift_fwd.1.k_ref.refs_1_ = bf16[2048,192]{1,0:T(8,128)(2,1)} custom-call(s32[2176]{0:T(1024)} %copy-done.23, bf16[8,192,256]{2,1,0:T(8,128)(2,1)} %copy-done.3, bf16[64,192]{1,0:T(8,128)(2,1)} %broadcast_in_dim.91.halo_ref, f32[2,64,128]{2,1,0:T(8,128)} %pad_maximum_fusion.10.taps_ref, s32[2176,1]{1,0:T(8,128)} %broadcast_in_dim.109.segcol_ref), custom_call_target="tpu_custom_call" | custom-call | flops 10000000 | bytes 262 | tf_op jit(solution)/shard_map/shift_fwd/pallas_call | solution.py:185
  100.1 2.7 collect_qv.1.q_ref.v_ref.refs_0_.refs_2_
  102.8 12.7 %mix_fwd.1 = bf16[8,192,256]{2,1,0:T(8,128)(2,1)} custom-call(bf16[8,384,256]{2,1,0:T(8,128)(2,1)} %collect_qv.1.q_ref.v_ref.refs_0_.refs_2_, bf16[2048,192]{1,0:T(8,128)(2,1)} %shift_fwd.1.k_ref.refs_1_, bf16[8,384,256]{2,1,0:T(8,128)(2,1)} %collect_qv.1.q_ref.v_ref.refs_0_.refs_2_, f32[3,1,2560]{2,1,0:T(1,128)} %broadcast_select_fusion.18.row_ref.refs_4_, ...), custom_call_target="tpu_custom_call" | custom-call | flops 20000000 | bytes 524 | tf_op jit(solution)/shard_map/mix_fwd/pallas_call | solution.py:356
  115.4 9.4 %all-to-all-start.1 = ((bf16[8,192,256]{2,1,0:T(8,128)(2,1)}), bf16[8,192,256]{2,1,0:T(8,128)(2,1)S(1)}, u32[]{:S(2)}, u32[]{:S(2)}) async-start(bf16[8,192,256]{2,1,0:T(8,128)(2,1)} %mix_fwd.1), calls=%async_computation.1 | async-start | bytes 1572864 | tf_op jit(solution)/shard_map/all_to_all | solution.py:1029
  127.3 4.5 %collective-permute-done.26.o1 = bf16[192,768]{1,0:T(8,128)(2,1)S(1)} collective-permute-done((bf16[192,768]{1,0:T(8,128)(2,1)}, bf16[192,768]{1,0:T(8,128)(2,1)S(1)}, u32[]{:S(2)}, u32[]{:S(2)}) %collective-permute-start.26) | collective-permute-done | bytes 294944 | tf_op jit(solution)/shard_map/ppermute | solution.py:869
  131.9 1.7 collective-permute-done.28.u3
  133.6 10.9 %all-to-all-done.1.y_ref = bf16[8,192,256]{2,1,0:T(8,128)(2,1)S(1)} async-done(((bf16[8,192,256]{2,1,0:T(8,128)(2,1)}), bf16[8,192,256]{2,1,0:T(8,128)(2,1)S(1)}, u32[]{:S(2)}, u32[]{:S(2)}) %all-to-all-start.1) | async-done | bytes 786464 | tf_op jit(solution)/shard_map/all_to_all | solution.py:1029
  145.4 19.7 %middle_call.1 = (f32[512,768]{1,0:T(8,128)}, bf16[512,768]{1,0:T(8,128)(2,1)}, bf16[512,3072]{1,0:T(8,128)(2,1)}, bf16[512,3072]{1,0:T(8,128)(2,1)}, f32[512,76...) custom-call(s32[2]{0:T(128)} %pad_add_fusion.1.me_ref, bf16[8,192,256]{2,1,0:T(8,128)(2,1)} %copy-done.2, ...), custom_call_target="tpu_custom_call" | custom-call | flops 15000000 | bytes 3145 | tf_op jit(solution)/shard_map/middle_call/pallas_call | solution.py:656
  165.2 6.6 %down_grads_call.1 = (bf16[2,768,768]{2,1,0:T(8,128)(2,1)}, bf16[2,768,768]{2,1,0:T(8,128)(2,1)}) custom-call(s32[2]{0:T(128)} %pad_add_fusion.1.me_ref, bf16[512,3072]{1,0:T(8,128)(2,1)} %get-tuple-element.118.hidden_ref, bf16[512,768]{1,0:T(8,128)(2,1)} %bitcast.128), custom_call_target="tpu_custom_call" | custom-call | flops 6000000 | bytes 2097 | tf_op jit(solution)/shard_map/down_grads_call/pallas_call | solution.py:696
  171.7 3.8 all-to-all-start.2
  176.5 2.2 add_convert_fusion.1
  179.9 12.7 %up_grads_call.1 = (bf16[512,768]{1,0:T(8,128)(2,1)}, bf16[2,960,768]{2,1,0:T(8,128)(2,1)}, bf16[2,960,768]{2,1,0:T(8,128)(2,1)}) custom-call(s32[2]{0:T(128)} %pad_add_fusion.1.me_ref, bf16[8,192,256]{2,1,0:T(8,128)(2,1)} %copy-done.2, f32[512,768]{1,0:T(8,128)} %get-tuple-element.116.resid_ref, bf16[512,768]{1,0:T(8,128)(2,1)} %get-tuple-element.121.act_ref, ...), custom_call_target="tpu_custom_call" | custom-call | flops 10000000 | bytes 3145 | tf_op jit(solution)/shard_map/up_grads_call/pallas_call | solution.py:744
  192.6 3.9 all-to-all-done.2.refs_3_
  197.9 4.2 collective-permute-done.32
  202.1 2.7 add_convert_fusion
  207.6 32.1 %mix_bwd.1 = (bf16[8,384,256]{2,1,0:T(8,128)(2,1)}, f32[2048,192]{1,0:T(8,128)}, f32[3,1,2560]{2,1,0:T(1,128)}) custom-call(bf16[8,384,256]{2,1,0:T(8,128)(2,1)} %collect_qv.1.q_ref.v_ref.refs_0_.refs_2_, bf16[2048,192]{1,0:T(8,128)(2,1)} %shift_fwd.1.k_ref.refs_1_, bf16[8,384,256]{2,1,0:T(8,128)(2,1)} %collect_qv.1.q_ref.v_ref.refs_0_.refs_2_, ...), custom_call_target="tpu_custom_call" | custom-call | flops 40000000 | bytes 1048 | tf_op jit(solution)/shard_map/mix_bwd/pallas_call | solution.py:456
  241.6 4.1 all-to-all-start.3
  245.7 1.7 add_convert_fusion.2
  248.5 2.0 collective-permute-start.36
  251.2 20.3 %shift_bwd.1 = (f32[64,192]{1,0:T(8,128)}, bf16[8,192,256]{2,1,0:T(8,128)(2,1)}) custom-call(s32[2176]{0:T(1024)} %copy-done.23, bf16[8,192,256]{2,1,0:T(8,128)(2,1)} %copy-done.3, bf16[64,192]{1,0:T(8,128)(2,1)} %broadcast_in_dim.91.halo_ref, f32[2048,192]{1,0:T(8,128)} %get-tuple-element.136.g_ref, f32[64,192]{1,0:T(8,128)} %broadcast_in_dim.97.ghalo_ref, ...), custom_call_target="tpu_custom_call" | custom-call | flops 20000000 | bytes 524 | tf_op jit(solution)/shard_map/shift_bwd/pallas_call | solution.py:259
  275.2 5.5 %collective-permute-done.36 = bf16[480,768]{1,0:T(8,128)(2,1)} collective-permute-done((bf16[480,768]{1,0:T(8,128)(2,1)}, bf16[480,768]{1,0:T(8,128)(2,1)}, u32[]{:S(2)}, u32[]{:S(2)}) %collective-permute-start.36) | collective-permute-done | bytes 737312 | tf_op jit(solution)/shard_map/ppermute | solution.py:869
  282.9 5.2 %fusion.19 = (f32[3,32]{1,0:T(4,128)S(1)}, bf16[3,32]{1,0:T(4,128)(2,1)S(1)}, f32[3,32]{1,0:T(4,128)S(1)}, f32[3,32]{1,0:T(4,128)S(1)}) fusion(f32[3,2560]{1,0:T(4,128)S(1)} %get-tuple-element.271, f32[3,32]{1,0:T(4,128)S(1)} %copy-done.40, f32[3,32]{1,0:T(4,128)S(1)} %reshape.369, f32[3,32]{1,0:T(4,128)S(1)} %copy-done.38, f32[2560]{0:T(1024)S(1)} %copy-done.34, ...), kind=kLoop, calls=%fused_computation.38 | loop fusion | flops 5652096 | bytes 43840 | tf_op jit(solution)/shard_map/transpose(jvp())/reduce_sum | solution.py:1000
  290.6 7.4 %qv_grads_call.1 = (bf16[2,384,768]{2,1,0:T(8,128)(2,1)}, bf16[2,384,768]{2,1,0:T(8,128)(2,1)}, f32[512,768]{1,0:T(8,128)}) custom-call(s32[2]{0:T(128)} %pad_add_fusion.1.me_ref, bf16[8,384,256]{2,1,0:T(8,128)(2,1)} %copy-done.4, bf16[512,768]{1,0:T(8,128)(2,1)} %get-tuple-element.97.act_ref, bf16[192,768]{1,0:T(8,128)(2,1)} %q0.1, ...), custom_call_target="tpu_custom_call" | custom-call | flops 8000000 | bytes 1572 | tf_op jit(solution)/shard_map/qv_grads_call/pallas_call | solution.py:797
  298.1 4.9 %all-to-all-start.4 = ((bf16[8,192,256]{2,1,0:T(8,128)(2,1)}), bf16[8,192,256]{2,1,0:T(8,128)(2,1)S(1)}, u32[]{:S(2)}, u32[]{:S(2)}) async-start(bf16[8,192,256]{2,1,0:T(8,128)(2,1)} %get-tuple-element.146), calls=%async_computation.4 | async-start | bytes 1572864 | tf_op jit(solution)/shard_map/all_to_all | solution.py:1029
  303.0 2.1 collective-permute-start.39
  305.1 1.6 add_convert_fusion.3
  306.8 19.6 %collective-permute-done.39 = bf16[240,768]{1,0:T(8,128)(2,1)S(1)} collective-permute-done((bf16[240,768]{1,0:T(8,128)(2,1)}, bf16[240,768]{1,0:T(8,128)(2,1)S(1)}, u32[]{:S(2)}, u32[]{:S(2)}) %collective-permute-start.39) | collective-permute-done | bytes 368672 | tf_op jit(solution)/shard_map/ppermute | solution.py:869
  327.5 7.4 %last_call.1 = (bf16[2,256,768]{2,1,0:T(8,128)(2,1)}, bf16[2,256,768]{2,1,0:T(8,128)(2,1)}, bf16[512,768]{1,0:T(8,128)(2,1)}) custom-call(s32[2]{0:T(128)} %pad_add_fusion.1.me_ref, bf16[8,192,256]{2,1,0:T(8,128)(2,1)} %copy-done.7, bf16[512,768]{1,0:T(8,128)(2,1)} %get-tuple-element.97.act_ref, f32[512,768]{1,0:T(8,128)} %get-tuple-element.153.ga_ref, ...), custom_call_target="tpu_custom_call" | custom-call | flops 6000000 | bytes 1048 | tf_op jit(solution)/shard_map/last_call/pallas_call | solution.py:846
  335.0 2.4 collective-permute-start.40
  339.5 10.1 %collective-permute-done.40 = bf16[96,768]{1,0:T(8,128)(2,1)S(1)} collective-permute-done((bf16[96,768]{1,0:T(8,128)(2,1)S(1)}, bf16[96,768]{1,0:T(8,128)(2,1)S(1)}, u32[]{:S(2)}, u32[]{:S(2)}) %collective-permute-start.40) | collective-permute-done | bytes 147488 | tf_op jit(solution)/shard_map/ppermute | solution.py:869
  351.1 1.6 collective-permute-start.45
  352.7 4.0 collective-permute-done.42
  358.3 5.5 %collective-permute-done.44 = bf16[96,768]{1,0:T(8,128)(2,1)S(1)} collective-permute-done((bf16[96,768]{1,0:T(8,128)(2,1)S(1)}, bf16[96,768]{1,0:T(8,128)(2,1)S(1)}, u32[]{:S(2)}, u32[]{:S(2)}) %collective-permute-start.44) | collective-permute-done | bytes 147488 | tf_op jit(solution)/shard_map/ppermute | solution.py:869
  364.7 2.8 collective-permute-done.46
  367.8 2.1 collective-permute-start.50
  369.8 4.5 %all-to-all-start.5 = ((bf16[8,32,768]{2,1,0:T(8,128)(2,1)}), bf16[8,32,768]{2,1,0:T(8,128)(2,1)S(1)}, u32[]{:S(2)}, u32[]{:S(2)}) async-start(bf16[8,32,768]{2,1,0:T(8,128)(2,1)} %bitcast.44), calls=%async_computation.5 | async-start | bytes 786432 | tf_op jit(solution)/shard_map/all_to_all | solution.py:981
  374.5 2.1 collective-permute-start.51
  376.6 7.8 %collective-permute-done.49 = bf16[240,768]{1,0:T(8,128)(2,1)S(1)} collective-permute-done((bf16[240,768]{1,0:T(8,128)(2,1)S(1)}, bf16[240,768]{1,0:T(8,128)(2,1)S(1)}, u32[]{:S(2)}, u32[]{:S(2)}) %collective-permute-start.49) | collective-permute-done | bytes 368672 | tf_op jit(solution)/shard_map/ppermute | solution.py:869
  384.5 6.6 %all-to-all-done.5 = bf16[8,32,768]{2,1,0:T(8,128)(2,1)S(1)} async-done(((bf16[8,32,768]{2,1,0:T(8,128)(2,1)}), bf16[8,32,768]{2,1,0:T(8,128)(2,1)S(1)}, u32[]{:S(2)}, u32[]{:S(2)}) %all-to-all-start.5) | async-done | bytes 393248 | tf_op jit(solution)/shard_map/all_to_all | solution.py:981
  391.6 1.7 collective-permute-start.52
  394.1 4.7 %all-to-all-start.6 = ((bf16[8,32,768]{2,1,0:T(8,128)(2,1)}), bf16[8,32,768]{2,1,0:T(8,128)(2,1)S(1)}, u32[]{:S(2)}, u32[]{:S(2)}) async-start(bf16[8,32,768]{2,1,0:T(8,128)(2,1)} %broadcast_in_dim.108), calls=%async_computation.6 | async-start | bytes 786432 | tf_op jit(solution)/shard_map/all_to_all | solution.py:988
  398.8 3.0 collective-permute-start.54
  401.8 11.2 %collective-permute-done.54 = bf16[48,768]{1,0:T(8,128)(2,1)S(1)} collective-permute-done((bf16[48,768]{1,0:T(8,128)(2,1)S(1)}, bf16[48,768]{1,0:T(8,128)(2,1)S(1)}, u32[]{:S(2)}, u32[]{:S(2)}) %collective-permute-start.54) | collective-permute-done | bytes 73760 | tf_op jit(solution)/shard_map/ppermute | solution.py:869
  413.1 1.6 fusion.40
  414.7 3.6 collective-permute-done.55
  422.7 1.8 copy.55
  (302 shorter events, 65.2 us)
Async XLA Ops:
  2.1 17.1 %collective-permute-start.1 = (bf16[2,192]{1,0:T(2,128)(2,1)S(1)}, bf16[2,192]{1,0:T(2,128)(2,1)S(1)}, u32[]{:S(2)}, u32[]{:S(2)}) collective-permute-start(bf16[2,192]{1,0:T(2,128)(2,1)S(1)} %pad_maximum_fusion.11.n0), channel_id=1, source_target_pairs={{0,16},{8,24},{16,0},{24,8},{1,17},{9,25},{17,1},{25,9},{2,18},{10... | collective-permute-start | bytes 2312 | tf_op jit(solution)/shard_map/ppermute | solution.py:869
  5.1 16.3 %collective-permute-start = (bf16[2,192]{1,0:T(2,128)(2,1)S(1)}, bf16[2,192]{1,0:T(2,128)(2,1)S(1)}, u32[]{:S(2)}, u32[]{:S(2)}) collective-permute-start(bf16[2,192]{1,0:T(2,128)(2,1)S(1)} %pad_maximum_fusion.11.n0), channel_id=1, source_target_pairs={{0,8},{8,0},{16,24},{24,16},{1,9},{9,1},{17,25},{25,17},{2,10},{10... | collective-permute-start | bytes 2312 | tf_op jit(solution)/shard_map/ppermute | solution.py:869
  5.1 9.6 %collective-permute-start.4 = (bf16[192,768]{1,0:T(8,128)(2,1)}, bf16[192,768]{1,0:T(8,128)(2,1)S(1)}, u32[]{:S(2)}, u32[]{:S(2)}) collective-permute-start(bf16[192,768]{1,0:T(8,128)(2,1)} %k0.1), channel_id=1, source_target_pairs={{0,16},{8,24},{16,0},{24,8},{1,17},{9,25},{17,1},{25,9},{2,18},{10... | collective-permute-start | bytes 884744 | tf_op jit(solution)/shard_map/ppermute | solution.py:869
  5.3 18.2 %collective-permute-start.3 = (bf16[192,768]{1,0:T(8,128)(2,1)}, bf16[192,768]{1,0:T(8,128)(2,1)S(1)}, u32[]{:S(2)}, u32[]{:S(2)}) collective-permute-start(bf16[192,768]{1,0:T(8,128)(2,1)} %k0.1), channel_id=1, source_target_pairs={{0,8},{8,0},{16,24},{24,16},{1,9},{9,1},{17,25},{25,17},{2,10},{10... | collective-permute-start | bytes 884744 | tf_op jit(solution)/shard_map/ppermute | solution.py:869
  14.8 3.8 collective-permute-start.13
  15.1 4.8 %collective-permute-start.12 = (bf16[104,128]{1,0:T(8,128)(2,1)S(1)}, bf16[104,128]{1,0:T(8,128)(2,1)S(1)}, u32[]{:S(2)}, u32[]{:S(2)}) collective-permute-start(bf16[104,128]{1,0:T(8,128)(2,1)S(1)} %pad_bitcast_fusion), channel_id=1, source_target_pairs={{0,8},{8,0},{16,24},{24,16},{1,9},{9,1},{17,25},{25,17},{2,10},{10... | collective-permute-start | bytes 79880 | tf_op jit(solution)/shard_map/ppermute | solution.py:869
  18.6 1.6 collective-permute-start.14
  19.2 4.1 collective-permute-start.2
  19.8 10.1 %collective-permute-start.10 = (bf16[192,768]{1,0:T(8,128)(2,1)}, bf16[192,768]{1,0:T(8,128)(2,1)S(1)}, u32[]{:S(2)}, u32[]{:S(2)}) collective-permute-start(bf16[192,768]{1,0:T(8,128)(2,1)} %v0.1), channel_id=1, source_target_pairs={{0,16},{8,24},{16,0},{24,8},{1,17},{9,25},{17,1},{25,9},{2,18},{10... | collective-permute-start | bytes 884744 | tf_op jit(solution)/shard_map/ppermute | solution.py:869
  20.2 10.5 %collective-permute-start.5 = (bf16[192,768]{1,0:T(8,128)(2,1)S(1)}, bf16[192,768]{1,0:T(8,128)(2,1)S(1)}, u32[]{:S(2)}, u32[]{:S(2)}) collective-permute-start(bf16[192,768]{1,0:T(8,128)(2,1)S(1)} %collective-permute-done.4.w2.k2), channel_id=1, source_target_pairs={{0,8},{8,0},{16,24},{24,16},{1,9},{9,1},{17,25},{25,17},{2,10},{10... | collective-permute-start | bytes 884744 | tf_op jit(solution)/shard_map/ppermute | solution.py:869
  21.5 26.1 %collective-permute-start.7 = (bf16[192,768]{1,0:T(8,128)(2,1)S(1)}, bf16[192,768]{1,0:T(8,128)(2,1)S(1)}, u32[]{:S(2)}, u32[]{:S(2)}) collective-permute-start(bf16[192,768]{1,0:T(8,128)(2,1)S(1)} %copy-done.10), channel_id=1, source_target_pairs={{0,16},{8,24},{16,0},{24,8},{1,17},{9,25},{17,1},{25,9},{2,18},{10... | collective-permute-start | bytes 884744 | tf_op jit(solution)/shard_map/ppermute | solution.py:869
  23.3 24.9 %collective-permute-start.6 = (bf16[192,768]{1,0:T(8,128)(2,1)S(1)}, bf16[192,768]{1,0:T(8,128)(2,1)S(1)}, u32[]{:S(2)}, u32[]{:S(2)}) collective-permute-start(bf16[192,768]{1,0:T(8,128)(2,1)S(1)} %copy-done.10), channel_id=1, source_target_pairs={{0,8},{8,0},{16,24},{24,16},{1,9},{9,1},{17,25},{25,17},{2,10},{10... | collective-permute-start | bytes 884744 | tf_op jit(solution)/shard_map/ppermute | solution.py:869
  23.5 24.8 %collective-permute-start.9 = (bf16[192,768]{1,0:T(8,128)(2,1)S(1)}, bf16[192,768]{1,0:T(8,128)(2,1)}, u32[]{:S(2)}, u32[]{:S(2)}) collective-permute-start(bf16[192,768]{1,0:T(8,128)(2,1)S(1)} %copy-done.11), channel_id=1, source_target_pairs={{0,8},{8,0},{16,24},{24,16},{1,9},{9,1},{17,25},{25,17},{2,10},{10... | collective-permute-start | bytes 884744 | tf_op jit(solution)/shard_map/ppermute | solution.py:869
  30.0 18.8 %collective-permute-start.16 = (bf16[192,768]{1,0:T(8,128)(2,1)}, bf16[192,768]{1,0:T(8,128)(2,1)}, u32[]{:S(2)}, u32[]{:S(2)}) collective-permute-start(bf16[192,768]{1,0:T(8,128)(2,1)} %o0), channel_id=1, source_target_pairs={{0,16},{8,24},{16,0},{24,8},{1,17},{9,25},{17,1},{25,9},{2,18},{10... | collective-permute-start | bytes 884744 | tf_op jit(solution)/shard_map/ppermute | solution.py:869
  30.8 46.6 %collective-permute-start.15 = (bf16[192,3072]{1,0:T(8,128)(2,1)}, bf16[192,3072]{1,0:T(8,128)(2,1)}, u32[]{:S(2)}, u32[]{:S(2)}) collective-permute-start(bf16[192,3072]{1,0:T(8,128)(2,1)} %u0), channel_id=1, source_target_pairs={{0,16},{8,24},{16,0},{24,8},{1,17},{9,25},{17,1},{25,9},{2,18},{10... | collective-permute-start | bytes 3538952 | tf_op jit(solution)/shard_map/ppermute | solution.py:869
  41.2 43.9 %all-to-all-start = ((bf16[8,192,256]{2,1,0:T(8,128)(2,1)}), bf16[8,192,256]{2,1,0:T(8,128)(2,1)S(1)}, u32[]{:S(2)}, u32[]{:S(2)}) async-start(bf16[8,192,256]{2,1,0:T(8,128)(2,1)} %get-tuple-element.102), calls=%async_computation | async-start | bytes 1572864 | tf_op jit(solution)/shard_map/all_to_all | solution.py:1029
  47.6 67.8 %collective-permute-start.25 = (bf16[768,768]{1,0:T(8,128)(2,1)S(1)}, bf16[768,768]{1,0:T(8,128)(2,1)}, u32[]{:S(2)}, u32[]{:S(2)}) collective-permute-start(bf16[768,768]{1,0:T(8,128)(2,1)S(1)} %copy-done.5), channel_id=1, source_target_pairs={{0,16},{8,24},{16,0},{24,8},{1,17},{9,25},{17,1},{25,9},{2,18},{10... | collective-permute-start | bytes 3538952 | tf_op jit(solution)/shard_map/ppermute | solution.py:869
  48.2 3.9 collective-permute-start.11
  48.3 3.9 collective-permute-start.8
  48.8 13.5 %collective-permute-start.17 = (bf16[192,768]{1,0:T(8,128)(2,1)}, bf16[192,768]{1,0:T(8,128)(2,1)}, u32[]{:S(2)}, u32[]{:S(2)}) collective-permute-start(bf16[192,768]{1,0:T(8,128)(2,1)} %collective-permute-done.16.o2), channel_id=1, source_target_pairs={{0,8},{8,0},{16,24},{24,16},{1,9},{9,1},{17,25},{25,17},{2,10},{10... | collective-permute-start | bytes 884744 | tf_op jit(solution)/shard_map/ppermute | solution.py:869
  58.7 8.2 %collective-permute-start.18 = (bf16[384,256]{1,0:T(8,128)(2,1)}, bf16[384,256]{1,0:T(8,128)(2,1)S(1)}, u32[]{:S(2)}, u32[]{:S(2)}) collective-permute-start(bf16[384,256]{1,0:T(8,128)(2,1)} %get-tuple-element.107), channel_id=1, source_target_pairs={{0,1},{1,0},{2,3},{3,2},{4,5},{5,4},{6,7},{7,6},{8,9},{9,8},{10,11... | collective-permute-start | bytes 589832 | tf_op jit(solution)/shard_map/ppermute | solution.py:869
  60.8 9.1 %collective-permute-start.19 = (bf16[384,256]{1,0:T(8,128)(2,1)}, bf16[384,256]{1,0:T(8,128)(2,1)S(1)}, u32[]{:S(2)}, u32[]{:S(2)}) collective-permute-start(bf16[384,256]{1,0:T(8,128)(2,1)} %get-tuple-element.108), channel_id=1, source_target_pairs={{0,2},{1,3},{2,0},{3,1},{4,6},{5,7},{6,4},{7,5},{8,10},{9,11},{10,... | collective-permute-start | bytes 589832 | tf_op jit(solution)/shard_map/ppermute | solution.py:869
  62.3 12.8 %collective-permute-start.20 = (bf16[384,256]{1,0:T(8,128)(2,1)}, bf16[384,256]{1,0:T(8,128)(2,1)S(1)}, u32[]{:S(2)}, u32[]{:S(2)}) collective-permute-start(bf16[384,256]{1,0:T(8,128)(2,1)} %get-tuple-element.109), channel_id=1, source_target_pairs={{0,3},{1,2},{2,1},{3,0},{4,7},{5,6},{6,5},{7,4},{8,11},{9,10},{10,... | collective-permute-start | bytes 589832 | tf_op jit(solution)/shard_map/ppermute | solution.py:869
  67.0 31.1 %collective-permute-start.21 = (bf16[384,256]{1,0:T(8,128)(2,1)}, bf16[384,256]{1,0:T(8,128)(2,1)S(1)}, u32[]{:S(2)}, u32[]{:S(2)}) collective-permute-start(bf16[384,256]{1,0:T(8,128)(2,1)} %get-tuple-element.110), channel_id=1, source_target_pairs={{0,4},{1,5},{2,6},{3,7},{4,0},{5,1},{6,2},{7,3},{8,12},{9,13},{10,... | collective-permute-start | bytes 589832 | tf_op jit(solution)/shard_map/ppermute | solution.py:869
  69.9 28.8 %collective-permute-start.22 = (bf16[384,256]{1,0:T(8,128)(2,1)}, bf16[384,256]{1,0:T(8,128)(2,1)S(1)}, u32[]{:S(2)}, u32[]{:S(2)}) collective-permute-start(bf16[384,256]{1,0:T(8,128)(2,1)} %get-tuple-element.111), channel_id=1, source_target_pairs={{0,5},{1,4},{2,7},{3,6},{4,1},{5,0},{6,3},{7,2},{8,13},{9,12},{10,... | collective-permute-start | bytes 589832 | tf_op jit(solution)/shard_map/ppermute | solution.py:869
  75.1 23.5 %collective-permute-start.23 = (bf16[384,256]{1,0:T(8,128)(2,1)}, bf16[384,256]{1,0:T(8,128)(2,1)S(1)}, u32[]{:S(2)}, u32[]{:S(2)}) collective-permute-start(bf16[384,256]{1,0:T(8,128)(2,1)} %get-tuple-element.112), channel_id=1, source_target_pairs={{0,6},{1,7},{2,4},{3,5},{4,2},{5,3},{6,0},{7,1},{8,14},{9,15},{10,... | collective-permute-start | bytes 589832 | tf_op jit(solution)/shard_map/ppermute | solution.py:869
  77.4 21.2 %collective-permute-start.24 = (bf16[384,256]{1,0:T(8,128)(2,1)}, bf16[384,256]{1,0:T(8,128)(2,1)S(1)}, u32[]{:S(2)}, u32[]{:S(2)}) collective-permute-start(bf16[384,256]{1,0:T(8,128)(2,1)} %get-tuple-element.113), channel_id=1, source_target_pairs={{0,7},{1,6},{2,5},{3,4},{4,3},{5,2},{6,1},{7,0},{8,15},{9,14},{10,... | collective-permute-start | bytes 589832 | tf_op jit(solution)/shard_map/ppermute | solution.py:869
  115.4 29.1 %all-to-all-start.1 = ((bf16[8,192,256]{2,1,0:T(8,128)(2,1)}), bf16[8,192,256]{2,1,0:T(8,128)(2,1)S(1)}, u32[]{:S(2)}, u32[]{:S(2)}) async-start(bf16[8,192,256]{2,1,0:T(8,128)(2,1)} %mix_fwd.1), calls=%async_computation.1 | async-start | bytes 1572864 | tf_op jit(solution)/shard_map/all_to_all | solution.py:1029
  124.9 7.0 %collective-permute-start.29 = (bf16[768,768]{1,0:T(8,128)(2,1)S(1)}, bf16[768,768]{1,0:T(8,128)(2,1)}, u32[]{:S(2)}, u32[]{:S(2)}) collective-permute-start(bf16[768,768]{1,0:T(8,128)(2,1)S(1)} %copy-done.5), channel_id=1, source_target_pairs={{0,8},{8,0},{16,24},{24,16},{1,9},{9,1},{17,25},{25,17},{2,10},{10... | collective-permute-start | bytes 3538952 | tf_op jit(solution)/shard_map/ppermute | solution.py:869
  124.9 6.9 %collective-permute-start.27 = (bf16[192,3072]{1,0:T(8,128)(2,1)}, bf16[192,3072]{1,0:T(8,128)(2,1)S(1)}, u32[]{:S(2)}, u32[]{:S(2)}) collective-permute-start(bf16[192,3072]{1,0:T(8,128)(2,1)} %u0), channel_id=1, source_target_pairs={{0,8},{8,0},{16,24},{24,16},{1,9},{9,1},{17,25},{25,17},{2,10},{10... | collective-permute-start | bytes 3538952 | tf_op jit(solution)/shard_map/ppermute | solution.py:869
  125.4 6.5 %collective-permute-start.30 = (bf16[768,768]{1,0:T(8,128)(2,1)}, bf16[768,768]{1,0:T(8,128)(2,1)}, u32[]{:S(2)}, u32[]{:S(2)}) collective-permute-start(bf16[768,768]{1,0:T(8,128)(2,1)} %collective-permute-done.25.d2), channel_id=1, source_target_pairs={{0,8},{8,0},{16,24},{24,16},{1,9},{9,1},{17,25},{25,17},{2,10},{10... | collective-permute-start | bytes 3538952 | tf_op jit(solution)/shard_map/ppermute | solution.py:869
  125.5 8.1 %collective-permute-start.28 = (bf16[192,3072]{1,0:T(8,128)(2,1)}, bf16[192,3072]{1,0:T(8,128)(2,1)}, u32[]{:S(2)}, u32[]{:S(2)}) collective-permute-start(bf16[192,3072]{1,0:T(8,128)(2,1)} %collective-permute-done.15.u2), channel_id=1, source_target_pairs={{0,8},{8,0},{16,24},{24,16},{1,9},{9,1},{17,25},{25,17},{2,10},{10... | collective-permute-start | bytes 3538952 | tf_op jit(solution)/shard_map/ppermute | solution.py:869
  125.9 5.9 %collective-permute-start.26 = (bf16[192,768]{1,0:T(8,128)(2,1)}, bf16[192,768]{1,0:T(8,128)(2,1)S(1)}, u32[]{:S(2)}, u32[]{:S(2)}) collective-permute-start(bf16[192,768]{1,0:T(8,128)(2,1)} %o0), channel_id=1, source_target_pairs={{0,8},{8,0},{16,24},{24,16},{1,9},{9,1},{17,25},{25,17},{2,10},{10... | collective-permute-start | bytes 884744 | tf_op jit(solution)/shard_map/ppermute | solution.py:869
  171.7 4.7 %collective-permute-start.31 = (bf16[2,768,768]{2,1,0:T(8,128)(2,1)}, bf16[2,768,768]{2,1,0:T(8,128)(2,1)S(1)}, u32[]{:S(2)}, u32[]{:S(2)}) collective-permute-start(bf16[2,768,768]{2,1,0:T(8,128)(2,1)} %get-tuple-element.120), channel_id=1, source_target_pairs={{0,8},{8,0},{16,24},{24,16},{1,9},{9,1},{17,25},{25,17},{2,10},{10... | collective-permute-start | bytes 7077896 | tf_op jit(solution)/shard_map/ppermute | solution.py:869
  171.7 24.8 %all-to-all-start.2 = ((bf16[8,192,256]{2,1,0:T(8,128)(2,1)}), bf16[8,192,256]{2,1,0:T(8,128)(2,1)S(1)}, u32[]{:S(2)}, u32[]{:S(2)}) async-start(bf16[8,192,256]{2,1,0:T(8,128)(2,1)} %get-tuple-element.126), calls=%async_computation.2 | async-start | bytes 1572864 | tf_op jit(solution)/shard_map/all_to_all | solution.py:1029
  196.5 5.6 %collective-permute-start.32 = (bf16[2,960,768]{2,1,0:T(8,128)(2,1)}, bf16[2,960,768]{2,1,0:T(8,128)(2,1)S(1)}, u32[]{:S(2)}, u32[]{:S(2)}) collective-permute-start(bf16[2,960,768]{2,1,0:T(8,128)(2,1)} %get-tuple-element.130), channel_id=1, source_target_pairs={{0,8},{8,0},{16,24},{24,16},{1,9},{9,1},{17,25},{25,17},{2,10},{10... | collective-permute-start | bytes 8847368 | tf_op jit(solution)/shard_map/ppermute | solution.py:869
  196.5 43.2 %collective-permute-start.33 = (bf16[2,384,768]{2,1,0:T(8,128)(2,1)}, bf16[2,384,768]{2,1,0:T(8,128)(2,1)S(1)}, u32[]{:S(2)}, u32[]{:S(2)}) collective-permute-start(bf16[2,384,768]{2,1,0:T(8,128)(2,1)} %get-tuple-element.219), channel_id=1, source_target_pairs={{0,1},{1,0},{2,3},{3,2},{4,5},{5,4},{6,7},{7,6},{8,9},{9,8},{10,11... | collective-permute-start | bytes 3538952 | tf_op jit(solution)/shard_map/ppermute | solution.py:869
  206.1 39.6 %collective-permute-start.34 = (bf16[960,768]{1,0:T(8,128)(2,1)}, bf16[960,768]{1,0:T(8,128)(2,1)}, u32[]{:S(2)}, u32[]{:S(2)}) collective-permute-start(bf16[960,768]{1,0:T(8,128)(2,1)} %get-tuple-element.217), channel_id=1, source_target_pairs={{0,16},{8,24},{16,0},{24,8},{1,17},{9,25},{17,1},{25,9},{2,18},{10... | collective-permute-start | bytes 4423688 | tf_op jit(solution)/shard_map/ppermute | solution.py:869
  241.1 31.3 %collective-permute-start.35 = (bf16[384,768]{1,0:T(8,128)(2,1)}, bf16[384,768]{1,0:T(8,128)(2,1)}, u32[]{:S(2)}, u32[]{:S(2)}) collective-permute-start(bf16[384,768]{1,0:T(8,128)(2,1)} %get-tuple-element.231), channel_id=1, source_target_pairs={{0,16},{8,24},{16,0},{24,8},{1,17},{9,25},{17,1},{25,9},{2,18},{10... | collective-permute-start | bytes 1769480 | tf_op jit(solution)/shard_map/ppermute | solution.py:869
  241.6 47.9 %all-to-all-start.3 = ((bf16[8,384,256]{2,1,0:T(8,128)(2,1)}), bf16[8,384,256]{2,1,0:T(8,128)(2,1)S(1)}, u32[]{:S(2)}, u32[]{:S(2)}) async-start(bf16[8,384,256]{2,1,0:T(8,128)(2,1)} %get-tuple-element.138), calls=%async_computation.3 | async-start | bytes 3145728 | tf_op jit(solution)/shard_map/all_to_all | solution.py:1029
  248.5 32.1 %collective-permute-start.36 = (bf16[480,768]{1,0:T(8,128)(2,1)}, bf16[480,768]{1,0:T(8,128)(2,1)}, u32[]{:S(2)}, u32[]{:S(2)}) collective-permute-start(bf16[480,768]{1,0:T(8,128)(2,1)} %get-tuple-element.223), channel_id=1, source_target_pairs={{0,1},{1,0},{2,3},{3,2},{4,5},{5,4},{6,7},{7,6},{8,9},{9,8},{10,11... | collective-permute-start | bytes 2211848 | tf_op jit(solution)/shard_map/ppermute | solution.py:869
  273.6 15.7 %collective-permute-start.37 = (bf16[192,768]{1,0:T(8,128)(2,1)S(1)}, bf16[192,768]{1,0:T(8,128)(2,1)S(1)}, u32[]{:S(2)}, u32[]{:S(2)}) collective-permute-start(bf16[192,768]{1,0:T(8,128)(2,1)S(1)} %get-tuple-element.249), channel_id=1, source_target_pairs={{0,2},{1,3},{2,0},{3,1},{4,6},{5,7},{6,4},{7,5},{8,10},{9,11},{10,... | collective-permute-start | bytes 884744 | tf_op jit(solution)/shard_map/ppermute | solution.py:869
  298.0 7.1 %collective-permute-start.38 = (bf16[2,384,768]{2,1,0:T(8,128)(2,1)}, bf16[2,384,768]{2,1,0:T(8,128)(2,1)}, u32[]{:S(2)}, u32[]{:S(2)}) collective-permute-start(bf16[2,384,768]{2,1,0:T(8,128)(2,1)} %get-tuple-element.149), channel_id=1, source_target_pairs={{0,8},{8,0},{16,24},{24,16},{1,9},{9,1},{17,25},{25,17},{2,10},{10... | collective-permute-start | bytes 3538952 | tf_op jit(solution)/shard_map/ppermute | solution.py:869
  298.1 28.5 %all-to-all-start.4 = ((bf16[8,192,256]{2,1,0:T(8,128)(2,1)}), bf16[8,192,256]{2,1,0:T(8,128)(2,1)S(1)}, u32[]{:S(2)}, u32[]{:S(2)}) async-start(bf16[8,192,256]{2,1,0:T(8,128)(2,1)} %get-tuple-element.146), calls=%async_computation.4 | async-start | bytes 1572864 | tf_op jit(solution)/shard_map/all_to_all | solution.py:1029
  303.0 23.4 %collective-permute-start.39 = (bf16[240,768]{1,0:T(8,128)(2,1)}, bf16[240,768]{1,0:T(8,128)(2,1)S(1)}, u32[]{:S(2)}, u32[]{:S(2)}) collective-permute-start(bf16[240,768]{1,0:T(8,128)(2,1)} %get-tuple-element.239), channel_id=1, source_target_pairs={{0,2},{1,3},{2,0},{3,1},{4,6},{5,7},{6,4},{7,5},{8,10},{9,11},{10,... | collective-permute-start | bytes 1105928 | tf_op jit(solution)/shard_map/ppermute | solution.py:869
  334.9 14.8 %collective-permute-start.41 = (bf16[2,256,768]{2,1,0:T(8,128)(2,1)}, bf16[2,256,768]{2,1,0:T(8,128)(2,1)S(1)}, u32[]{:S(2)}, u32[]{:S(2)}) collective-permute-start(bf16[2,256,768]{2,1,0:T(8,128)(2,1)} %get-tuple-element.157), channel_id=1, source_target_pairs={{0,8},{8,0},{16,24},{24,16},{1,9},{9,1},{17,25},{25,17},{2,10},{10... | collective-permute-start | bytes 2359304 | tf_op jit(solution)/shard_map/ppermute | solution.py:869
  335.0 14.6 %collective-permute-start.40 = (bf16[96,768]{1,0:T(8,128)(2,1)S(1)}, bf16[96,768]{1,0:T(8,128)(2,1)S(1)}, u32[]{:S(2)}, u32[]{:S(2)}) collective-permute-start(bf16[96,768]{1,0:T(8,128)(2,1)S(1)} %get-tuple-element.261), channel_id=1, source_target_pairs={{0,4},{1,5},{2,6},{3,7},{4,0},{5,1},{6,2},{7,3},{8,12},{9,13},{10,... | collective-permute-start | bytes 442376 | tf_op jit(solution)/shard_map/ppermute | solution.py:869
  337.4 19.3 %collective-permute-start.42 = (bf16[120,768]{1,0:T(8,128)(2,1)S(1)}, bf16[120,768]{1,0:T(8,128)(2,1)S(1)}, u32[]{:S(2)}, u32[]{:S(2)}) collective-permute-start(bf16[120,768]{1,0:T(8,128)(2,1)S(1)} %get-tuple-element.253), channel_id=1, source_target_pairs={{0,4},{1,5},{2,6},{3,7},{4,0},{5,1},{6,2},{7,3},{8,12},{9,13},{10,... | collective-permute-start | bytes 552968 | tf_op jit(solution)/shard_map/ppermute | solution.py:869
  337.9 18.8 %collective-permute-start.43 = (bf16[384,768]{1,0:T(8,128)(2,1)S(1)}, bf16[384,768]{1,0:T(8,128)(2,1)S(1)}, u32[]{:S(2)}, u32[]{:S(2)}) collective-permute-start(bf16[384,768]{1,0:T(8,128)(2,1)S(1)} %get-tuple-element.229), channel_id=1, source_target_pairs={{0,16},{8,24},{16,0},{24,8},{1,17},{9,25},{17,1},{25,9},{2,18},{10... | collective-permute-start | bytes 1769480 | tf_op jit(solution)/shard_map/ppermute | solution.py:869
  349.6 14.2 %collective-permute-start.44 = (bf16[96,768]{1,0:T(8,128)(2,1)S(1)}, bf16[96,768]{1,0:T(8,128)(2,1)S(1)}, u32[]{:S(2)}, u32[]{:S(2)}) collective-permute-start(bf16[96,768]{1,0:T(8,128)(2,1)S(1)} %add_convert_fusion.15), channel_id=1, source_target_pairs={{0,4},{1,5},{2,6},{3,7},{4,0},{5,1},{6,2},{7,3},{8,12},{9,13},{10,... | collective-permute-start | bytes 442376 | tf_op jit(solution)/shard_map/ppermute | solution.py:869
  351.1 12.8 %collective-permute-start.45 = (bf16[256,768]{1,0:T(8,128)(2,1)S(1)}, bf16[256,768]{1,0:T(8,128)(2,1)S(1)}, u32[]{:S(2)}, u32[]{:S(2)}) collective-permute-start(bf16[256,768]{1,0:T(8,128)(2,1)S(1)} %get-tuple-element.235), channel_id=1, source_target_pairs={{0,16},{8,24},{16,0},{24,8},{1,17},{9,25},{17,1},{25,9},{2,18},{10... | collective-permute-start | bytes 1179656 | tf_op jit(solution)/shard_map/ppermute | solution.py:869
  356.7 10.8 %collective-permute-start.46 = (bf16[120,768]{1,0:T(8,128)(2,1)S(1)}, bf16[120,768]{1,0:T(8,128)(2,1)S(1)}, u32[]{:S(2)}, u32[]{:S(2)}) collective-permute-start(bf16[120,768]{1,0:T(8,128)(2,1)S(1)} %add_convert_fusion.13), channel_id=1, source_target_pairs={{0,4},{1,5},{2,6},{3,7},{4,0},{5,1},{6,2},{7,3},{8,12},{9,13},{10,... | collective-permute-start | bytes 552968 | tf_op jit(solution)/shard_map/ppermute | solution.py:869
  357.0 10.7 %collective-permute-start.47 = (bf16[192,768]{1,0:T(8,128)(2,1)S(1)}, bf16[192,768]{1,0:T(8,128)(2,1)S(1)}, u32[]{:S(2)}, u32[]{:S(2)}) collective-permute-start(bf16[192,768]{1,0:T(8,128)(2,1)S(1)} %get-tuple-element.247), channel_id=1, source_target_pairs={{0,1},{1,0},{2,3},{3,2},{4,5},{5,4},{6,7},{7,6},{8,9},{9,8},{10,11... | collective-permute-start | bytes 884744 | tf_op jit(solution)/shard_map/ppermute | solution.py:869
  363.8 10.5 %collective-permute-start.48 = (bf16[192,768]{1,0:T(8,128)(2,1)S(1)}, bf16[192,768]{1,0:T(8,128)(2,1)S(1)}, u32[]{:S(2)}, u32[]{:S(2)}) collective-permute-start(bf16[192,768]{1,0:T(8,128)(2,1)S(1)} %pad_maximum_fusion.5), channel_id=1, source_target_pairs={{0,2},{1,3},{2,0},{3,1},{4,6},{5,7},{6,4},{7,5},{8,10},{9,11},{10,... | collective-permute-start | bytes 884744 | tf_op jit(solution)/shard_map/ppermute | solution.py:869
  367.6 16.8 %collective-permute-start.49 = (bf16[240,768]{1,0:T(8,128)(2,1)S(1)}, bf16[240,768]{1,0:T(8,128)(2,1)S(1)}, u32[]{:S(2)}, u32[]{:S(2)}) collective-permute-start(bf16[240,768]{1,0:T(8,128)(2,1)S(1)} %pad_maximum_fusion.4), channel_id=1, source_target_pairs={{0,2},{1,3},{2,0},{3,1},{4,6},{5,7},{6,4},{7,5},{8,10},{9,11},{10,... | collective-permute-start | bytes 1105928 | tf_op jit(solution)/shard_map/ppermute | solution.py:869
  367.8 23.4 %collective-permute-start.50 = (bf16[96,768]{1,0:T(8,128)(2,1)S(1)}, bf16[96,768]{1,0:T(8,128)(2,1)S(1)}, u32[]{:S(2)}, u32[]{:S(2)}) collective-permute-start(bf16[96,768]{1,0:T(8,128)(2,1)S(1)} %get-tuple-element.257), channel_id=1, source_target_pairs={{0,2},{1,3},{2,0},{3,1},{4,6},{5,7},{6,4},{7,5},{8,10},{9,11},{10,... | collective-permute-start | bytes 442376 | tf_op jit(solution)/shard_map/ppermute | solution.py:869
  369.8 21.3 %all-to-all-start.5 = ((bf16[8,32,768]{2,1,0:T(8,128)(2,1)}), bf16[8,32,768]{2,1,0:T(8,128)(2,1)S(1)}, u32[]{:S(2)}, u32[]{:S(2)}) async-start(bf16[8,32,768]{2,1,0:T(8,128)(2,1)} %bitcast.44), calls=%async_computation.5 | async-start | bytes 786432 | tf_op jit(solution)/shard_map/all_to_all | solution.py:981
  374.5 27.3 %collective-permute-start.51 = (bf16[384,768]{1,0:T(8,128)(2,1)S(1)}, bf16[384,768]{1,0:T(8,128)(2,1)S(1)}, u32[]{:S(2)}, u32[]{:S(2)}) collective-permute-start(bf16[384,768]{1,0:T(8,128)(2,1)S(1)} %pad_maximum_fusion.3), channel_id=1, source_target_pairs={{0,1},{1,0},{2,3},{3,2},{4,5},{5,4},{6,7},{7,6},{8,9},{9,8},{10,11... | collective-permute-start | bytes 1769480 | tf_op jit(solution)/shard_map/ppermute | solution.py:869
  391.2 7.5 %collective-permute-start.53 = (bf16[48,768]{1,0:T(8,128)(2,1)S(1)}, bf16[48,768]{1,0:T(8,128)(2,1)S(1)}, u32[]{:S(2)}, u32[]{:S(2)}) collective-permute-start(bf16[48,768]{1,0:T(8,128)(2,1)S(1)} %get-tuple-element.265), channel_id=1, source_target_pairs={{0,4},{1,5},{2,6},{3,7},{4,0},{5,1},{6,2},{7,3},{8,12},{9,13},{10,... | collective-permute-start | bytes 221192 | tf_op jit(solution)/shard_map/ppermute | solution.py:869
  391.6 28.3 %collective-permute-start.52 = (bf16[480,768]{1,0:T(8,128)(2,1)S(1)}, bf16[480,768]{1,0:T(8,128)(2,1)S(1)}, u32[]{:S(2)}, u32[]{:S(2)}) collective-permute-start(bf16[480,768]{1,0:T(8,128)(2,1)S(1)} %pad_maximum_fusion.2), channel_id=1, source_target_pairs={{0,1},{1,0},{2,3},{3,2},{4,5},{5,4},{6,7},{7,6},{8,9},{9,8},{10,11... | collective-permute-start | bytes 2211848 | tf_op jit(solution)/shard_map/ppermute | solution.py:869
  394.1 32.2 %all-to-all-start.6 = ((bf16[8,32,768]{2,1,0:T(8,128)(2,1)}), bf16[8,32,768]{2,1,0:T(8,128)(2,1)S(1)}, u32[]{:S(2)}, u32[]{:S(2)}) async-start(bf16[8,32,768]{2,1,0:T(8,128)(2,1)} %broadcast_in_dim.108), calls=%async_computation.6 | async-start | bytes 786432 | tf_op jit(solution)/shard_map/all_to_all | solution.py:988
  398.8 14.2 %collective-permute-start.54 = (bf16[48,768]{1,0:T(8,128)(2,1)S(1)}, bf16[48,768]{1,0:T(8,128)(2,1)S(1)}, u32[]{:S(2)}, u32[]{:S(2)}) collective-permute-start(bf16[48,768]{1,0:T(8,128)(2,1)S(1)} %add_convert_fusion.16), channel_id=1, source_target_pairs={{0,4},{1,5},{2,6},{3,7},{4,0},{5,1},{6,2},{7,3},{8,12},{9,13},{10,... | collective-permute-start | bytes 221192 | tf_op jit(solution)/shard_map/ppermute | solution.py:869
  413.0 5.2 %collective-permute-start.55 = (bf16[96,768]{1,0:T(8,128)(2,1)S(1)}, bf16[96,768]{1,0:T(8,128)(2,1)S(1)}, u32[]{:S(2)}, u32[]{:S(2)}) collective-permute-start(bf16[96,768]{1,0:T(8,128)(2,1)S(1)} %pad_maximum_fusion.7), channel_id=1, source_target_pairs={{0,2},{1,3},{2,0},{3,1},{4,6},{5,7},{6,4},{7,5},{8,10},{9,11},{10,... | collective-permute-start | bytes 442376 | tf_op jit(solution)/shard_map/ppermute | solution.py:869
  418.3 6.8 %collective-permute-start.56 = (bf16[192,768]{1,0:T(8,128)(2,1)S(1)}, bf16[192,768]{1,0:T(8,128)(2,1)S(1)}, u32[]{:S(2)}, u32[]{:S(2)}) collective-permute-start(bf16[192,768]{1,0:T(8,128)(2,1)S(1)} %pad_maximum_fusion.6), channel_id=1, source_target_pairs={{0,1},{1,0},{2,3},{3,2},{4,5},{5,4},{6,7},{7,6},{8,9},{9,8},{10,11... | collective-permute-start | bytes 884744 | tf_op jit(solution)/shard_map/ppermute | solution.py:869
  (45 other events, 549.8 us)
where the time goes:
time: 437 us; the launch traced here: 431 us
  Pallas kernels  144 us (33%)
  waiting for transfers between devices  125 us (29%)
  starting transfers between devices  92.5 us (21%)
  local copies, waits for them, and re-layouts  38.6 us (9%)
  other arithmetic  30.1 us (7%)
    ppermute x57, waiting for transfers between devices, xor_permute(): lax.ppermute(value, axis, [(source, source ^ mask) for source in range(co...  103 us
    ppermute x57, starting transfers between devices, xor_permute(): lax.ppermute(value, axis, [(source, source ^ mask) for source in range(co...  54.7 us
    pallas_call x1, Pallas kernels, mix_bwd(): pl.pallas_call(functools.partial(mix_bwd_merged if v_base else mix_bwd_ke...  32.1 us
    all_to_all x5, starting transfers between devices, exchange(): return lax.all_to_all(value, 'dp', 0, 0, axis_index_groups=groups)  28.6 us
    pallas_call x1, Pallas kernels, shift_bwd(): pl.pallas_call(shift_bwd_kernel, out_shape=(jax.ShapeDtypeStruct((SHIFT,...  20.3 us
    pallas_call x1, Pallas kernels, middle_call(): pl.pallas_call(middle_kernel, out_shape=(jax.ShapeDtypeStruct((tokens, wi...  19.7 us
    all_to_all x5, waiting for transfers between devices, exchange(): return lax.all_to_all(value, 'dp', 0, 0, axis_index_groups=groups)  14.9 us
    convert_element_type x17, other arithmetic, add(): return (self.order(self.keep).astype(F32) + came.astype(F32)).astype(BF)  13.6 us
  transfers between devices with their start and end apart: 64, of which 24 were waited for; matrix products, arithmetic and copies ran while one was open for 13% of the time, Pallas kernels for 24%

commit v1 on v0

--- a/solution.py
+++ b/solution.py
@@ -34,7 +34,7 @@
     return pltpu.CompilerParams(vmem_limit_bytes=VMEM_BYTES)
 
 
-SCALE = 1000
+SCALE = 1
 
 
 def cost(micros, moved):
@@ -681,35 +681,9 @@
     )(me, y, x, gain, bias, cot, *o_pieces, *u_pieces, *d_pieces)
 
 
-def down_grads_kernel(me_ref, hidden_ref, cot_ref, keep_ref, send_ref):
-    me = me_ref[0]
-    wide = keep_ref.shape[1]
-    for slot in range(2):
-        for dest, mask in ((keep_ref, 2 * slot), (send_ref, 2 * slot + 1)):
-            part = hidden_ref[:, pl.ds(pl.multiple_of((me ^ mask) * wide, wide), wide)]
-            dest[slot] = mm(turn(part), cot_ref[...]).astype(dest.dtype)
-
-
-def down_grads_call(me, hidden, cot, shards_count):
-    width = cot.shape[1]
-    wide = hidden.shape[1] // shards_count
-    return pl.pallas_call(
-        down_grads_kernel,
-        out_shape=(
-            jax.ShapeDtypeStruct((2, wide, width), BF),
-            jax.ShapeDtypeStruct((2, wide, width), BF),
-        ),
-        in_specs=[smem()] + [vmem()] * 2,
-        out_specs=(vmem(),) * 2,
-        compiler_params=params(),
-        cost_estimate=cost(6, 16 << 20),
-        name="down_grads_call",
-    )(me, hidden, cot)
-
-
-def up_grads_kernel(
-    me_ref, y_ref, resid_ref, act_ref, hidden_ref, gz_ref, gr_ref, d0, d1, d2, d3,
-    out_ref, keep_ref, send_ref, dfull, act_t, low, sem,
+def ffn_grads_kernel(
+    me_ref, y_ref, resid_ref, act_ref, hidden_ref, gz_ref, gr_ref, cot_ref, d0, d1, d2, d3,
+    out_ref, down_keep, down_send, up_keep, up_send, dfull, act_t, low, sem,
 ):
     me = me_ref[0]
     wait_d = load_pieces(me, (d0, d1, d2, d3), dfull, sem, 0)
@@ -717,39 +691,49 @@
     hidden = hidden_ref.shape[1]
     groups = width // y_ref.shape[1]
     share = width // groups
+    wide = hidden // groups
     seqs = tokens // TILE
     act_t[...] = turn(act_ref[...])
     low[...] = gr_ref[...].astype(BF)
     blocks = hidden // width
-    for slot in range(2):
-        for dest, mask in ((keep_ref, 2 * slot), (send_ref, 2 * slot + 1)):
-            owner = me ^ mask
+
+    def body(slot, carry):
+        for down, up, side in ((down_keep, up_keep, 0), (down_send, up_send, 1)):
+            owner = me ^ (2 * slot + side)
+            part = hidden_ref[:, pl.ds(pl.multiple_of(owner * wide, wide), wide)]
+            down[slot] = mm(turn(part), cot_ref[...]).astype(BF)
             part = act_t[pl.ds(pl.multiple_of(owner * share, share), share), :]
             for block in range(blocks):
                 value = mm(part, gz_ref[:, block * width : (block + 1) * width])
-                dest[slot, block * share : (block + 1) * share, :] = value.astype(dest.dtype)
+                up[slot, block * share : (block + 1) * share, :] = value.astype(BF)
             value = mm(y_ref[owner], low[0:TILE, :])
             for seq in range(1, seqs):
                 value = value + mm(y_ref[seq * groups + owner], low[seq * TILE : (seq + 1) * TILE, :])
-            dest[slot, blocks * share : (blocks + 1) * share, :] = value.astype(dest.dtype)
+            up[slot, blocks * share : (blocks + 1) * share, :] = value.astype(BF)
+        return carry
+
+    lax.fori_loop(0, 2, body, 0)
     wait_d()
     out_ref[...] = (resid_ref[...] + mm(hidden_ref[...], dfull[...])).astype(BF)
 
 
-def up_grads_call(me, y, resid, act, hidden, gz, gr, d_pieces):
+def ffn_grads_call(me, y, resid, act, hidden, gz, gr, cot, d_pieces):
     tokens, width = resid.shape
     wide = hidden.shape[1]
     groups = width // y.shape[1]
-    rows = (wide // width + 1) * (width // groups)
+    down_rows = wide // groups
+    up_rows = (wide // width + 1) * (width // groups)
     return pl.pallas_call(
-        up_grads_kernel,
+        ffn_grads_kernel,
         out_shape=(
             jax.ShapeDtypeStruct((tokens, width), BF),
-            jax.ShapeDtypeStruct((2, rows, width), BF),
-            jax.ShapeDtypeStruct((2, rows, width), BF),
+            jax.ShapeDtypeStruct((2, down_rows, width), BF),
+            jax.ShapeDtypeStruct((2, down_rows, width), BF),
+            jax.ShapeDtypeStruct((2, up_rows, width), BF),
+            jax.ShapeDtypeStruct((2, up_rows, width), BF),
         ),
-        in_specs=[smem()] + [vmem()] * 6 + [hbm()] * 4,
-        out_specs=(vmem(),) * 3,
+        in_specs=[smem()] + [vmem()] * 7 + [hbm()] * 4,
+        out_specs=(vmem(),) * 5,
         scratch_shapes=[
             pltpu.VMEM((wide, width), BF),
             pltpu.VMEM((width, tokens), BF),
@@ -757,16 +741,20 @@
             pltpu.SemaphoreType.DMA((4,)),
         ],
         compiler_params=params(),
-        cost_estimate=cost(10, 24 << 20),
-        name="up_grads_call",
-    )(me, y, resid, act, hidden, gz, gr, *d_pieces)
-
-
-def input_grads(me, act_t, grad, share, base, keep_ref, send_ref):
-    for slot in range(2):
-        for dest, mask in ((keep_ref, 2 * slot), (send_ref, 2 * slot + 1)):
-            part = act_t[pl.ds(pl.multiple_of((me ^ mask) * share, share), share), :]
-            dest[slot, base : base + share, :] = mm(part, grad).astype(dest.dtype)
+        cost_estimate=cost(19, 24 << 20),
+        name="ffn_grads_call",
+    )(me, y, resid, act, hidden, gz, gr, cot, *d_pieces)
+
+
+def input_grads(me, act_t, grad_ref, share, base, keep_ref, send_ref):
+    def body(slot, carry):
+        for dest, side in ((keep_ref, 0), (send_ref, 1)):
+            owner = me ^ (2 * slot + side)
+            part = act_t[pl.ds(pl.multiple_of(owner * share, share), share), :]
+            dest[slot, base : base + share, :] = mm(part, grad_ref[...]).astype(dest.dtype)
+        return carry
+
+    lax.fori_loop(0, 2, body, 0)
 
 
 def qv_grads_kernel(
@@ -782,11 +770,11 @@
     seqs = tokens // TILE
     act_t[...] = turn(act_ref[...])
     from_blocks(rows, gqv_ref, seqs, groups)
-    input_grads(me, act_t, rows[...], share, 0, keep_ref, send_ref)
+    input_grads(me, act_t, rows, share, 0, keep_ref, send_ref)
     wait_q()
     ga_ref[...] = mm_nt(rows[...], qfull[...])
     from_blocks(rows, gqv_ref, seqs, groups, share)
-    input_grads(me, act_t, rows[...], share, share, keep_ref, send_ref)
+    input_grads(me, act_t, rows, share, share, keep_ref, send_ref)
     wait_v()
     ga_ref[...] += mm_nt(rows[...], vfull[...])
 
@@ -826,7 +814,7 @@
     share = gk_ref.shape[1]
     act_t[...] = turn(act_ref[...])
     from_blocks(rows, gk_ref, tokens // TILE, width // share)
-    input_grads(me, act_t, rows[...], share, 0, keep_ref, send_ref)
+    input_grads(me, act_t, rows, share, 0, keep_ref, send_ref)
     wait_k()
     ga = ga_ref[...] + mm_nt(rows[...], kfull[...])
     hat, scale = normal_stats(x_ref[...].astype(F32))
@@ -1071,7 +1059,6 @@
     kern, kern_pull = jax.vjp(lambda *leaves: kernel_rows(*leaves, lags, reach), rate, freq, coef, skip)
     kern = kern[:, None, :]
 
-    segments, _ = lax.optimization_barrier((segments, key_w[3]))
     seg_row = lax.dynamic_index_in_dim(segments, seq, 0, keepdims=False)
     seg_wide = jnp.concatenate(
         [jnp.full((span,), -1, jnp.int32), seg_row, jnp.full((HALO,), -2, jnp.int32)]
@@ -1091,7 +1078,7 @@
     k_halo = from_prev(k_own[-1, :, rows - HALO :].T)
     ks_own = shift_fwd(seg_full, k_own, k_halo, taps_tiles)
     forward = Order()
-    forward.mark((ks_own, up_w[2], out_w[3]))
+    forward.mark((ks_own, up_w[2]))
     qv_own = swap_parts(which, qv_parts, "collect_qv", forward)
     if multi:
         ks_win = jnp.concatenate([from_prev(ks_own), ks_own], axis=0)
@@ -1107,13 +1094,14 @@
     )
     gy_own = exchange(gy_mine)
     order = Order()
-    down_sum = Reduction(order, *down_grads_call(which, hidden, cot, fsdp), near_first=True)
-    order.mark(down_sum.move)
+    output, down_keep, down_send, up_keep, up_send = ffn_grads_call(
+        which, y_mine, resid, act_two, hidden, gz, gr, cot, down_w
+    )
+    down_sum = Reduction(order, down_keep, down_send, near_first=True)
+    up_sum = Reduction(order, up_keep, up_send)
+
+    down_sum.move, up_sum.move, gy_own = lax.optimization_barrier((down_sum.move, up_sum.move, gy_own))
     down_sum.next()
-    output, *up_parts = up_grads_call(which, y_mine, resid, order(act_two), hidden, gz, gr, down_w)
-    up_sum = Reduction(order, *up_parts)
-
-    up_sum.move, gy_own = lax.optimization_barrier((up_sum.move, gy_own))
     up_sum.next()
     gy_own = order(gy_own)
     if multi:
@@ -1144,21 +1132,21 @@
     extra = jnp.concatenate([jnp.broadcast_to(gln_two, (fsdp, 2, width)), by_group], axis=1).astype(BF)
     extra = jnp.pad(extra, ((0, 0), (0, 56 - extra.shape[1]), (0, 0)))
     order.mark(extra)
-    down_sum.next()
     gk_own, gqv_mine = lax.optimization_barrier((gk_own, order(gqv_mine)))
     gk_mine = exchange(gk_own)
     *qv_grads, ga = qv_grads_call(which, gqv_mine, act_one, query_w, value_w)
     qv_sum = Reduction(order, *qv_grads)
     order.mark(qv_sum.move)
-    qv_sum.next()
-    up_sum.next()
+    chains = {"q": qv_sum, "u": up_sum, "d": down_sum}
+    for name in "":
+        chains[name].next()
     keep_c, send_c, input_grad = last_call(which, order(gk_mine), act_one, ga, x, gr, norm, extra, key_w)
     key_sum = Reduction(order, keep_c, send_c, direct=True)
     order.mark(send_c)
 
     shard = width // fsdp
-    chains = {"k": key_sum, "q": qv_sum, "u": up_sum, "d": down_sum}
-    for name in "dkuqdkuqdukqduqkq":
+    chains["k"] = key_sum
+    for name in "qdukdquqdukqdukqkqqq":
         chains[name].next()
     key_rows, query_value, up_out, down_grad = (
         chain.result() for chain in (key_sum, qv_sum, up_sum, down_sum)

time: 437 us -> 409 us (0.936)
  starting transfers between devices: 92.5 us -> 81.2 us
  waiting for transfers between devices: 125 us -> 118 us
  Pallas kernels: 144 us -> 139 us
    ppermute x57, waiting for transfers between devices: 103 us -> 96.7 us  [xor_permute(): lax.ppermute(value, axis, [(source, source ^ mask) for source in range(co...]
    ppermute x57, starting transfers between devices: 54.7 us -> 48.3 us  [xor_permute(): lax.ppermute(value, axis, [(source, source ^ mask) for source in range(co...]
    all_to_all x1, waiting for transfers between devices: 6.64 us -> 1.72 us  [scatter_all(): lax.all_to_all(self.move.reshape(count, rows // count, cols), 'dp', 0, 0)]
    all_to_all x5, starting transfers between devices: 28.6 us -> 23.9 us  [exchange(): return lax.all_to_all(value, 'dp', 0, 0, axis_index_groups=groups)]
    pallas_call x2 -> x1, Pallas kernels: 19.2 us -> 15 us  [ffn_grads_call(): pl.pallas_call(ffn_grads_kernel, out_shape=(jax.ShapeDtypeStruct((tokens,...]
    unnamed x95 -> x107, local copies, waits for them, and re-layouts: 8.75 us -> 8.3 us
  transfers between devices with their start and end apart: 64 -> 64, of which waited for: 24 -> 24; matrix products, arithmetic and copies ran while one was open for 13% -> 13% of each run, Pallas kernels for 24% -> 29%
where the time goes in v1:
time: 409 us; the launch traced here: 404 us
  Pallas kernels  139 us (34%)
  waiting for transfers between devices  118 us (29%)
  starting transfers between devices  81.2 us (20%)
  local copies, waits for them, and re-layouts  35.1 us (9%)
  other arithmetic  29.3 us (7%)
    ppermute x57, waiting for transfers between devices, xor_permute(): lax.ppermute(value, axis, [(source, source ^ mask) for source in range(co...  96.7 us
    ppermute x57, starting transfers between devices, xor_permute(): lax.ppermute(value, axis, [(source, source ^ mask) for source in range(co...  48.3 us
    pallas_call x1, Pallas kernels, mix_bwd(): pl.pallas_call(functools.partial(mix_bwd_merged if v_base else mix_bwd_ke...  31.9 us
    all_to_all x5, starting transfers between devices, exchange(): return lax.all_to_all(value, 'dp', 0, 0, axis_index_groups=groups)  23.9 us
    pallas_call x1, Pallas kernels, shift_bwd(): pl.pallas_call(shift_bwd_kernel, out_shape=(jax.ShapeDtypeStruct((SHIFT,...  20.6 us
    pallas_call x1, Pallas kernels, middle_call(): pl.pallas_call(middle_kernel, out_shape=(jax.ShapeDtypeStruct((tokens, wi...  19.8 us
    all_to_all x5, waiting for transfers between devices, exchange(): return lax.all_to_all(value, 'dp', 0, 0, axis_index_groups=groups)  19.1 us
    pallas_call x1, Pallas kernels, ffn_grads_call(): pl.pallas_call(ffn_grads_kernel, out_shape=(jax.ShapeDtypeStruct((tokens,...  15 us
  transfers between devices with their start and end apart: 64, of which 24 were waited for; matrix products, arithmetic and copies ran while one was open for 13% of the time, Pallas kernels for 29%

profile of v1, /device:TPU:0, one launch (start us, length us, event | category | flops | bytes accessed | tf_op | source)
XLA Modules:
  0.0 404.3 jit_solution(2652234167068021401)
XLA Ops:
  2.1 3.0 collective-permute-start.1
  9.0 2.1 concatenate.51
  11.1 3.6 collective-permute-done.4.w2.k2
  15.0 3.6 collective-permute-done.13
  24.2 1.8 collective-permute-start.7
  27.3 4.2 %key_call.1 = (bf16[512,768]{1,0:T(8,128)(2,1)}, bf16[8,192,256]{2,1,0:T(8,128)(2,1)}, f32[2,768]{1,0:T(2,128)}) custom-call(s32[2]{0:T(128)} %pad_add_fusion.1.me_ref, bf16[512,768]{1,0:T(8,128)(2,1)} %bitcast.131, bf16[2,192]{1,0:T(2,128)(2,1)} %copy-done.34, bf16[2,192]{1,0:T(2,128)(2,1)} %copy-done.44, bf16[2,192]{1,0:T(2,128)(2,1)} %copy-done.43, ...), custom_call_target="tpu_custom_call" | custom-call | flops 100000000 | bytes 8192 | tf_op jit(solution)/shard_map/key_call/pallas_call | solution.py:550
  31.5 6.4 %all-to-all-start = ((bf16[8,192,256]{2,1,0:T(8,128)(2,1)}), bf16[8,192,256]{2,1,0:T(8,128)(2,1)S(1)}, u32[]{:S(2)}, u32[]{:S(2)}) async-start(bf16[8,192,256]{2,1,0:T(8,128)(2,1)} %get-tuple-element.99), calls=%async_computation | async-start | bytes 1572864 | tf_op jit(solution)/shard_map/all_to_all | solution.py:1017
  39.0 4.2 %fusion.13 = f32[3,2560]{1,0:T(4,128)S(1)} fusion(f32[3,32]{1,0:T(4,128)S(1)} %mul.141, f32[3,32]{1,0:T(4,128)S(1)} %reshape.369, f32[3,32]{1,0:T(4,128)S(1)} %mul.136, f32[2560]{0:T(1024)S(1)} %convert_select_fusion, f32[3,32]{1,0:T(4,128)S(1)} %neg.27), kind=kLoop, calls=%fused_computation.31 | loop fusion | flops 1712640 | bytes 42496 | tf_op jit(solution)/shard_map/jvp()/reduce_sum | solution.py:992
  46.0 5.7 %query_value_call.1 = (bf16[384,256]{1,0:T(8,128)(2,1)}, bf16[384,256]{1,0:T(8,128)(2,1)}, bf16[384,256]{1,0:T(8,128)(2,1)}, bf16[384,256]{1,0:T(8,128)(2,1)}, b...) custom-call(s32[2]{0:T(128)} %pad_add_fusion.1.me_ref, ...), custom_call_target="tpu_custom_call" | custom-call | flops 100000000 | bytes 8192 | tf_op jit(solution)/shard_map/query_value_call/pallas_call | solution.py:586
  51.7 2.1 collective-permute-start.16
  53.8 1.5 collective-permute-start.17
  56.1 2.8 collective-permute-start.19
  59.6 3.2 collective-permute-start.20
  62.8 6.0 %collective-permute-done.17.refs_2_ = bf16[384,256]{1,0:T(8,128)(2,1)S(1)} collective-permute-done((bf16[384,256]{1,0:T(8,128)(2,1)}, bf16[384,256]{1,0:T(8,128)(2,1)S(1)}, u32[]{:S(2)}, u32[]{:S(2)}) %collective-permute-start.17) | collective-permute-done | bytes 196640 | tf_op jit(solution)/shard_map/ppermute | solution.py:857
  68.8 1.7 collective-permute-start.21
  70.5 2.6 collective-permute-start.22
  74.0 12.5 %shift_fwd.1.k_ref.refs_1_ = bf16[2048,192]{1,0:T(8,128)(2,1)} custom-call(s32[2176]{0:T(1024)} %copy-done.27, bf16[8,192,256]{2,1,0:T(8,128)(2,1)} %copy-done.4, bf16[64,192]{1,0:T(8,128)(2,1)} %broadcast_in_dim.91.halo_ref, f32[2,64,128]{2,1,0:T(8,128)} %pad_maximum_fusion.10.taps_ref, s32[2176,1]{1,0:T(8,128)} %broadcast_in_dim.109.segcol_ref), custom_call_target="tpu_custom_call" | custom-call | flops 10000000000 | bytes 262144 | tf_op jit(solution)/shard_map/shift_fwd/pallas_call | solution.py:185
  88.8 2.7 collect_qv.1.q_ref.v_ref.refs_0_.refs_2_
  91.5 12.7 %mix_fwd.1 = bf16[8,192,256]{2,1,0:T(8,128)(2,1)} custom-call(bf16[8,384,256]{2,1,0:T(8,128)(2,1)} %collect_qv.1.q_ref.v_ref.refs_0_.refs_2_, bf16[2048,192]{1,0:T(8,128)(2,1)} %shift_fwd.1.k_ref.refs_1_, bf16[8,384,256]{2,1,0:T(8,128)(2,1)} %collect_qv.1.q_ref.v_ref.refs_0_.refs_2_, f32[3,1,2560]{2,1,0:T(1,128)} %broadcast_select_fusion.18.row_ref.refs_4_, ...), custom_call_target="tpu_custom_call" | custom-call | flops 20000000000 | bytes 524288 | tf_op jit(solution)/shard_map/mix_fwd/pallas_call | solution.py:356
  104.2 9.1 %collective-permute-done.23.d2 = bf16[768,768]{1,0:T(8,128)(2,1)} collective-permute-done((bf16[768,768]{1,0:T(8,128)(2,1)S(1)}, bf16[768,768]{1,0:T(8,128)(2,1)}, u32[]{:S(2)}, u32[]{:S(2)}) %collective-permute-start.23) | collective-permute-done | bytes 1179680 | tf_op jit(solution)/shard_map/ppermute | solution.py:857
  113.3 3.7 all-to-all-start.1
  118.9 8.6 %collective-permute-done.25.o2 = bf16[192,768]{1,0:T(8,128)(2,1)} collective-permute-done((bf16[192,768]{1,0:T(8,128)(2,1)}, bf16[192,768]{1,0:T(8,128)(2,1)}, u32[]{:S(2)}, u32[]{:S(2)}) %collective-permute-start.25) | collective-permute-done | bytes 294944 | tf_op jit(solution)/shard_map/ppermute | solution.py:857
  127.5 1.9 collective-permute-done.24.o1
  131.3 4.2 %all-to-all-done.1.y_ref = bf16[8,192,256]{2,1,0:T(8,128)(2,1)S(1)} async-done(((bf16[8,192,256]{2,1,0:T(8,128)(2,1)}), bf16[8,192,256]{2,1,0:T(8,128)(2,1)S(1)}, u32[]{:S(2)}, u32[]{:S(2)}) %all-to-all-start.1) | async-done | bytes 786464 | tf_op jit(solution)/shard_map/all_to_all | solution.py:1017
  136.4 19.8 %middle_call.1 = (f32[512,768]{1,0:T(8,128)}, bf16[512,768]{1,0:T(8,128)(2,1)}, bf16[512,3072]{1,0:T(8,128)(2,1)}, bf16[512,3072]{1,0:T(8,128)(2,1)}, f32[512,76...) custom-call(s32[2]{0:T(128)} %pad_add_fusion.1.me_ref, bf16[8,192,256]{2,1,0:T(8,128)(2,1)} %copy-done.7, ...), custom_call_target="tpu_custom_call" | custom-call | flops 15000000512 | bytes 3145728 | tf_op jit(solution)/shard_map/middle_call/pallas_call | solution.py:656
  156.2 3.6 all-to-all-start.2
  159.8 15.0 %ffn_grads_call.1 = (bf16[512,768]{1,0:T(8,128)(2,1)}, bf16[2,768,768]{2,1,0:T(8,128)(2,1)}, bf16[2,768,768]{2,1,0:T(8,128)(2,1)}, bf16[2,960,768]{2,1,0:T(8,128)(2,1)}, bf16[2,960,768]{2,1,0:T(8,128)(2,1)}) custom-call(s32[2]{0:T(128)} %pad_add_fusion.1.me_ref, bf16[8,192,256]{2,1,0:T(8,128)(2,1)} %copy-done.7, f32[512,768]{1,0:T(8,128)} %get-tuple-element.113.resid_ref, ...), custom_call_target="tpu_custom_call" | custom-call | flops 19000000512 | bytes 3145728 | tf_op jit(solution)/shard_map/ffn_grads_call/pallas_call | solution.py:726
  174.7 4.5 %all-to-all-done.2.refs_3_ = bf16[8,192,256]{2,1,0:T(8,128)(2,1)S(1)} async-done(((bf16[8,192,256]{2,1,0:T(8,128)(2,1)}), bf16[8,192,256]{2,1,0:T(8,128)(2,1)S(1)}, u32[]{:S(2)}, u32[]{:S(2)}) %all-to-all-start.2) | async-done | bytes 786464 | tf_op jit(solution)/shard_map/all_to_all | solution.py:1017
  180.8 7.0 %collective-permute-done.31 = bf16[2,768,768]{2,1,0:T(8,128)(2,1)S(1)} collective-permute-done((bf16[2,768,768]{2,1,0:T(8,128)(2,1)}, bf16[2,768,768]{2,1,0:T(8,128)(2,1)S(1)}, u32[]{:S(2)}, u32[]{:S(2)}) %collective-permute-start.31) | collective-permute-done | bytes 2359328 | tf_op jit(solution)/shard_map/ppermute | solution.py:857
  187.8 2.2 add_convert_fusion.1
  192.6 2.6 add_convert_fusion
  197.3 31.9 %mix_bwd.1 = (bf16[8,384,256]{2,1,0:T(8,128)(2,1)}, f32[2048,192]{1,0:T(8,128)}, f32[3,1,2560]{2,1,0:T(1,128)}) custom-call(bf16[8,384,256]{2,1,0:T(8,128)(2,1)} %collect_qv.1.q_ref.v_ref.refs_0_.refs_2_, bf16[2048,192]{1,0:T(8,128)(2,1)} %shift_fwd.1.k_ref.refs_1_, bf16[8,384,256]{2,1,0:T(8,128)(2,1)} %collect_qv.1.q_ref.v_ref.refs_0_.refs_2_, ...), custom_call_target="tpu_custom_call" | custom-call | flops 40000000000 | bytes 1048576 | tf_op jit(solution)/shard_map/mix_bwd/pallas_call | solution.py:456
  229.2 4.7 %all-to-all-start.3 = ((bf16[8,384,256]{2,1,0:T(8,128)(2,1)}), bf16[8,384,256]{2,1,0:T(8,128)(2,1)}, u32[]{:S(2)}, u32[]{:S(2)}) async-start(bf16[8,384,256]{2,1,0:T(8,128)(2,1)} %get-tuple-element.135), calls=%async_computation.3 | async-start | bytes 3145728 | tf_op jit(solution)/shard_map/all_to_all | solution.py:1017
  233.9 1.5 add_convert_fusion.4
  237.7 1.7 add_convert_fusion.2
  239.5 2.0 collective-permute-start.36
  242.2 20.6 %shift_bwd.1 = (f32[64,192]{1,0:T(8,128)}, bf16[8,192,256]{2,1,0:T(8,128)(2,1)}) custom-call(s32[2176]{0:T(1024)} %copy-done.27, bf16[8,192,256]{2,1,0:T(8,128)(2,1)} %copy-done.4, bf16[64,192]{1,0:T(8,128)(2,1)} %broadcast_in_dim.91.halo_ref, f32[2048,192]{1,0:T(8,128)} %get-tuple-element.133.g_ref, f32[64,192]{1,0:T(8,128)} %broadcast_in_dim.97.ghalo_ref, ...), custom_call_target="tpu_custom_call" | custom-call | flops 20000000000 | bytes 524288 | tf_op jit(solution)/shard_map/shift_bwd/pallas_call | solution.py:259
  265.7 3.3 collective-permute-done.36
  269.5 5.2 %fusion.19 = (f32[3,32]{1,0:T(4,128)S(1)}, bf16[3,32]{1,0:T(4,128)(2,1)S(1)}, f32[3,32]{1,0:T(4,128)S(1)}, f32[3,32]{1,0:T(4,128)S(1)}) fusion(f32[3,2560]{1,0:T(4,128)S(1)} %get-tuple-element.268, f32[3,32]{1,0:T(4,128)S(1)} %copy-done.42, f32[3,32]{1,0:T(4,128)S(1)} %copy-done.38, f32[3,32]{1,0:T(4,128)S(1)} %copy-done.40, f32[2560]{0:T(1024)S(1)} %copy-done.31, ...), kind=kLoop, calls=%fused_computation.38 | loop fusion | flops 5652096 | bytes 43840 | tf_op jit(solution)/shard_map/transpose(jvp())/reduce_sum | solution.py:988
  276.0 5.4 %all-to-all-start.4 = ((bf16[8,192,256]{2,1,0:T(8,128)(2,1)}), bf16[8,192,256]{2,1,0:T(8,128)(2,1)S(1)}, u32[]{:S(2)}, u32[]{:S(2)}) async-start(bf16[8,192,256]{2,1,0:T(8,128)(2,1)} %get-tuple-element.142), calls=%async_computation.4 | async-start | bytes 1572864 | tf_op jit(solution)/shard_map/all_to_all | solution.py:1017
  281.5 6.9 %qv_grads_call.1 = (bf16[2,384,768]{2,1,0:T(8,128)(2,1)}, bf16[2,384,768]{2,1,0:T(8,128)(2,1)}, f32[512,768]{1,0:T(8,128)}) custom-call(s32[2]{0:T(128)} %pad_add_fusion.1.me_ref, bf16[8,384,256]{2,1,0:T(8,128)(2,1)} %all-to-all-done.3.gqv_ref, bf16[512,768]{1,0:T(8,128)(2,1)} %get-tuple-element.95.act_ref, bf16[192,768]{1,0:T(8,128)(2,1)} %q0.1, ...), custom_call_target="tpu_custom_call" | custom-call | flops 8000000000 | bytes 1572864 | tf_op jit(solution)/shard_map/qv_grads_call/pallas_call | solution.py:785
  288.4 2.1 collective-permute-start.38
  290.6 10.5 %all-to-all-done.4.gk_ref = bf16[8,192,256]{2,1,0:T(8,128)(2,1)S(1)} async-done(((bf16[8,192,256]{2,1,0:T(8,128)(2,1)}), bf16[8,192,256]{2,1,0:T(8,128)(2,1)S(1)}, u32[]{:S(2)}, u32[]{:S(2)}) %all-to-all-start.4) | async-done | bytes 786464 | tf_op jit(solution)/shard_map/all_to_all | solution.py:1017
  302.0 7.0 %last_call.1 = (bf16[2,256,768]{2,1,0:T(8,128)(2,1)}, bf16[2,256,768]{2,1,0:T(8,128)(2,1)}, bf16[512,768]{1,0:T(8,128)(2,1)}) custom-call(s32[2]{0:T(128)} %pad_add_fusion.1.me_ref, bf16[8,192,256]{2,1,0:T(8,128)(2,1)} %copy-done.6, bf16[512,768]{1,0:T(8,128)(2,1)} %get-tuple-element.95.act_ref, f32[512,768]{1,0:T(8,128)} %get-tuple-element.146.ga_ref, ...), custom_call_target="tpu_custom_call" | custom-call | flops 6000000000 | bytes 1048576 | tf_op jit(solution)/shard_map/last_call/pallas_call | solution.py:834
  309.5 1.4 collective-permute-start.42
  312.3 3.0 collective-permute-start.43
  315.6 10.2 %collective-permute-done.41 = bf16[96,768]{1,0:T(8,128)(2,1)S(1)} collective-permute-done((bf16[96,768]{1,0:T(8,128)(2,1)S(1)}, bf16[96,768]{1,0:T(8,128)(2,1)S(1)}, u32[]{:S(2)}, u32[]{:S(2)}) %collective-permute-start.41) | collective-permute-done | bytes 147488 | tf_op jit(solution)/shard_map/ppermute | solution.py:857
  328.2 8.1 %collective-permute-done.43 = bf16[120,768]{1,0:T(8,128)(2,1)S(1)} collective-permute-done((bf16[120,768]{1,0:T(8,128)(2,1)S(1)}, bf16[120,768]{1,0:T(8,128)(2,1)S(1)}, u32[]{:S(2)}, u32[]{:S(2)}) %collective-permute-start.43) | collective-permute-done | bytes 184352 | tf_op jit(solution)/shard_map/ppermute | solution.py:857
  336.7 3.4 collective-permute-done.45
  340.2 3.8 collective-permute-done.46
  345.0 4.1 %all-to-all-start.5 = ((bf16[8,32,768]{2,1,0:T(8,128)(2,1)}), bf16[8,32,768]{2,1,0:T(8,128)(2,1)S(1)}, u32[]{:S(2)}, u32[]{:S(2)}) async-start(bf16[8,32,768]{2,1,0:T(8,128)(2,1)} %bitcast.47), calls=%async_computation.5 | async-start | bytes 786432 | tf_op jit(solution)/shard_map/all_to_all | solution.py:969
  349.2 3.0 collective-permute-start.51
  352.2 2.0 collective-permute-done.49
  354.8 12.4 %collective-permute-done.50 = bf16[240,768]{1,0:T(8,128)(2,1)S(1)} collective-permute-done((bf16[240,768]{1,0:T(8,128)(2,1)S(1)}, bf16[240,768]{1,0:T(8,128)(2,1)S(1)}, u32[]{:S(2)}, u32[]{:S(2)}) %collective-permute-start.50) | collective-permute-done | bytes 368672 | tf_op jit(solution)/shard_map/ppermute | solution.py:857
  367.3 1.7 all-to-all-done.5
  371.1 4.9 %all-to-all-start.6 = ((bf16[8,32,768]{2,1,0:T(8,128)(2,1)}), bf16[8,32,768]{2,1,0:T(8,128)(2,1)S(1)}, u32[]{:S(2)}, u32[]{:S(2)}) async-start(bf16[8,32,768]{2,1,0:T(8,128)(2,1)} %broadcast_in_dim.108), calls=%async_computation.6 | async-start | bytes 786432 | tf_op jit(solution)/shard_map/all_to_all | solution.py:976
  376.0 2.1 collective-permute-start.53
  378.2 1.6 maximum_convert_fusion
  379.8 7.4 %collective-permute-done.53 = bf16[96,768]{1,0:T(8,128)(2,1)S(1)} collective-permute-done((bf16[96,768]{1,0:T(8,128)(2,1)S(1)}, bf16[96,768]{1,0:T(8,128)(2,1)S(1)}, u32[]{:S(2)}, u32[]{:S(2)}) %collective-permute-start.53) | collective-permute-done | bytes 147488 | tf_op jit(solution)/shard_map/ppermute | solution.py:857
  387.2 1.6 collective-permute-start.54
  388.8 3.0 collective-permute-done.55
  393.1 1.5 copy.48
  394.7 1.8 copy.55
  396.5 1.5 collective-permute-done.54
  (312 shorter events, 56.1 us)
Async XLA Ops:
  2.1 19.9 %collective-permute-start.1 = (bf16[2,192]{1,0:T(2,128)(2,1)S(1)}, bf16[2,192]{1,0:T(2,128)(2,1)S(1)}, u32[]{:S(2)}, u32[]{:S(2)}) collective-permute-start(bf16[2,192]{1,0:T(2,128)(2,1)S(1)} %pad_maximum_fusion.11.n0), channel_id=1, source_target_pairs={{0,16},{8,24},{16,0},{24,8},{1,17},{9,25},{17,1},{25,9},{2,18},{10... | collective-permute-start | bytes 2312 | tf_op jit(solution)/shard_map/ppermute | solution.py:857
  5.1 19.1 %collective-permute-start = (bf16[2,192]{1,0:T(2,128)(2,1)S(1)}, bf16[2,192]{1,0:T(2,128)(2,1)S(1)}, u32[]{:S(2)}, u32[]{:S(2)}) collective-permute-start(bf16[2,192]{1,0:T(2,128)(2,1)S(1)} %pad_maximum_fusion.11.n0), channel_id=1, source_target_pairs={{0,8},{8,0},{16,24},{24,16},{1,9},{9,1},{17,25},{25,17},{2,10},{10... | collective-permute-start | bytes 2312 | tf_op jit(solution)/shard_map/ppermute | solution.py:857
  5.1 9.6 %collective-permute-start.4 = (bf16[192,768]{1,0:T(8,128)(2,1)}, bf16[192,768]{1,0:T(8,128)(2,1)S(1)}, u32[]{:S(2)}, u32[]{:S(2)}) collective-permute-start(bf16[192,768]{1,0:T(8,128)(2,1)} %k0.1), channel_id=1, source_target_pairs={{0,16},{8,24},{16,0},{24,8},{1,17},{9,25},{17,1},{25,9},{2,18},{10... | collective-permute-start | bytes 884744 | tf_op jit(solution)/shard_map/ppermute | solution.py:857
  5.3 21.0 %collective-permute-start.3 = (bf16[192,768]{1,0:T(8,128)(2,1)}, bf16[192,768]{1,0:T(8,128)(2,1)S(1)}, u32[]{:S(2)}, u32[]{:S(2)}) collective-permute-start(bf16[192,768]{1,0:T(8,128)(2,1)} %k0.1), channel_id=1, source_target_pairs={{0,8},{8,0},{16,24},{24,16},{1,9},{9,1},{17,25},{25,17},{2,10},{10... | collective-permute-start | bytes 884744 | tf_op jit(solution)/shard_map/ppermute | solution.py:857
  14.7 3.8 collective-permute-start.13
  15.0 7.5 %collective-permute-start.12 = (bf16[104,128]{1,0:T(8,128)(2,1)S(1)}, bf16[104,128]{1,0:T(8,128)(2,1)S(1)}, u32[]{:S(2)}, u32[]{:S(2)}) collective-permute-start(bf16[104,128]{1,0:T(8,128)(2,1)S(1)} %pad_bitcast_fusion), channel_id=1, source_target_pairs={{0,8},{8,0},{16,24},{24,16},{1,9},{9,1},{17,25},{25,17},{2,10},{10... | collective-permute-start | bytes 79880 | tf_op jit(solution)/shard_map/ppermute | solution.py:857
  18.6 4.4 %collective-permute-start.14 = (bf16[104,128]{1,0:T(8,128)(2,1)S(1)}, bf16[104,128]{1,0:T(8,128)(2,1)S(1)}, u32[]{:S(2)}, u32[]{:S(2)}) collective-permute-start(bf16[104,128]{1,0:T(8,128)(2,1)S(1)} %collective-permute-done.13), channel_id=1, source_target_pairs={{0,8},{8,0},{16,24},{24,16},{1,9},{9,1},{17,25},{25,17},{2,10},{10... | collective-permute-start | bytes 79880 | tf_op jit(solution)/shard_map/ppermute | solution.py:857
  22.0 4.1 %collective-permute-start.2 = (bf16[2,192]{1,0:T(2,128)(2,1)S(1)}, bf16[2,192]{1,0:T(2,128)(2,1)S(1)}, u32[]{:S(2)}, u32[]{:S(2)}) collective-permute-start(bf16[2,192]{1,0:T(2,128)(2,1)S(1)} %collective-permute-done.1.n2), channel_id=1, source_target_pairs={{0,8},{8,0},{16,24},{24,16},{1,9},{9,1},{17,25},{25,17},{2,10},{10... | collective-permute-start | bytes 2312 | tf_op jit(solution)/shard_map/ppermute | solution.py:857
  22.6 15.8 %collective-permute-start.10 = (bf16[192,768]{1,0:T(8,128)(2,1)S(1)}, bf16[192,768]{1,0:T(8,128)(2,1)S(1)}, u32[]{:S(2)}, u32[]{:S(2)}) collective-permute-start(bf16[192,768]{1,0:T(8,128)(2,1)S(1)} %copy-done.10), channel_id=1, source_target_pairs={{0,16},{8,24},{16,0},{24,8},{1,17},{9,25},{17,1},{25,9},{2,18},{10... | collective-permute-start | bytes 884744 | tf_op jit(solution)/shard_map/ppermute | solution.py:857
  23.0 3.6 collective-permute-start.5
  24.2 19.1 %collective-permute-start.7 = (bf16[192,768]{1,0:T(8,128)(2,1)S(1)}, bf16[192,768]{1,0:T(8,128)(2,1)S(1)}, u32[]{:S(2)}, u32[]{:S(2)}) collective-permute-start(bf16[192,768]{1,0:T(8,128)(2,1)S(1)} %copy-done.9), channel_id=1, source_target_pairs={{0,16},{8,24},{16,0},{24,8},{1,17},{9,25},{17,1},{25,9},{2,18},{10... | collective-permute-start | bytes 884744 | tf_op jit(solution)/shard_map/ppermute | solution.py:857
  26.1 18.7 %collective-permute-start.6 = (bf16[192,768]{1,0:T(8,128)(2,1)S(1)}, bf16[192,768]{1,0:T(8,128)(2,1)S(1)}, u32[]{:S(2)}, u32[]{:S(2)}) collective-permute-start(bf16[192,768]{1,0:T(8,128)(2,1)S(1)} %copy-done.9), channel_id=1, source_target_pairs={{0,8},{8,0},{16,24},{24,16},{1,9},{9,1},{17,25},{25,17},{2,10},{10... | collective-permute-start | bytes 884744 | tf_op jit(solution)/shard_map/ppermute | solution.py:857
  26.3 18.5 %collective-permute-start.9 = (bf16[192,768]{1,0:T(8,128)(2,1)S(1)}, bf16[192,768]{1,0:T(8,128)(2,1)S(1)}, u32[]{:S(2)}, u32[]{:S(2)}) collective-permute-start(bf16[192,768]{1,0:T(8,128)(2,1)S(1)} %copy-done.10), channel_id=1, source_target_pairs={{0,8},{8,0},{16,24},{24,16},{1,9},{9,1},{17,25},{25,17},{2,10},{10... | collective-permute-start | bytes 884744 | tf_op jit(solution)/shard_map/ppermute | solution.py:857
  31.5 41.6 %all-to-all-start = ((bf16[8,192,256]{2,1,0:T(8,128)(2,1)}), bf16[8,192,256]{2,1,0:T(8,128)(2,1)S(1)}, u32[]{:S(2)}, u32[]{:S(2)}) async-start(bf16[8,192,256]{2,1,0:T(8,128)(2,1)} %get-tuple-element.99), calls=%async_computation | async-start | bytes 1572864 | tf_op jit(solution)/shard_map/all_to_all | solution.py:1017
  38.4 32.1 %collective-permute-start.15 = (bf16[192,3072]{1,0:T(8,128)(2,1)}, bf16[192,3072]{1,0:T(8,128)(2,1)}, u32[]{:S(2)}, u32[]{:S(2)}) collective-permute-start(bf16[192,3072]{1,0:T(8,128)(2,1)} %u0), channel_id=1, source_target_pairs={{0,16},{8,24},{16,0},{24,8},{1,17},{9,25},{17,1},{25,9},{2,18},{10... | collective-permute-start | bytes 3538952 | tf_op jit(solution)/shard_map/ppermute | solution.py:857
  43.2 1.6 collective-permute-start.11
  43.3 2.0 collective-permute-start.8
  51.7 7.9 %collective-permute-start.16 = (bf16[384,256]{1,0:T(8,128)(2,1)}, bf16[384,256]{1,0:T(8,128)(2,1)S(1)}, u32[]{:S(2)}, u32[]{:S(2)}) collective-permute-start(bf16[384,256]{1,0:T(8,128)(2,1)} %get-tuple-element.103), channel_id=1, source_target_pairs={{0,1},{1,0},{2,3},{3,2},{4,5},{5,4},{6,7},{7,6},{8,9},{9,8},{10,11... | collective-permute-start | bytes 589832 | tf_op jit(solution)/shard_map/ppermute | solution.py:857
  53.8 15.0 %collective-permute-start.17 = (bf16[384,256]{1,0:T(8,128)(2,1)}, bf16[384,256]{1,0:T(8,128)(2,1)S(1)}, u32[]{:S(2)}, u32[]{:S(2)}) collective-permute-start(bf16[384,256]{1,0:T(8,128)(2,1)} %get-tuple-element.104), channel_id=1, source_target_pairs={{0,2},{1,3},{2,0},{3,1},{4,6},{5,7},{6,4},{7,5},{8,10},{9,11},{10,... | collective-permute-start | bytes 589832 | tf_op jit(solution)/shard_map/ppermute | solution.py:857
  56.0 30.4 %collective-permute-start.18 = (bf16[384,256]{1,0:T(8,128)(2,1)}, bf16[384,256]{1,0:T(8,128)(2,1)S(1)}, u32[]{:S(2)}, u32[]{:S(2)}) collective-permute-start(bf16[384,256]{1,0:T(8,128)(2,1)} %get-tuple-element.105), channel_id=1, source_target_pairs={{0,3},{1,2},{2,1},{3,0},{4,7},{5,6},{6,5},{7,4},{8,11},{9,10},{10,... | collective-permute-start | bytes 589832 | tf_op jit(solution)/shard_map/ppermute | solution.py:857
  56.1 31.2 %collective-permute-start.19 = (bf16[384,256]{1,0:T(8,128)(2,1)}, bf16[384,256]{1,0:T(8,128)(2,1)S(1)}, u32[]{:S(2)}, u32[]{:S(2)}) collective-permute-start(bf16[384,256]{1,0:T(8,128)(2,1)} %get-tuple-element.106), channel_id=1, source_target_pairs={{0,4},{1,5},{2,6},{3,7},{4,0},{5,1},{6,2},{7,3},{8,12},{9,13},{10,... | collective-permute-start | bytes 589832 | tf_op jit(solution)/shard_map/ppermute | solution.py:857
  59.6 27.7 %collective-permute-start.20 = (bf16[384,256]{1,0:T(8,128)(2,1)}, bf16[384,256]{1,0:T(8,128)(2,1)S(1)}, u32[]{:S(2)}, u32[]{:S(2)}) collective-permute-start(bf16[384,256]{1,0:T(8,128)(2,1)} %get-tuple-element.107), channel_id=1, source_target_pairs={{0,5},{1,4},{2,7},{3,6},{4,1},{5,0},{6,3},{7,2},{8,13},{9,12},{10,... | collective-permute-start | bytes 589832 | tf_op jit(solution)/shard_map/ppermute | solution.py:857
  68.8 18.5 %collective-permute-start.21 = (bf16[384,256]{1,0:T(8,128)(2,1)}, bf16[384,256]{1,0:T(8,128)(2,1)S(1)}, u32[]{:S(2)}, u32[]{:S(2)}) collective-permute-start(bf16[384,256]{1,0:T(8,128)(2,1)} %get-tuple-element.108), channel_id=1, source_target_pairs={{0,6},{1,7},{2,4},{3,5},{4,2},{5,3},{6,0},{7,1},{8,14},{9,15},{10,... | collective-permute-start | bytes 589832 | tf_op jit(solution)/shard_map/ppermute | solution.py:857
  70.5 16.8 %collective-permute-start.22 = (bf16[384,256]{1,0:T(8,128)(2,1)}, bf16[384,256]{1,0:T(8,128)(2,1)S(1)}, u32[]{:S(2)}, u32[]{:S(2)}) collective-permute-start(bf16[384,256]{1,0:T(8,128)(2,1)} %get-tuple-element.109), channel_id=1, source_target_pairs={{0,7},{1,6},{2,5},{3,4},{4,3},{5,2},{6,1},{7,0},{8,15},{9,14},{10,... | collective-permute-start | bytes 589832 | tf_op jit(solution)/shard_map/ppermute | solution.py:857
  86.5 26.8 %collective-permute-start.23 = (bf16[768,768]{1,0:T(8,128)(2,1)S(1)}, bf16[768,768]{1,0:T(8,128)(2,1)}, u32[]{:S(2)}, u32[]{:S(2)}) collective-permute-start(bf16[768,768]{1,0:T(8,128)(2,1)S(1)} %copy-done.48), channel_id=1, source_target_pairs={{0,16},{8,24},{16,0},{24,8},{1,17},{9,25},{17,1},{25,9},{2,18},{10... | collective-permute-start | bytes 3538952 | tf_op jit(solution)/shard_map/ppermute | solution.py:857
  113.3 22.2 %all-to-all-start.1 = ((bf16[8,192,256]{2,1,0:T(8,128)(2,1)}), bf16[8,192,256]{2,1,0:T(8,128)(2,1)S(1)}, u32[]{:S(2)}, u32[]{:S(2)}) async-start(bf16[8,192,256]{2,1,0:T(8,128)(2,1)} %mix_fwd.1), calls=%async_computation.1 | async-start | bytes 1572864 | tf_op jit(solution)/shard_map/all_to_all | solution.py:1017
  117.1 14.3 %collective-permute-start.29 = (bf16[768,768]{1,0:T(8,128)(2,1)S(1)}, bf16[768,768]{1,0:T(8,128)(2,1)}, u32[]{:S(2)}, u32[]{:S(2)}) collective-permute-start(bf16[768,768]{1,0:T(8,128)(2,1)S(1)} %copy-done.49), channel_id=1, source_target_pairs={{0,8},{8,0},{16,24},{24,16},{1,9},{9,1},{17,25},{25,17},{2,10},{10... | collective-permute-start | bytes 3538952 | tf_op jit(solution)/shard_map/ppermute | solution.py:857
  117.1 14.2 %collective-permute-start.27 = (bf16[192,3072]{1,0:T(8,128)(2,1)S(1)}, bf16[192,3072]{1,0:T(8,128)(2,1)}, u32[]{:S(2)}, u32[]{:S(2)}) collective-permute-start(bf16[192,3072]{1,0:T(8,128)(2,1)S(1)} %copy-done.47), channel_id=1, source_target_pairs={{0,8},{8,0},{16,24},{24,16},{1,9},{9,1},{17,25},{25,17},{2,10},{10... | collective-permute-start | bytes 3538952 | tf_op jit(solution)/shard_map/ppermute | solution.py:857
  117.6 13.7 %collective-permute-start.30 = (bf16[768,768]{1,0:T(8,128)(2,1)}, bf16[768,768]{1,0:T(8,128)(2,1)}, u32[]{:S(2)}, u32[]{:S(2)}) collective-permute-start(bf16[768,768]{1,0:T(8,128)(2,1)} %collective-permute-done.23.d2), channel_id=1, source_target_pairs={{0,8},{8,0},{16,24},{24,16},{1,9},{9,1},{17,25},{25,17},{2,10},{10... | collective-permute-start | bytes 3538952 | tf_op jit(solution)/shard_map/ppermute | solution.py:857
  117.7 13.6 %collective-permute-start.28 = (bf16[192,3072]{1,0:T(8,128)(2,1)}, bf16[192,3072]{1,0:T(8,128)(2,1)}, u32[]{:S(2)}, u32[]{:S(2)}) collective-permute-start(bf16[192,3072]{1,0:T(8,128)(2,1)} %collective-permute-done.15.u2), channel_id=1, source_target_pairs={{0,8},{8,0},{16,24},{24,16},{1,9},{9,1},{17,25},{25,17},{2,10},{10... | collective-permute-start | bytes 3538952 | tf_op jit(solution)/shard_map/ppermute | solution.py:857
  118.1 9.3 %collective-permute-start.25 = (bf16[192,768]{1,0:T(8,128)(2,1)}, bf16[192,768]{1,0:T(8,128)(2,1)}, u32[]{:S(2)}, u32[]{:S(2)}) collective-permute-start(bf16[192,768]{1,0:T(8,128)(2,1)} %o0), channel_id=1, source_target_pairs={{0,16},{8,24},{16,0},{24,8},{1,17},{9,25},{17,1},{25,9},{2,18},{10... | collective-permute-start | bytes 884744 | tf_op jit(solution)/shard_map/ppermute | solution.py:857
  127.5 1.9 collective-permute-start.24
  129.4 1.9 collective-permute-start.26
  156.2 23.0 %all-to-all-start.2 = ((bf16[8,192,256]{2,1,0:T(8,128)(2,1)}), bf16[8,192,256]{2,1,0:T(8,128)(2,1)S(1)}, u32[]{:S(2)}, u32[]{:S(2)}) async-start(bf16[8,192,256]{2,1,0:T(8,128)(2,1)} %get-tuple-element.121), calls=%async_computation.2 | async-start | bytes 1572864 | tf_op jit(solution)/shard_map/all_to_all | solution.py:1017
  179.2 13.4 %collective-permute-start.32 = (bf16[2,960,768]{2,1,0:T(8,128)(2,1)}, bf16[2,960,768]{2,1,0:T(8,128)(2,1)}, u32[]{:S(2)}, u32[]{:S(2)}) collective-permute-start(bf16[2,960,768]{2,1,0:T(8,128)(2,1)} %get-tuple-element.127), channel_id=1, source_target_pairs={{0,8},{8,0},{16,24},{24,16},{1,9},{9,1},{17,25},{25,17},{2,10},{10... | collective-permute-start | bytes 8847368 | tf_op jit(solution)/shard_map/ppermute | solution.py:857
  179.2 8.6 %collective-permute-start.31 = (bf16[2,768,768]{2,1,0:T(8,128)(2,1)}, bf16[2,768,768]{2,1,0:T(8,128)(2,1)S(1)}, u32[]{:S(2)}, u32[]{:S(2)}) collective-permute-start(bf16[2,768,768]{2,1,0:T(8,128)(2,1)} %get-tuple-element.125), channel_id=1, source_target_pairs={{0,8},{8,0},{16,24},{24,16},{1,9},{9,1},{17,25},{25,17},{2,10},{10... | collective-permute-start | bytes 7077896 | tf_op jit(solution)/shard_map/ppermute | solution.py:857
  191.2 42.7 %collective-permute-start.33 = (bf16[2,384,768]{2,1,0:T(8,128)(2,1)}, bf16[2,384,768]{2,1,0:T(8,128)(2,1)}, u32[]{:S(2)}, u32[]{:S(2)}) collective-permute-start(bf16[2,384,768]{2,1,0:T(8,128)(2,1)} %get-tuple-element.216), channel_id=1, source_target_pairs={{0,1},{1,0},{2,3},{3,2},{4,5},{5,4},{6,7},{7,6},{8,9},{9,8},{10,11... | collective-permute-start | bytes 3538952 | tf_op jit(solution)/shard_map/ppermute | solution.py:857
  196.5 41.1 %collective-permute-start.34 = (bf16[960,768]{1,0:T(8,128)(2,1)}, bf16[960,768]{1,0:T(8,128)(2,1)}, u32[]{:S(2)}, u32[]{:S(2)}) collective-permute-start(bf16[960,768]{1,0:T(8,128)(2,1)} %get-tuple-element.214), channel_id=1, source_target_pairs={{0,16},{8,24},{16,0},{24,8},{1,17},{9,25},{17,1},{25,9},{2,18},{10... | collective-permute-start | bytes 4423688 | tf_op jit(solution)/shard_map/ppermute | solution.py:857
  229.2 46.8 %all-to-all-start.3 = ((bf16[8,384,256]{2,1,0:T(8,128)(2,1)}), bf16[8,384,256]{2,1,0:T(8,128)(2,1)}, u32[]{:S(2)}, u32[]{:S(2)}) async-start(bf16[8,384,256]{2,1,0:T(8,128)(2,1)} %get-tuple-element.135), calls=%async_computation.3 | async-start | bytes 3145728 | tf_op jit(solution)/shard_map/all_to_all | solution.py:1017
  236.4 27.3 %collective-permute-start.35 = (bf16[384,768]{1,0:T(8,128)(2,1)}, bf16[384,768]{1,0:T(8,128)(2,1)}, u32[]{:S(2)}, u32[]{:S(2)}) collective-permute-start(bf16[384,768]{1,0:T(8,128)(2,1)} %get-tuple-element.228), channel_id=1, source_target_pairs={{0,16},{8,24},{16,0},{24,8},{1,17},{9,25},{17,1},{25,9},{2,18},{10... | collective-permute-start | bytes 1769480 | tf_op jit(solution)/shard_map/ppermute | solution.py:857
  239.5 29.5 %collective-permute-start.36 = (bf16[480,768]{1,0:T(8,128)(2,1)S(1)}, bf16[480,768]{1,0:T(8,128)(2,1)S(1)}, u32[]{:S(2)}, u32[]{:S(2)}) collective-permute-start(bf16[480,768]{1,0:T(8,128)(2,1)S(1)} %get-tuple-element.220), channel_id=1, source_target_pairs={{0,1},{1,0},{2,3},{3,2},{4,5},{5,4},{6,7},{7,6},{8,9},{9,8},{10,11... | collective-permute-start | bytes 2211848 | tf_op jit(solution)/shard_map/ppermute | solution.py:857
  276.0 25.1 %all-to-all-start.4 = ((bf16[8,192,256]{2,1,0:T(8,128)(2,1)}), bf16[8,192,256]{2,1,0:T(8,128)(2,1)S(1)}, u32[]{:S(2)}, u32[]{:S(2)}) async-start(bf16[8,192,256]{2,1,0:T(8,128)(2,1)} %get-tuple-element.142), calls=%async_computation.4 | async-start | bytes 1572864 | tf_op jit(solution)/shard_map/all_to_all | solution.py:1017
  288.3 20.8 %collective-permute-start.37 = (bf16[2,384,768]{2,1,0:T(8,128)(2,1)}, bf16[2,384,768]{2,1,0:T(8,128)(2,1)S(1)}, u32[]{:S(2)}, u32[]{:S(2)}) collective-permute-start(bf16[2,384,768]{2,1,0:T(8,128)(2,1)} %get-tuple-element.144), channel_id=1, source_target_pairs={{0,8},{8,0},{16,24},{24,16},{1,9},{9,1},{17,25},{25,17},{2,10},{10... | collective-permute-start | bytes 3538952 | tf_op jit(solution)/shard_map/ppermute | solution.py:857
  288.4 22.5 %collective-permute-start.38 = (bf16[192,768]{1,0:T(8,128)(2,1)}, bf16[192,768]{1,0:T(8,128)(2,1)}, u32[]{:S(2)}, u32[]{:S(2)}) collective-permute-start(bf16[192,768]{1,0:T(8,128)(2,1)} %get-tuple-element.246), channel_id=1, source_target_pairs={{0,2},{1,3},{2,0},{3,1},{4,6},{5,7},{6,4},{7,5},{8,10},{9,11},{10,... | collective-permute-start | bytes 884744 | tf_op jit(solution)/shard_map/ppermute | solution.py:857
  290.6 21.6 %collective-permute-start.39 = (bf16[240,768]{1,0:T(8,128)(2,1)S(1)}, bf16[240,768]{1,0:T(8,128)(2,1)S(1)}, u32[]{:S(2)}, u32[]{:S(2)}) collective-permute-start(bf16[240,768]{1,0:T(8,128)(2,1)S(1)} %get-tuple-element.236), channel_id=1, source_target_pairs={{0,2},{1,3},{2,0},{3,1},{4,6},{5,7},{6,4},{7,5},{8,10},{9,11},{10,... | collective-permute-start | bytes 1105928 | tf_op jit(solution)/shard_map/ppermute | solution.py:857
  309.0 6.3 %collective-permute-start.40 = (bf16[2,256,768]{2,1,0:T(8,128)(2,1)}, bf16[2,256,768]{2,1,0:T(8,128)(2,1)S(1)}, u32[]{:S(2)}, u32[]{:S(2)}) collective-permute-start(bf16[2,256,768]{2,1,0:T(8,128)(2,1)} %get-tuple-element.151), channel_id=1, source_target_pairs={{0,8},{8,0},{16,24},{24,16},{1,9},{9,1},{17,25},{25,17},{2,10},{10... | collective-permute-start | bytes 2359304 | tf_op jit(solution)/shard_map/ppermute | solution.py:857
  309.5 16.3 %collective-permute-start.42 = (bf16[384,768]{1,0:T(8,128)(2,1)S(1)}, bf16[384,768]{1,0:T(8,128)(2,1)S(1)}, u32[]{:S(2)}, u32[]{:S(2)}) collective-permute-start(bf16[384,768]{1,0:T(8,128)(2,1)S(1)} %get-tuple-element.226), channel_id=1, source_target_pairs={{0,16},{8,24},{16,0},{24,8},{1,17},{9,25},{17,1},{25,9},{2,18},{10... | collective-permute-start | bytes 1769480 | tf_op jit(solution)/shard_map/ppermute | solution.py:857
  312.1 13.7 %collective-permute-start.41 = (bf16[96,768]{1,0:T(8,128)(2,1)S(1)}, bf16[96,768]{1,0:T(8,128)(2,1)S(1)}, u32[]{:S(2)}, u32[]{:S(2)}) collective-permute-start(bf16[96,768]{1,0:T(8,128)(2,1)S(1)} %get-tuple-element.258), channel_id=1, source_target_pairs={{0,4},{1,5},{2,6},{3,7},{4,0},{5,1},{6,2},{7,3},{8,12},{9,13},{10,... | collective-permute-start | bytes 442376 | tf_op jit(solution)/shard_map/ppermute | solution.py:857
  312.3 24.0 %collective-permute-start.43 = (bf16[120,768]{1,0:T(8,128)(2,1)S(1)}, bf16[120,768]{1,0:T(8,128)(2,1)S(1)}, u32[]{:S(2)}, u32[]{:S(2)}) collective-permute-start(bf16[120,768]{1,0:T(8,128)(2,1)S(1)} %get-tuple-element.250), channel_id=1, source_target_pairs={{0,4},{1,5},{2,6},{3,7},{4,0},{5,1},{6,2},{7,3},{8,12},{9,13},{10,... | collective-permute-start | bytes 552968 | tf_op jit(solution)/shard_map/ppermute | solution.py:857
  326.1 10.4 %collective-permute-start.44 = (bf16[192,768]{1,0:T(8,128)(2,1)S(1)}, bf16[192,768]{1,0:T(8,128)(2,1)S(1)}, u32[]{:S(2)}, u32[]{:S(2)}) collective-permute-start(bf16[192,768]{1,0:T(8,128)(2,1)S(1)} %get-tuple-element.244), channel_id=1, source_target_pairs={{0,1},{1,0},{2,3},{3,2},{4,5},{5,4},{6,7},{7,6},{8,9},{9,8},{10,11... | collective-permute-start | bytes 884744 | tf_op jit(solution)/shard_map/ppermute | solution.py:857
  326.9 13.1 %collective-permute-start.45 = (bf16[96,768]{1,0:T(8,128)(2,1)S(1)}, bf16[96,768]{1,0:T(8,128)(2,1)S(1)}, u32[]{:S(2)}, u32[]{:S(2)}) collective-permute-start(bf16[96,768]{1,0:T(8,128)(2,1)S(1)} %add_convert_fusion.15), channel_id=1, source_target_pairs={{0,4},{1,5},{2,6},{3,7},{4,0},{5,1},{6,2},{7,3},{8,12},{9,13},{10,... | collective-permute-start | bytes 442376 | tf_op jit(solution)/shard_map/ppermute | solution.py:857
  326.9 17.3 %collective-permute-start.47 = (bf16[256,768]{1,0:T(8,128)(2,1)S(1)}, bf16[256,768]{1,0:T(8,128)(2,1)S(1)}, u32[]{:S(2)}, u32[]{:S(2)}) collective-permute-start(bf16[256,768]{1,0:T(8,128)(2,1)S(1)} %get-tuple-element.232), channel_id=1, source_target_pairs={{0,16},{8,24},{16,0},{24,8},{1,17},{9,25},{17,1},{25,9},{2,18},{10... | collective-permute-start | bytes 1179656 | tf_op jit(solution)/shard_map/ppermute | solution.py:857
  336.4 7.6 %collective-permute-start.46 = (bf16[120,768]{1,0:T(8,128)(2,1)S(1)}, bf16[120,768]{1,0:T(8,128)(2,1)S(1)}, u32[]{:S(2)}, u32[]{:S(2)}) collective-permute-start(bf16[120,768]{1,0:T(8,128)(2,1)S(1)} %add_convert_fusion.13), channel_id=1, source_target_pairs={{0,4},{1,5},{2,6},{3,7},{4,0},{5,1},{6,2},{7,3},{8,12},{9,13},{10,... | collective-permute-start | bytes 552968 | tf_op jit(solution)/shard_map/ppermute | solution.py:857
  336.6 12.6 %collective-permute-start.48 = (bf16[96,768]{1,0:T(8,128)(2,1)S(1)}, bf16[96,768]{1,0:T(8,128)(2,1)S(1)}, u32[]{:S(2)}, u32[]{:S(2)}) collective-permute-start(bf16[96,768]{1,0:T(8,128)(2,1)S(1)} %get-tuple-element.254), channel_id=1, source_target_pairs={{0,2},{1,3},{2,0},{3,1},{4,6},{5,7},{6,4},{7,5},{8,10},{9,11},{10,... | collective-permute-start | bytes 442376 | tf_op jit(solution)/shard_map/ppermute | solution.py:857
  340.1 14.1 %collective-permute-start.49 = (bf16[192,768]{1,0:T(8,128)(2,1)S(1)}, bf16[192,768]{1,0:T(8,128)(2,1)S(1)}, u32[]{:S(2)}, u32[]{:S(2)}) collective-permute-start(bf16[192,768]{1,0:T(8,128)(2,1)S(1)} %pad_maximum_fusion.5), channel_id=1, source_target_pairs={{0,2},{1,3},{2,0},{3,1},{4,6},{5,7},{6,4},{7,5},{8,10},{9,11},{10,... | collective-permute-start | bytes 884744 | tf_op jit(solution)/shard_map/ppermute | solution.py:857
  344.1 23.1 %collective-permute-start.50 = (bf16[240,768]{1,0:T(8,128)(2,1)S(1)}, bf16[240,768]{1,0:T(8,128)(2,1)S(1)}, u32[]{:S(2)}, u32[]{:S(2)}) collective-permute-start(bf16[240,768]{1,0:T(8,128)(2,1)S(1)} %pad_maximum_fusion.4), channel_id=1, source_target_pairs={{0,2},{1,3},{2,0},{3,1},{4,6},{5,7},{6,4},{7,5},{8,10},{9,11},{10,... | collective-permute-start | bytes 1105928 | tf_op jit(solution)/shard_map/ppermute | solution.py:857
  345.0 24.0 %all-to-all-start.5 = ((bf16[8,32,768]{2,1,0:T(8,128)(2,1)}), bf16[8,32,768]{2,1,0:T(8,128)(2,1)S(1)}, u32[]{:S(2)}, u32[]{:S(2)}) async-start(bf16[8,32,768]{2,1,0:T(8,128)(2,1)} %bitcast.47), calls=%async_computation.5 | async-start | bytes 786432 | tf_op jit(solution)/shard_map/all_to_all | solution.py:969
  349.2 19.9 %collective-permute-start.51 = (bf16[48,768]{1,0:T(8,128)(2,1)S(1)}, bf16[48,768]{1,0:T(8,128)(2,1)S(1)}, u32[]{:S(2)}, u32[]{:S(2)}) collective-permute-start(bf16[48,768]{1,0:T(8,128)(2,1)S(1)} %get-tuple-element.262), channel_id=1, source_target_pairs={{0,4},{1,5},{2,6},{3,7},{4,0},{5,1},{6,2},{7,3},{8,12},{9,13},{10,... | collective-permute-start | bytes 221192 | tf_op jit(solution)/shard_map/ppermute | solution.py:857
  354.3 23.8 %collective-permute-start.56 = (bf16[384,768]{1,0:T(8,128)(2,1)S(1)}, bf16[384,768]{1,0:T(8,128)(2,1)S(1)}, u32[]{:S(2)}, u32[]{:S(2)}) collective-permute-start(bf16[384,768]{1,0:T(8,128)(2,1)S(1)} %pad_maximum_fusion.2), channel_id=1, source_target_pairs={{0,1},{1,0},{2,3},{3,2},{4,5},{5,4},{6,7},{7,6},{8,9},{9,8},{10,11... | collective-permute-start | bytes 1769480 | tf_op jit(solution)/shard_map/ppermute | solution.py:857
  369.1 6.9 %collective-permute-start.52 = (bf16[48,768]{1,0:T(8,128)(2,1)S(1)}, bf16[48,768]{1,0:T(8,128)(2,1)S(1)}, u32[]{:S(2)}, u32[]{:S(2)}) collective-permute-start(bf16[48,768]{1,0:T(8,128)(2,1)S(1)} %add_convert_fusion.16), channel_id=1, source_target_pairs={{0,4},{1,5},{2,6},{3,7},{4,0},{5,1},{6,2},{7,3},{8,12},{9,13},{10,... | collective-permute-start | bytes 221192 | tf_op jit(solution)/shard_map/ppermute | solution.py:857
  369.2 22.6 %collective-permute-start.55 = (bf16[480,768]{1,0:T(8,128)(2,1)S(1)}, bf16[480,768]{1,0:T(8,128)(2,1)S(1)}, u32[]{:S(2)}, u32[]{:S(2)}) collective-permute-start(bf16[480,768]{1,0:T(8,128)(2,1)S(1)} %pad_maximum_fusion.1), channel_id=1, source_target_pairs={{0,1},{1,0},{2,3},{3,2},{4,5},{5,4},{6,7},{7,6},{8,9},{9,8},{10,11... | collective-permute-start | bytes 2211848 | tf_op jit(solution)/shard_map/ppermute | solution.py:857
  371.1 28.2 %all-to-all-start.6 = ((bf16[8,32,768]{2,1,0:T(8,128)(2,1)}), bf16[8,32,768]{2,1,0:T(8,128)(2,1)S(1)}, u32[]{:S(2)}, u32[]{:S(2)}) async-start(bf16[8,32,768]{2,1,0:T(8,128)(2,1)} %broadcast_in_dim.108), calls=%async_computation.6 | async-start | bytes 786432 | tf_op jit(solution)/shard_map/all_to_all | solution.py:976
  376.0 11.1 %collective-permute-start.53 = (bf16[96,768]{1,0:T(8,128)(2,1)S(1)}, bf16[96,768]{1,0:T(8,128)(2,1)S(1)}, u32[]{:S(2)}, u32[]{:S(2)}) collective-permute-start(bf16[96,768]{1,0:T(8,128)(2,1)S(1)} %pad_maximum_fusion.7), channel_id=1, source_target_pairs={{0,2},{1,3},{2,0},{3,1},{4,6},{5,7},{6,4},{7,5},{8,10},{9,11},{10,... | collective-permute-start | bytes 442376 | tf_op jit(solution)/shard_map/ppermute | solution.py:857
  387.2 10.8 %collective-permute-start.54 = (bf16[192,768]{1,0:T(8,128)(2,1)S(1)}, bf16[192,768]{1,0:T(8,128)(2,1)S(1)}, u32[]{:S(2)}, u32[]{:S(2)}) collective-permute-start(bf16[192,768]{1,0:T(8,128)(2,1)S(1)} %pad_maximum_fusion.6), channel_id=1, source_target_pairs={{0,1},{1,0},{2,3},{3,2},{4,5},{5,4},{6,7},{7,6},{8,9},{9,8},{10,11... | collective-permute-start | bytes 884744 | tf_op jit(solution)/shard_map/ppermute | solution.py:857
  (50 other events, 333.6 us)

commit v2 on v1

--- a/solution.py
+++ b/solution.py
@@ -1121,7 +1121,6 @@
     taps_grad, gk_own = shift_bwd(seg_full, k_own, k_halo, gks_own, gks_halo, taps_tiles)
     order.mark(taps_grad)
     down_sum.next()
-    up_sum.next()
     rate_grad, freq_grad, coef_grad, skip_grad = kern_pull(order(gkern)[:, 0, :])
 
     ssm_line = jnp.concatenate([grad.reshape(-1) for grad in (rate_grad, freq_grad, coef_grad, skip_grad)])
@@ -1138,15 +1137,13 @@
     qv_sum = Reduction(order, *qv_grads)
     order.mark(qv_sum.move)
     chains = {"q": qv_sum, "u": up_sum, "d": down_sum}
-    for name in "":
-        chains[name].next()
     keep_c, send_c, input_grad = last_call(which, order(gk_mine), act_one, ga, x, gr, norm, extra, key_w)
     key_sum = Reduction(order, keep_c, send_c, direct=True)
     order.mark(send_c)
 
     shard = width // fsdp
     chains["k"] = key_sum
-    for name in "qdukdquqdukqdukqkqqq":
+    for name in "uqdukdquqdukqdukqkqqq":
         chains[name].next()
     key_rows, query_value, up_out, down_grad = (
         chain.result() for chain in (key_sum, qv_sum, up_sum, down_sum)

time: 409 us -> 407 us (level)
    ppermute x57, waiting for transfers between devices: 96.7 us -> 90.9 us  [xor_permute(): lax.ppermute(value, axis, [(source, source ^ mask) for source in range(co...]
    ppermute x57, starting transfers between devices: 48.3 us -> 52.5 us  [xor_permute(): lax.ppermute(value, axis, [(source, source ^ mask) for source in range(co...]
    unnamed x107 -> x109, local copies, waits for them, and re-layouts: 8.3 us -> 8.35 us
  transfers between devices with their start and end apart: 64 -> 64, of which waited for: 24 -> 25; matrix products, arithmetic and copies ran while one was open for 13% -> 13% of each run, Pallas kernels for 29% -> 30%
where the time goes in v2:
time: 407 us; the launch traced here: 403 us
  Pallas kernels  139 us (34%)
  waiting for transfers between devices  115 us (28%)
  starting transfers between devices  84.2 us (21%)
  local copies, waits for them, and re-layouts  35.3 us (9%)
  other arithmetic  27.3 us (7%)
    ppermute x57, waiting for transfers between devices, xor_permute(): lax.ppermute(value, axis, [(source, source ^ mask) for source in range(co...  90.9 us
    ppermute x57, starting transfers between devices, xor_permute(): lax.ppermute(value, axis, [(source, source ^ mask) for source in range(co...  52.5 us
    pallas_call x1, Pallas kernels, mix_bwd(): pl.pallas_call(functools.partial(mix_bwd_merged if v_base else mix_bwd_ke...  31.9 us
    all_to_all x5, starting transfers between devices, exchange(): return lax.all_to_all(value, 'dp', 0, 0, axis_index_groups=groups)  22.3 us
    all_to_all x5, waiting for transfers between devices, exchange(): return lax.all_to_all(value, 'dp', 0, 0, axis_index_groups=groups)  22 us
    pallas_call x1, Pallas kernels, shift_bwd(): pl.pallas_call(shift_bwd_kernel, out_shape=(jax.ShapeDtypeStruct((SHIFT,...  20.6 us
    pallas_call x1, Pallas kernels, middle_call(): pl.pallas_call(middle_kernel, out_shape=(jax.ShapeDtypeStruct((tokens, wi...  19.8 us
    pallas_call x1, Pallas kernels, ffn_grads_call(): pl.pallas_call(ffn_grads_kernel, out_shape=(jax.ShapeDtypeStruct((tokens,...  15 us
  transfers between devices with their start and end apart: 64, of which 25 were waited for; matrix products, arithmetic and copies ran while one was open for 13% of the time, Pallas kernels for 30%

profile of v2, /device:TPU:0, one launch (start us, length us, event | category | flops | bytes accessed | tf_op | source)
XLA Modules:
  0.0 402.8 jit_solution(13633284885736094863)
XLA Ops:
  2.1 3.0 collective-permute-start.1
  9.0 2.1 concatenate.51
  11.1 3.6 collective-permute-done.4.w2.k2
  15.0 3.6 collective-permute-done.13
  24.3 1.8 collective-permute-start.7
  27.4 4.2 %key_call.1 = (bf16[512,768]{1,0:T(8,128)(2,1)}, bf16[8,192,256]{2,1,0:T(8,128)(2,1)}, f32[2,768]{1,0:T(2,128)}) custom-call(s32[2]{0:T(128)} %pad_add_fusion.1.me_ref, bf16[512,768]{1,0:T(8,128)(2,1)} %bitcast.131, bf16[2,192]{1,0:T(2,128)(2,1)} %copy-done.33, bf16[2,192]{1,0:T(2,128)(2,1)} %copy-done.43, bf16[2,192]{1,0:T(2,128)(2,1)} %copy-done.42, ...), custom_call_target="tpu_custom_call" | custom-call | flops 100000000 | bytes 8192 | tf_op jit(solution)/shard_map/key_call/pallas_call | solution.py:550
  31.6 6.4 %all-to-all-start = ((bf16[8,192,256]{2,1,0:T(8,128)(2,1)}), bf16[8,192,256]{2,1,0:T(8,128)(2,1)S(1)}, u32[]{:S(2)}, u32[]{:S(2)}) async-start(bf16[8,192,256]{2,1,0:T(8,128)(2,1)} %get-tuple-element.99), calls=%async_computation | async-start | bytes 1572864 | tf_op jit(solution)/shard_map/all_to_all | solution.py:1017
  39.1 4.2 %fusion.13 = f32[3,2560]{1,0:T(4,128)S(1)} fusion(f32[3,32]{1,0:T(4,128)S(1)} %mul.141, f32[3,32]{1,0:T(4,128)S(1)} %reshape.369, f32[3,32]{1,0:T(4,128)S(1)} %mul.136, f32[2560]{0:T(1024)S(1)} %convert_select_fusion, f32[3,32]{1,0:T(4,128)S(1)} %neg.27), kind=kLoop, calls=%fused_computation.31 | loop fusion | flops 1712640 | bytes 42496 | tf_op jit(solution)/shard_map/jvp()/reduce_sum | solution.py:992
  46.1 5.7 %query_value_call.1 = (bf16[384,256]{1,0:T(8,128)(2,1)}, bf16[384,256]{1,0:T(8,128)(2,1)}, bf16[384,256]{1,0:T(8,128)(2,1)}, bf16[384,256]{1,0:T(8,128)(2,1)}, b...) custom-call(s32[2]{0:T(128)} %pad_add_fusion.1.me_ref, ...), custom_call_target="tpu_custom_call" | custom-call | flops 100000000 | bytes 8192 | tf_op jit(solution)/shard_map/query_value_call/pallas_call | solution.py:586
  51.8 2.1 collective-permute-start.16
  56.2 2.8 collective-permute-start.19
  59.7 3.2 collective-permute-start.20
  62.9 6.0 %collective-permute-done.17.refs_2_ = bf16[384,256]{1,0:T(8,128)(2,1)S(1)} collective-permute-done((bf16[384,256]{1,0:T(8,128)(2,1)}, bf16[384,256]{1,0:T(8,128)(2,1)S(1)}, u32[]{:S(2)}, u32[]{:S(2)}) %collective-permute-start.17) | collective-permute-done | bytes 196640 | tf_op jit(solution)/shard_map/ppermute | solution.py:857
  68.9 1.7 collective-permute-start.21
  70.6 2.6 collective-permute-start.22
  74.1 12.5 %shift_fwd.1.k_ref.refs_1_ = bf16[2048,192]{1,0:T(8,128)(2,1)} custom-call(s32[2176]{0:T(1024)} %copy-done.27, bf16[8,192,256]{2,1,0:T(8,128)(2,1)} %copy-done.4, bf16[64,192]{1,0:T(8,128)(2,1)} %broadcast_in_dim.91.halo_ref, f32[2,64,128]{2,1,0:T(8,128)} %pad_maximum_fusion.10.taps_ref, s32[2176,1]{1,0:T(8,128)} %broadcast_in_dim.109.segcol_ref), custom_call_target="tpu_custom_call" | custom-call | flops 10000000000 | bytes 262144 | tf_op jit(solution)/shard_map/shift_fwd/pallas_call | solution.py:185
  88.9 2.7 collect_qv.1.q_ref.v_ref.refs_0_.refs_2_
  91.6 12.6 %mix_fwd.1 = bf16[8,192,256]{2,1,0:T(8,128)(2,1)} custom-call(bf16[8,384,256]{2,1,0:T(8,128)(2,1)} %collect_qv.1.q_ref.v_ref.refs_0_.refs_2_, bf16[2048,192]{1,0:T(8,128)(2,1)} %shift_fwd.1.k_ref.refs_1_, bf16[8,384,256]{2,1,0:T(8,128)(2,1)} %collect_qv.1.q_ref.v_ref.refs_0_.refs_2_, f32[3,1,2560]{2,1,0:T(1,128)} %broadcast_select_fusion.18.row_ref.refs_4_, ...), custom_call_target="tpu_custom_call" | custom-call | flops 20000000000 | bytes 524288 | tf_op jit(solution)/shard_map/mix_fwd/pallas_call | solution.py:356
  104.2 8.9 %collective-permute-done.23.d2 = bf16[768,768]{1,0:T(8,128)(2,1)} collective-permute-done((bf16[768,768]{1,0:T(8,128)(2,1)S(1)}, bf16[768,768]{1,0:T(8,128)(2,1)}, u32[]{:S(2)}, u32[]{:S(2)}) %collective-permute-start.23) | collective-permute-done | bytes 1179680 | tf_op jit(solution)/shard_map/ppermute | solution.py:857
  113.1 3.7 all-to-all-start.1
  119.1 7.8 %collective-permute-done.25.o2 = bf16[192,768]{1,0:T(8,128)(2,1)S(1)} collective-permute-done((bf16[192,768]{1,0:T(8,128)(2,1)S(1)}, bf16[192,768]{1,0:T(8,128)(2,1)S(1)}, u32[]{:S(2)}, u32[]{:S(2)}) %collective-permute-start.25) | collective-permute-done | bytes 294944 | tf_op jit(solution)/shard_map/ppermute | solution.py:857
  127.0 1.6 collective-permute-done.24.o1
  130.2 4.9 %all-to-all-done.1.y_ref = bf16[8,192,256]{2,1,0:T(8,128)(2,1)S(1)} async-done(((bf16[8,192,256]{2,1,0:T(8,128)(2,1)}), bf16[8,192,256]{2,1,0:T(8,128)(2,1)S(1)}, u32[]{:S(2)}, u32[]{:S(2)}) %all-to-all-start.1) | async-done | bytes 786464 | tf_op jit(solution)/shard_map/all_to_all | solution.py:1017
  135.9 19.8 %middle_call.1 = (f32[512,768]{1,0:T(8,128)}, bf16[512,768]{1,0:T(8,128)(2,1)}, bf16[512,3072]{1,0:T(8,128)(2,1)}, bf16[512,3072]{1,0:T(8,128)(2,1)}, f32[512,76...) custom-call(s32[2]{0:T(128)} %pad_add_fusion.1.me_ref, bf16[8,192,256]{2,1,0:T(8,128)(2,1)} %copy-done.7, ...), custom_call_target="tpu_custom_call" | custom-call | flops 15000000512 | bytes 3145728 | tf_op jit(solution)/shard_map/middle_call/pallas_call | solution.py:656
  155.8 3.6 all-to-all-start.2
  159.3 15.0 %ffn_grads_call.1 = (bf16[512,768]{1,0:T(8,128)(2,1)}, bf16[2,768,768]{2,1,0:T(8,128)(2,1)}, bf16[2,768,768]{2,1,0:T(8,128)(2,1)}, bf16[2,960,768]{2,1,0:T(8,128)(2,1)}, bf16[2,960,768]{2,1,0:T(8,128)(2,1)}) custom-call(s32[2]{0:T(128)} %pad_add_fusion.1.me_ref, bf16[8,192,256]{2,1,0:T(8,128)(2,1)} %copy-done.7, f32[512,768]{1,0:T(8,128)} %get-tuple-element.113.resid_ref, ...), custom_call_target="tpu_custom_call" | custom-call | flops 19000000512 | bytes 3145728 | tf_op jit(solution)/shard_map/ffn_grads_call/pallas_call | solution.py:726
  174.3 4.2 %all-to-all-done.2.refs_3_ = bf16[8,192,256]{2,1,0:T(8,128)(2,1)S(1)} async-done(((bf16[8,192,256]{2,1,0:T(8,128)(2,1)}), bf16[8,192,256]{2,1,0:T(8,128)(2,1)S(1)}, u32[]{:S(2)}, u32[]{:S(2)}) %all-to-all-start.2) | async-done | bytes 786464 | tf_op jit(solution)/shard_map/all_to_all | solution.py:1017
  179.1 8.1 %collective-permute-done.31 = bf16[2,768,768]{2,1,0:T(8,128)(2,1)S(1)} collective-permute-done((bf16[2,768,768]{2,1,0:T(8,128)(2,1)}, bf16[2,768,768]{2,1,0:T(8,128)(2,1)S(1)}, u32[]{:S(2)}, u32[]{:S(2)}) %collective-permute-start.31) | collective-permute-done | bytes 2359328 | tf_op jit(solution)/shard_map/ppermute | solution.py:857
  187.1 2.2 add_convert_fusion.1
  191.9 2.6 add_convert_fusion
  195.8 2.0 collective-permute-start.34
  197.9 31.9 %mix_bwd.1 = (bf16[8,384,256]{2,1,0:T(8,128)(2,1)}, f32[2048,192]{1,0:T(8,128)}, f32[3,1,2560]{2,1,0:T(1,128)}) custom-call(bf16[8,384,256]{2,1,0:T(8,128)(2,1)} %collect_qv.1.q_ref.v_ref.refs_0_.refs_2_, bf16[2048,192]{1,0:T(8,128)(2,1)} %shift_fwd.1.k_ref.refs_1_, bf16[8,384,256]{2,1,0:T(8,128)(2,1)} %collect_qv.1.q_ref.v_ref.refs_0_.refs_2_, ...), custom_call_target="tpu_custom_call" | custom-call | flops 40000000000 | bytes 1048576 | tf_op jit(solution)/shard_map/mix_bwd/pallas_call | solution.py:456
  229.8 4.7 %all-to-all-start.3 = ((bf16[8,384,256]{2,1,0:T(8,128)(2,1)}), bf16[8,384,256]{2,1,0:T(8,128)(2,1)}, u32[]{:S(2)}, u32[]{:S(2)}) async-start(bf16[8,384,256]{2,1,0:T(8,128)(2,1)} %get-tuple-element.135), calls=%async_computation.3 | async-start | bytes 3145728 | tf_op jit(solution)/shard_map/all_to_all | solution.py:1017
  234.5 1.5 add_convert_fusion.4
  236.3 1.7 add_convert_fusion.2
  239.6 20.6 %shift_bwd.1 = (f32[64,192]{1,0:T(8,128)}, bf16[8,192,256]{2,1,0:T(8,128)(2,1)}) custom-call(s32[2176]{0:T(1024)} %copy-done.27, bf16[8,192,256]{2,1,0:T(8,128)(2,1)} %copy-done.4, bf16[64,192]{1,0:T(8,128)(2,1)} %broadcast_in_dim.91.halo_ref, f32[2048,192]{1,0:T(8,128)} %get-tuple-element.133.g_ref, f32[64,192]{1,0:T(8,128)} %broadcast_in_dim.97.ghalo_ref, ...), custom_call_target="tpu_custom_call" | custom-call | flops 20000000000 | bytes 524288 | tf_op jit(solution)/shard_map/shift_bwd/pallas_call | solution.py:259
  262.4 5.2 %fusion.19 = (f32[3,32]{1,0:T(4,128)S(1)}, bf16[3,32]{1,0:T(4,128)(2,1)S(1)}, f32[3,32]{1,0:T(4,128)S(1)}, f32[3,32]{1,0:T(4,128)S(1)}) fusion(f32[3,2560]{1,0:T(4,128)S(1)} %get-tuple-element.268, f32[3,32]{1,0:T(4,128)S(1)} %copy-done.41, f32[3,32]{1,0:T(4,128)S(1)} %copy-done.37, f32[3,32]{1,0:T(4,128)S(1)} %copy-done.39, f32[2560]{0:T(1024)S(1)} %copy-done.31, ...), kind=kLoop, calls=%fused_computation.38 | loop fusion | flops 5652096 | bytes 43840 | tf_op jit(solution)/shard_map/transpose(jvp())/reduce_sum | solution.py:988
  268.8 2.9 all-to-all-done.3.gqv_ref
  271.8 3.8 all-to-all-start.4
  275.6 6.9 %qv_grads_call.1 = (bf16[2,384,768]{2,1,0:T(8,128)(2,1)}, bf16[2,384,768]{2,1,0:T(8,128)(2,1)}, f32[512,768]{1,0:T(8,128)}) custom-call(s32[2]{0:T(128)} %pad_add_fusion.1.me_ref, bf16[8,384,256]{2,1,0:T(8,128)(2,1)} %all-to-all-done.3.gqv_ref, bf16[512,768]{1,0:T(8,128)(2,1)} %get-tuple-element.95.act_ref, bf16[192,768]{1,0:T(8,128)(2,1)} %q0.1, ...), custom_call_target="tpu_custom_call" | custom-call | flops 8000000000 | bytes 1572864 | tf_op jit(solution)/shard_map/qv_grads_call/pallas_call | solution.py:785
  282.6 2.1 collective-permute-start.36
  286.1 9.9 %all-to-all-done.4.gk_ref = bf16[8,192,256]{2,1,0:T(8,128)(2,1)S(1)} async-done(((bf16[8,192,256]{2,1,0:T(8,128)(2,1)}), bf16[8,192,256]{2,1,0:T(8,128)(2,1)S(1)}, u32[]{:S(2)}, u32[]{:S(2)}) %all-to-all-start.4) | async-done | bytes 786464 | tf_op jit(solution)/shard_map/all_to_all | solution.py:1017
  297.0 6.9 %last_call.1 = (bf16[2,256,768]{2,1,0:T(8,128)(2,1)}, bf16[2,256,768]{2,1,0:T(8,128)(2,1)}, bf16[512,768]{1,0:T(8,128)(2,1)}) custom-call(s32[2]{0:T(128)} %pad_add_fusion.1.me_ref, bf16[8,192,256]{2,1,0:T(8,128)(2,1)} %copy-done.6, bf16[512,768]{1,0:T(8,128)(2,1)} %get-tuple-element.95.act_ref, f32[512,768]{1,0:T(8,128)} %get-tuple-element.145.ga_ref, ...), custom_call_target="tpu_custom_call" | custom-call | flops 6000000000 | bytes 1048576 | tf_op jit(solution)/shard_map/last_call/pallas_call | solution.py:834
  305.8 2.8 collective-permute-start.39
  310.9 9.6 %collective-permute-done.39 = bf16[240,768]{1,0:T(8,128)(2,1)S(1)} collective-permute-done((bf16[240,768]{1,0:T(8,128)(2,1)S(1)}, bf16[240,768]{1,0:T(8,128)(2,1)S(1)}, u32[]{:S(2)}, u32[]{:S(2)}) %collective-permute-start.39) | collective-permute-done | bytes 368672 | tf_op jit(solution)/shard_map/ppermute | solution.py:857
  321.3 2.7 collective-permute-done.42
  324.3 2.1 collective-permute-start.45
  327.1 6.8 %collective-permute-done.43 = bf16[120,768]{1,0:T(8,128)(2,1)S(1)} collective-permute-done((bf16[120,768]{1,0:T(8,128)(2,1)S(1)}, bf16[120,768]{1,0:T(8,128)(2,1)S(1)}, u32[]{:S(2)}, u32[]{:S(2)}) %collective-permute-start.43) | collective-permute-done | bytes 184352 | tf_op jit(solution)/shard_map/ppermute | solution.py:857
  334.2 2.6 collective-permute-start.48
  336.8 3.5 collective-permute-done.45
  340.5 4.5 %collective-permute-done.46 = bf16[120,768]{1,0:T(8,128)(2,1)S(1)} collective-permute-done((bf16[120,768]{1,0:T(8,128)(2,1)S(1)}, bf16[120,768]{1,0:T(8,128)(2,1)S(1)}, u32[]{:S(2)}, u32[]{:S(2)}) %collective-permute-start.46) | collective-permute-done | bytes 184352 | tf_op jit(solution)/shard_map/ppermute | solution.py:857
  346.0 4.1 %all-to-all-start.5 = ((bf16[8,32,768]{2,1,0:T(8,128)(2,1)}), bf16[8,32,768]{2,1,0:T(8,128)(2,1)S(1)}, u32[]{:S(2)}, u32[]{:S(2)}) async-start(bf16[8,32,768]{2,1,0:T(8,128)(2,1)} %bitcast.47), calls=%async_computation.5 | async-start | bytes 786432 | tf_op jit(solution)/shard_map/all_to_all | solution.py:969
  350.2 3.0 collective-permute-start.51
  353.2 1.5 collective-permute-start.56
  354.8 10.4 %collective-permute-done.50 = bf16[240,768]{1,0:T(8,128)(2,1)S(1)} collective-permute-done((bf16[240,768]{1,0:T(8,128)(2,1)S(1)}, bf16[240,768]{1,0:T(8,128)(2,1)S(1)}, u32[]{:S(2)}, u32[]{:S(2)}) %collective-permute-start.50) | collective-permute-done | bytes 368672 | tf_op jit(solution)/shard_map/ppermute | solution.py:857
  365.3 2.1 all-to-all-done.5
  369.0 5.3 %all-to-all-start.6 = ((bf16[8,32,768]{2,1,0:T(8,128)(2,1)}), bf16[8,32,768]{2,1,0:T(8,128)(2,1)S(1)}, u32[]{:S(2)}, u32[]{:S(2)}) async-start(bf16[8,32,768]{2,1,0:T(8,128)(2,1)} %broadcast_in_dim.108), calls=%async_computation.6 | async-start | bytes 786432 | tf_op jit(solution)/shard_map/all_to_all | solution.py:976
  374.4 2.1 collective-permute-start.53
  376.5 1.6 maximum_convert_fusion
  378.1 7.5 %collective-permute-done.53 = bf16[96,768]{1,0:T(8,128)(2,1)S(1)} collective-permute-done((bf16[96,768]{1,0:T(8,128)(2,1)S(1)}, bf16[96,768]{1,0:T(8,128)(2,1)S(1)}, u32[]{:S(2)}, u32[]{:S(2)}) %collective-permute-start.53) | collective-permute-done | bytes 147488 | tf_op jit(solution)/shard_map/ppermute | solution.py:857
  385.7 1.6 collective-permute-start.54
  387.2 3.0 collective-permute-done.55
  393.1 1.8 copy.55
  394.9 1.6 collective-permute-done.54
  (314 shorter events, 56.8 us)
Async XLA Ops:
  2.1 20.0 %collective-permute-start.1 = (bf16[2,192]{1,0:T(2,128)(2,1)S(1)}, bf16[2,192]{1,0:T(2,128)(2,1)S(1)}, u32[]{:S(2)}, u32[]{:S(2)}) collective-permute-start(bf16[2,192]{1,0:T(2,128)(2,1)S(1)} %pad_maximum_fusion.11.n0), channel_id=1, source_target_pairs={{0,16},{8,24},{16,0},{24,8},{1,17},{9,25},{17,1},{25,9},{2,18},{10... | collective-permute-start | bytes 2312 | tf_op jit(solution)/shard_map/ppermute | solution.py:857
  5.1 19.2 %collective-permute-start = (bf16[2,192]{1,0:T(2,128)(2,1)S(1)}, bf16[2,192]{1,0:T(2,128)(2,1)S(1)}, u32[]{:S(2)}, u32[]{:S(2)}) collective-permute-start(bf16[2,192]{1,0:T(2,128)(2,1)S(1)} %pad_maximum_fusion.11.n0), channel_id=1, source_target_pairs={{0,8},{8,0},{16,24},{24,16},{1,9},{9,1},{17,25},{25,17},{2,10},{10... | collective-permute-start | bytes 2312 | tf_op jit(solution)/shard_map/ppermute | solution.py:857
  5.1 9.6 %collective-permute-start.4 = (bf16[192,768]{1,0:T(8,128)(2,1)}, bf16[192,768]{1,0:T(8,128)(2,1)S(1)}, u32[]{:S(2)}, u32[]{:S(2)}) collective-permute-start(bf16[192,768]{1,0:T(8,128)(2,1)} %k0.1), channel_id=1, source_target_pairs={{0,16},{8,24},{16,0},{24,8},{1,17},{9,25},{17,1},{25,9},{2,18},{10... | collective-permute-start | bytes 884744 | tf_op jit(solution)/shard_map/ppermute | solution.py:857
  5.3 21.1 %collective-permute-start.3 = (bf16[192,768]{1,0:T(8,128)(2,1)}, bf16[192,768]{1,0:T(8,128)(2,1)S(1)}, u32[]{:S(2)}, u32[]{:S(2)}) collective-permute-start(bf16[192,768]{1,0:T(8,128)(2,1)} %k0.1), channel_id=1, source_target_pairs={{0,8},{8,0},{16,24},{24,16},{1,9},{9,1},{17,25},{25,17},{2,10},{10... | collective-permute-start | bytes 884744 | tf_op jit(solution)/shard_map/ppermute | solution.py:857
  14.7 3.8 collective-permute-start.13
  15.0 7.6 %collective-permute-start.12 = (bf16[104,128]{1,0:T(8,128)(2,1)S(1)}, bf16[104,128]{1,0:T(8,128)(2,1)S(1)}, u32[]{:S(2)}, u32[]{:S(2)}) collective-permute-start(bf16[104,128]{1,0:T(8,128)(2,1)S(1)} %pad_bitcast_fusion), channel_id=1, source_target_pairs={{0,8},{8,0},{16,24},{24,16},{1,9},{9,1},{17,25},{25,17},{2,10},{10... | collective-permute-start | bytes 79880 | tf_op jit(solution)/shard_map/ppermute | solution.py:857
  18.6 4.5 %collective-permute-start.14 = (bf16[104,128]{1,0:T(8,128)(2,1)S(1)}, bf16[104,128]{1,0:T(8,128)(2,1)S(1)}, u32[]{:S(2)}, u32[]{:S(2)}) collective-permute-start(bf16[104,128]{1,0:T(8,128)(2,1)S(1)} %collective-permute-done.13), channel_id=1, source_target_pairs={{0,8},{8,0},{16,24},{24,16},{1,9},{9,1},{17,25},{25,17},{2,10},{10... | collective-permute-start | bytes 79880 | tf_op jit(solution)/shard_map/ppermute | solution.py:857
  22.0 4.1 %collective-permute-start.2 = (bf16[2,192]{1,0:T(2,128)(2,1)S(1)}, bf16[2,192]{1,0:T(2,128)(2,1)S(1)}, u32[]{:S(2)}, u32[]{:S(2)}) collective-permute-start(bf16[2,192]{1,0:T(2,128)(2,1)S(1)} %collective-permute-done.1.n2), channel_id=1, source_target_pairs={{0,8},{8,0},{16,24},{24,16},{1,9},{9,1},{17,25},{25,17},{2,10},{10... | collective-permute-start | bytes 2312 | tf_op jit(solution)/shard_map/ppermute | solution.py:857
  22.7 15.8 %collective-permute-start.10 = (bf16[192,768]{1,0:T(8,128)(2,1)S(1)}, bf16[192,768]{1,0:T(8,128)(2,1)S(1)}, u32[]{:S(2)}, u32[]{:S(2)}) collective-permute-start(bf16[192,768]{1,0:T(8,128)(2,1)S(1)} %copy-done.10), channel_id=1, source_target_pairs={{0,16},{8,24},{16,0},{24,8},{1,17},{9,25},{17,1},{25,9},{2,18},{10... | collective-permute-start | bytes 884744 | tf_op jit(solution)/shard_map/ppermute | solution.py:857
  23.1 3.6 collective-permute-start.5
  24.3 19.0 %collective-permute-start.7 = (bf16[192,768]{1,0:T(8,128)(2,1)S(1)}, bf16[192,768]{1,0:T(8,128)(2,1)S(1)}, u32[]{:S(2)}, u32[]{:S(2)}) collective-permute-start(bf16[192,768]{1,0:T(8,128)(2,1)S(1)} %copy-done.9), channel_id=1, source_target_pairs={{0,16},{8,24},{16,0},{24,8},{1,17},{9,25},{17,1},{25,9},{2,18},{10... | collective-permute-start | bytes 884744 | tf_op jit(solution)/shard_map/ppermute | solution.py:857
  26.1 18.7 %collective-permute-start.6 = (bf16[192,768]{1,0:T(8,128)(2,1)S(1)}, bf16[192,768]{1,0:T(8,128)(2,1)S(1)}, u32[]{:S(2)}, u32[]{:S(2)}) collective-permute-start(bf16[192,768]{1,0:T(8,128)(2,1)S(1)} %copy-done.9), channel_id=1, source_target_pairs={{0,8},{8,0},{16,24},{24,16},{1,9},{9,1},{17,25},{25,17},{2,10},{10... | collective-permute-start | bytes 884744 | tf_op jit(solution)/shard_map/ppermute | solution.py:857
  26.4 18.5 %collective-permute-start.9 = (bf16[192,768]{1,0:T(8,128)(2,1)S(1)}, bf16[192,768]{1,0:T(8,128)(2,1)S(1)}, u32[]{:S(2)}, u32[]{:S(2)}) collective-permute-start(bf16[192,768]{1,0:T(8,128)(2,1)S(1)} %copy-done.10), channel_id=1, source_target_pairs={{0,8},{8,0},{16,24},{24,16},{1,9},{9,1},{17,25},{25,17},{2,10},{10... | collective-permute-start | bytes 884744 | tf_op jit(solution)/shard_map/ppermute | solution.py:857
  31.6 41.6 %all-to-all-start = ((bf16[8,192,256]{2,1,0:T(8,128)(2,1)}), bf16[8,192,256]{2,1,0:T(8,128)(2,1)S(1)}, u32[]{:S(2)}, u32[]{:S(2)}) async-start(bf16[8,192,256]{2,1,0:T(8,128)(2,1)} %get-tuple-element.99), calls=%async_computation | async-start | bytes 1572864 | tf_op jit(solution)/shard_map/all_to_all | solution.py:1017
  38.5 32.1 %collective-permute-start.15 = (bf16[192,3072]{1,0:T(8,128)(2,1)}, bf16[192,3072]{1,0:T(8,128)(2,1)}, u32[]{:S(2)}, u32[]{:S(2)}) collective-permute-start(bf16[192,3072]{1,0:T(8,128)(2,1)} %u0), channel_id=1, source_target_pairs={{0,16},{8,24},{16,0},{24,8},{1,17},{9,25},{17,1},{25,9},{2,18},{10... | collective-permute-start | bytes 3538952 | tf_op jit(solution)/shard_map/ppermute | solution.py:857
  43.3 1.6 collective-permute-start.11
  43.4 2.0 collective-permute-start.8
  51.8 7.9 %collective-permute-start.16 = (bf16[384,256]{1,0:T(8,128)(2,1)}, bf16[384,256]{1,0:T(8,128)(2,1)S(1)}, u32[]{:S(2)}, u32[]{:S(2)}) collective-permute-start(bf16[384,256]{1,0:T(8,128)(2,1)} %get-tuple-element.103), channel_id=1, source_target_pairs={{0,1},{1,0},{2,3},{3,2},{4,5},{5,4},{6,7},{7,6},{8,9},{9,8},{10,11... | collective-permute-start | bytes 589832 | tf_op jit(solution)/shard_map/ppermute | solution.py:857
  53.9 15.0 %collective-permute-start.17 = (bf16[384,256]{1,0:T(8,128)(2,1)}, bf16[384,256]{1,0:T(8,128)(2,1)S(1)}, u32[]{:S(2)}, u32[]{:S(2)}) collective-permute-start(bf16[384,256]{1,0:T(8,128)(2,1)} %get-tuple-element.104), channel_id=1, source_target_pairs={{0,2},{1,3},{2,0},{3,1},{4,6},{5,7},{6,4},{7,5},{8,10},{9,11},{10,... | collective-permute-start | bytes 589832 | tf_op jit(solution)/shard_map/ppermute | solution.py:857
  56.1 30.5 %collective-permute-start.18 = (bf16[384,256]{1,0:T(8,128)(2,1)}, bf16[384,256]{1,0:T(8,128)(2,1)S(1)}, u32[]{:S(2)}, u32[]{:S(2)}) collective-permute-start(bf16[384,256]{1,0:T(8,128)(2,1)} %get-tuple-element.105), channel_id=1, source_target_pairs={{0,3},{1,2},{2,1},{3,0},{4,7},{5,6},{6,5},{7,4},{8,11},{9,10},{10,... | collective-permute-start | bytes 589832 | tf_op jit(solution)/shard_map/ppermute | solution.py:857
  56.2 31.2 %collective-permute-start.19 = (bf16[384,256]{1,0:T(8,128)(2,1)}, bf16[384,256]{1,0:T(8,128)(2,1)S(1)}, u32[]{:S(2)}, u32[]{:S(2)}) collective-permute-start(bf16[384,256]{1,0:T(8,128)(2,1)} %get-tuple-element.106), channel_id=1, source_target_pairs={{0,4},{1,5},{2,6},{3,7},{4,0},{5,1},{6,2},{7,3},{8,12},{9,13},{10,... | collective-permute-start | bytes 589832 | tf_op jit(solution)/shard_map/ppermute | solution.py:857
  59.7 27.7 %collective-permute-start.20 = (bf16[384,256]{1,0:T(8,128)(2,1)}, bf16[384,256]{1,0:T(8,128)(2,1)S(1)}, u32[]{:S(2)}, u32[]{:S(2)}) collective-permute-start(bf16[384,256]{1,0:T(8,128)(2,1)} %get-tuple-element.107), channel_id=1, source_target_pairs={{0,5},{1,4},{2,7},{3,6},{4,1},{5,0},{6,3},{7,2},{8,13},{9,12},{10,... | collective-permute-start | bytes 589832 | tf_op jit(solution)/shard_map/ppermute | solution.py:857
  68.9 18.5 %collective-permute-start.21 = (bf16[384,256]{1,0:T(8,128)(2,1)}, bf16[384,256]{1,0:T(8,128)(2,1)S(1)}, u32[]{:S(2)}, u32[]{:S(2)}) collective-permute-start(bf16[384,256]{1,0:T(8,128)(2,1)} %get-tuple-element.108), channel_id=1, source_target_pairs={{0,6},{1,7},{2,4},{3,5},{4,2},{5,3},{6,0},{7,1},{8,14},{9,15},{10,... | collective-permute-start | bytes 589832 | tf_op jit(solution)/shard_map/ppermute | solution.py:857
  70.6 16.9 %collective-permute-start.22 = (bf16[384,256]{1,0:T(8,128)(2,1)}, bf16[384,256]{1,0:T(8,128)(2,1)S(1)}, u32[]{:S(2)}, u32[]{:S(2)}) collective-permute-start(bf16[384,256]{1,0:T(8,128)(2,1)} %get-tuple-element.109), channel_id=1, source_target_pairs={{0,7},{1,6},{2,5},{3,4},{4,3},{5,2},{6,1},{7,0},{8,15},{9,14},{10,... | collective-permute-start | bytes 589832 | tf_op jit(solution)/shard_map/ppermute | solution.py:857
  86.6 26.6 %collective-permute-start.23 = (bf16[768,768]{1,0:T(8,128)(2,1)S(1)}, bf16[768,768]{1,0:T(8,128)(2,1)}, u32[]{:S(2)}, u32[]{:S(2)}) collective-permute-start(bf16[768,768]{1,0:T(8,128)(2,1)S(1)} %copy-done.46), channel_id=1, source_target_pairs={{0,16},{8,24},{16,0},{24,8},{1,17},{9,25},{17,1},{25,9},{2,18},{10... | collective-permute-start | bytes 3538952 | tf_op jit(solution)/shard_map/ppermute | solution.py:857
  113.1 21.9 %all-to-all-start.1 = ((bf16[8,192,256]{2,1,0:T(8,128)(2,1)}), bf16[8,192,256]{2,1,0:T(8,128)(2,1)S(1)}, u32[]{:S(2)}, u32[]{:S(2)}) async-start(bf16[8,192,256]{2,1,0:T(8,128)(2,1)} %mix_fwd.1), calls=%async_computation.1 | async-start | bytes 1572864 | tf_op jit(solution)/shard_map/all_to_all | solution.py:1017
  116.9 13.3 %collective-permute-start.29 = (bf16[768,768]{1,0:T(8,128)(2,1)}, bf16[768,768]{1,0:T(8,128)(2,1)}, u32[]{:S(2)}, u32[]{:S(2)}) collective-permute-start(bf16[768,768]{1,0:T(8,128)(2,1)} %d0.1), channel_id=1, source_target_pairs={{0,8},{8,0},{16,24},{24,16},{1,9},{9,1},{17,25},{25,17},{2,10},{10... | collective-permute-start | bytes 3538952 | tf_op jit(solution)/shard_map/ppermute | solution.py:857
  117.0 13.2 %collective-permute-start.27 = (bf16[192,3072]{1,0:T(8,128)(2,1)S(1)}, bf16[192,3072]{1,0:T(8,128)(2,1)}, u32[]{:S(2)}, u32[]{:S(2)}) collective-permute-start(bf16[192,3072]{1,0:T(8,128)(2,1)S(1)} %copy-done.45), channel_id=1, source_target_pairs={{0,8},{8,0},{16,24},{24,16},{1,9},{9,1},{17,25},{25,17},{2,10},{10... | collective-permute-start | bytes 3538952 | tf_op jit(solution)/shard_map/ppermute | solution.py:857
  117.5 12.7 %collective-permute-start.30 = (bf16[768,768]{1,0:T(8,128)(2,1)}, bf16[768,768]{1,0:T(8,128)(2,1)}, u32[]{:S(2)}, u32[]{:S(2)}) collective-permute-start(bf16[768,768]{1,0:T(8,128)(2,1)} %collective-permute-done.23.d2), channel_id=1, source_target_pairs={{0,8},{8,0},{16,24},{24,16},{1,9},{9,1},{17,25},{25,17},{2,10},{10... | collective-permute-start | bytes 3538952 | tf_op jit(solution)/shard_map/ppermute | solution.py:857
  117.5 12.6 %collective-permute-start.28 = (bf16[192,3072]{1,0:T(8,128)(2,1)}, bf16[192,3072]{1,0:T(8,128)(2,1)}, u32[]{:S(2)}, u32[]{:S(2)}) collective-permute-start(bf16[192,3072]{1,0:T(8,128)(2,1)} %collective-permute-done.15.u2), channel_id=1, source_target_pairs={{0,8},{8,0},{16,24},{24,16},{1,9},{9,1},{17,25},{25,17},{2,10},{10... | collective-permute-start | bytes 3538952 | tf_op jit(solution)/shard_map/ppermute | solution.py:857
  118.0 9.0 %collective-permute-start.25 = (bf16[192,768]{1,0:T(8,128)(2,1)S(1)}, bf16[192,768]{1,0:T(8,128)(2,1)S(1)}, u32[]{:S(2)}, u32[]{:S(2)}) collective-permute-start(bf16[192,768]{1,0:T(8,128)(2,1)S(1)} %copy-done.47), channel_id=1, source_target_pairs={{0,16},{8,24},{16,0},{24,8},{1,17},{9,25},{17,1},{25,9},{2,18},{10... | collective-permute-start | bytes 884744 | tf_op jit(solution)/shard_map/ppermute | solution.py:857
  127.0 1.6 collective-permute-start.24
  128.6 1.6 collective-permute-start.26
  155.8 22.8 %all-to-all-start.2 = ((bf16[8,192,256]{2,1,0:T(8,128)(2,1)}), bf16[8,192,256]{2,1,0:T(8,128)(2,1)S(1)}, u32[]{:S(2)}, u32[]{:S(2)}) async-start(bf16[8,192,256]{2,1,0:T(8,128)(2,1)} %get-tuple-element.121), calls=%async_computation.2 | async-start | bytes 1572864 | tf_op jit(solution)/shard_map/all_to_all | solution.py:1017
  178.5 13.4 %collective-permute-start.32 = (bf16[2,960,768]{2,1,0:T(8,128)(2,1)}, bf16[2,960,768]{2,1,0:T(8,128)(2,1)}, u32[]{:S(2)}, u32[]{:S(2)}) collective-permute-start(bf16[2,960,768]{2,1,0:T(8,128)(2,1)} %get-tuple-element.127), channel_id=1, source_target_pairs={{0,8},{8,0},{16,24},{24,16},{1,9},{9,1},{17,25},{25,17},{2,10},{10... | collective-permute-start | bytes 8847368 | tf_op jit(solution)/shard_map/ppermute | solution.py:857
  178.5 8.6 %collective-permute-start.31 = (bf16[2,768,768]{2,1,0:T(8,128)(2,1)}, bf16[2,768,768]{2,1,0:T(8,128)(2,1)S(1)}, u32[]{:S(2)}, u32[]{:S(2)}) collective-permute-start(bf16[2,768,768]{2,1,0:T(8,128)(2,1)} %get-tuple-element.125), channel_id=1, source_target_pairs={{0,8},{8,0},{16,24},{24,16},{1,9},{9,1},{17,25},{25,17},{2,10},{10... | collective-permute-start | bytes 7077896 | tf_op jit(solution)/shard_map/ppermute | solution.py:857
  190.5 44.0 %collective-permute-start.33 = (bf16[2,384,768]{2,1,0:T(8,128)(2,1)}, bf16[2,384,768]{2,1,0:T(8,128)(2,1)}, u32[]{:S(2)}, u32[]{:S(2)}) collective-permute-start(bf16[2,384,768]{2,1,0:T(8,128)(2,1)} %get-tuple-element.216), channel_id=1, source_target_pairs={{0,1},{1,0},{2,3},{3,2},{4,5},{5,4},{6,7},{7,6},{8,9},{9,8},{10,11... | collective-permute-start | bytes 3538952 | tf_op jit(solution)/shard_map/ppermute | solution.py:857
  195.8 40.4 %collective-permute-start.34 = (bf16[960,768]{1,0:T(8,128)(2,1)}, bf16[960,768]{1,0:T(8,128)(2,1)}, u32[]{:S(2)}, u32[]{:S(2)}) collective-permute-start(bf16[960,768]{1,0:T(8,128)(2,1)} %get-tuple-element.214), channel_id=1, source_target_pairs={{0,16},{8,24},{16,0},{24,8},{1,17},{9,25},{17,1},{25,9},{2,18},{10... | collective-permute-start | bytes 4423688 | tf_op jit(solution)/shard_map/ppermute | solution.py:857
  229.8 42.0 %all-to-all-start.3 = ((bf16[8,384,256]{2,1,0:T(8,128)(2,1)}), bf16[8,384,256]{2,1,0:T(8,128)(2,1)}, u32[]{:S(2)}, u32[]{:S(2)}) async-start(bf16[8,384,256]{2,1,0:T(8,128)(2,1)} %get-tuple-element.135), calls=%async_computation.3 | async-start | bytes 3145728 | tf_op jit(solution)/shard_map/all_to_all | solution.py:1017
  236.2 25.1 %collective-permute-start.35 = (bf16[384,768]{1,0:T(8,128)(2,1)S(1)}, bf16[384,768]{1,0:T(8,128)(2,1)S(1)}, u32[]{:S(2)}, u32[]{:S(2)}) collective-permute-start(bf16[384,768]{1,0:T(8,128)(2,1)S(1)} %get-tuple-element.228), channel_id=1, source_target_pairs={{0,16},{8,24},{16,0},{24,8},{1,17},{9,25},{17,1},{25,9},{2,18},{10... | collective-permute-start | bytes 1769480 | tf_op jit(solution)/shard_map/ppermute | solution.py:857
  271.8 24.3 %all-to-all-start.4 = ((bf16[8,192,256]{2,1,0:T(8,128)(2,1)}), bf16[8,192,256]{2,1,0:T(8,128)(2,1)S(1)}, u32[]{:S(2)}, u32[]{:S(2)}) async-start(bf16[8,192,256]{2,1,0:T(8,128)(2,1)} %get-tuple-element.141), calls=%async_computation.4 | async-start | bytes 1572864 | tf_op jit(solution)/shard_map/all_to_all | solution.py:1017
  282.5 26.1 %collective-permute-start.37 = (bf16[2,384,768]{2,1,0:T(8,128)(2,1)}, bf16[2,384,768]{2,1,0:T(8,128)(2,1)S(1)}, u32[]{:S(2)}, u32[]{:S(2)}) collective-permute-start(bf16[2,384,768]{2,1,0:T(8,128)(2,1)} %get-tuple-element.143), channel_id=1, source_target_pairs={{0,8},{8,0},{16,24},{24,16},{1,9},{9,1},{17,25},{25,17},{2,10},{10... | collective-permute-start | bytes 3538952 | tf_op jit(solution)/shard_map/ppermute | solution.py:857
  282.6 21.8 %collective-permute-start.36 = (bf16[480,768]{1,0:T(8,128)(2,1)}, bf16[480,768]{1,0:T(8,128)(2,1)}, u32[]{:S(2)}, u32[]{:S(2)}) collective-permute-start(bf16[480,768]{1,0:T(8,128)(2,1)} %get-tuple-element.220), channel_id=1, source_target_pairs={{0,1},{1,0},{2,3},{3,2},{4,5},{5,4},{6,7},{7,6},{8,9},{9,8},{10,11... | collective-permute-start | bytes 2211848 | tf_op jit(solution)/shard_map/ppermute | solution.py:857
  284.7 24.9 %collective-permute-start.38 = (bf16[192,768]{1,0:T(8,128)(2,1)}, bf16[192,768]{1,0:T(8,128)(2,1)S(1)}, u32[]{:S(2)}, u32[]{:S(2)}) collective-permute-start(bf16[192,768]{1,0:T(8,128)(2,1)} %get-tuple-element.246), channel_id=1, source_target_pairs={{0,2},{1,3},{2,0},{3,1},{4,6},{5,7},{6,4},{7,5},{8,10},{9,11},{10,... | collective-permute-start | bytes 884744 | tf_op jit(solution)/shard_map/ppermute | solution.py:857
  303.9 17.1 %collective-permute-start.40 = (bf16[2,256,768]{2,1,0:T(8,128)(2,1)}, bf16[2,256,768]{2,1,0:T(8,128)(2,1)S(1)}, u32[]{:S(2)}, u32[]{:S(2)}) collective-permute-start(bf16[2,256,768]{2,1,0:T(8,128)(2,1)} %get-tuple-element.149), channel_id=1, source_target_pairs={{0,8},{8,0},{16,24},{24,16},{1,9},{9,1},{17,25},{25,17},{2,10},{10... | collective-permute-start | bytes 2359304 | tf_op jit(solution)/shard_map/ppermute | solution.py:857
  305.8 14.7 %collective-permute-start.39 = (bf16[240,768]{1,0:T(8,128)(2,1)S(1)}, bf16[240,768]{1,0:T(8,128)(2,1)S(1)}, u32[]{:S(2)}, u32[]{:S(2)}) collective-permute-start(bf16[240,768]{1,0:T(8,128)(2,1)S(1)} %get-tuple-element.236), channel_id=1, source_target_pairs={{0,2},{1,3},{2,0},{3,1},{4,6},{5,7},{6,4},{7,5},{8,10},{9,11},{10,... | collective-permute-start | bytes 1105928 | tf_op jit(solution)/shard_map/ppermute | solution.py:857
  309.0 15.0 %collective-permute-start.42 = (bf16[384,768]{1,0:T(8,128)(2,1)S(1)}, bf16[384,768]{1,0:T(8,128)(2,1)S(1)}, u32[]{:S(2)}, u32[]{:S(2)}) collective-permute-start(bf16[384,768]{1,0:T(8,128)(2,1)S(1)} %get-tuple-element.226), channel_id=1, source_target_pairs={{0,16},{8,24},{16,0},{24,8},{1,17},{9,25},{17,1},{25,9},{2,18},{10... | collective-permute-start | bytes 1769480 | tf_op jit(solution)/shard_map/ppermute | solution.py:857
  309.7 11.6 %collective-permute-start.41 = (bf16[96,768]{1,0:T(8,128)(2,1)S(1)}, bf16[96,768]{1,0:T(8,128)(2,1)S(1)}, u32[]{:S(2)}, u32[]{:S(2)}) collective-permute-start(bf16[96,768]{1,0:T(8,128)(2,1)S(1)} %get-tuple-element.258), channel_id=1, source_target_pairs={{0,4},{1,5},{2,6},{3,7},{4,0},{5,1},{6,2},{7,3},{8,12},{9,13},{10,... | collective-permute-start | bytes 442376 | tf_op jit(solution)/shard_map/ppermute | solution.py:857
  320.6 13.3 %collective-permute-start.43 = (bf16[120,768]{1,0:T(8,128)(2,1)S(1)}, bf16[120,768]{1,0:T(8,128)(2,1)S(1)}, u32[]{:S(2)}, u32[]{:S(2)}) collective-permute-start(bf16[120,768]{1,0:T(8,128)(2,1)S(1)} %get-tuple-element.250), channel_id=1, source_target_pairs={{0,4},{1,5},{2,6},{3,7},{4,0},{5,1},{6,2},{7,3},{8,12},{9,13},{10,... | collective-permute-start | bytes 552968 | tf_op jit(solution)/shard_map/ppermute | solution.py:857
  324.2 9.9 %collective-permute-start.44 = (bf16[192,768]{1,0:T(8,128)(2,1)S(1)}, bf16[192,768]{1,0:T(8,128)(2,1)S(1)}, u32[]{:S(2)}, u32[]{:S(2)}) collective-permute-start(bf16[192,768]{1,0:T(8,128)(2,1)S(1)} %get-tuple-element.244), channel_id=1, source_target_pairs={{0,1},{1,0},{2,3},{3,2},{4,5},{5,4},{6,7},{7,6},{8,9},{9,8},{10,11... | collective-permute-start | bytes 884744 | tf_op jit(solution)/shard_map/ppermute | solution.py:857
  324.3 16.1 %collective-permute-start.45 = (bf16[96,768]{1,0:T(8,128)(2,1)S(1)}, bf16[96,768]{1,0:T(8,128)(2,1)S(1)}, u32[]{:S(2)}, u32[]{:S(2)}) collective-permute-start(bf16[96,768]{1,0:T(8,128)(2,1)S(1)} %add_convert_fusion.15), channel_id=1, source_target_pairs={{0,4},{1,5},{2,6},{3,7},{4,0},{5,1},{6,2},{7,3},{8,12},{9,13},{10,... | collective-permute-start | bytes 442376 | tf_op jit(solution)/shard_map/ppermute | solution.py:857
  326.4 18.7 %collective-permute-start.47 = (bf16[256,768]{1,0:T(8,128)(2,1)S(1)}, bf16[256,768]{1,0:T(8,128)(2,1)S(1)}, u32[]{:S(2)}, u32[]{:S(2)}) collective-permute-start(bf16[256,768]{1,0:T(8,128)(2,1)S(1)} %get-tuple-element.232), channel_id=1, source_target_pairs={{0,16},{8,24},{16,0},{24,8},{1,17},{9,25},{17,1},{25,9},{2,18},{10... | collective-permute-start | bytes 1179656 | tf_op jit(solution)/shard_map/ppermute | solution.py:857
  334.0 11.0 %collective-permute-start.46 = (bf16[120,768]{1,0:T(8,128)(2,1)S(1)}, bf16[120,768]{1,0:T(8,128)(2,1)S(1)}, u32[]{:S(2)}, u32[]{:S(2)}) collective-permute-start(bf16[120,768]{1,0:T(8,128)(2,1)S(1)} %add_convert_fusion.13), channel_id=1, source_target_pairs={{0,4},{1,5},{2,6},{3,7},{4,0},{5,1},{6,2},{7,3},{8,12},{9,13},{10,... | collective-permute-start | bytes 552968 | tf_op jit(solution)/shard_map/ppermute | solution.py:857
  334.2 15.9 %collective-permute-start.48 = (bf16[96,768]{1,0:T(8,128)(2,1)S(1)}, bf16[96,768]{1,0:T(8,128)(2,1)S(1)}, u32[]{:S(2)}, u32[]{:S(2)}) collective-permute-start(bf16[96,768]{1,0:T(8,128)(2,1)S(1)} %get-tuple-element.254), channel_id=1, source_target_pairs={{0,2},{1,3},{2,0},{3,1},{4,6},{5,7},{6,4},{7,5},{8,10},{9,11},{10,... | collective-permute-start | bytes 442376 | tf_op jit(solution)/shard_map/ppermute | solution.py:857
  340.4 12.7 %collective-permute-start.49 = (bf16[192,768]{1,0:T(8,128)(2,1)S(1)}, bf16[192,768]{1,0:T(8,128)(2,1)S(1)}, u32[]{:S(2)}, u32[]{:S(2)}) collective-permute-start(bf16[192,768]{1,0:T(8,128)(2,1)S(1)} %pad_maximum_fusion.5), channel_id=1, source_target_pairs={{0,2},{1,3},{2,0},{3,1},{4,6},{5,7},{6,4},{7,5},{8,10},{9,11},{10,... | collective-permute-start | bytes 884744 | tf_op jit(solution)/shard_map/ppermute | solution.py:857
  345.1 20.1 %collective-permute-start.50 = (bf16[240,768]{1,0:T(8,128)(2,1)S(1)}, bf16[240,768]{1,0:T(8,128)(2,1)S(1)}, u32[]{:S(2)}, u32[]{:S(2)}) collective-permute-start(bf16[240,768]{1,0:T(8,128)(2,1)S(1)} %pad_maximum_fusion.4), channel_id=1, source_target_pairs={{0,2},{1,3},{2,0},{3,1},{4,6},{5,7},{6,4},{7,5},{8,10},{9,11},{10,... | collective-permute-start | bytes 1105928 | tf_op jit(solution)/shard_map/ppermute | solution.py:857
  346.0 21.4 %all-to-all-start.5 = ((bf16[8,32,768]{2,1,0:T(8,128)(2,1)}), bf16[8,32,768]{2,1,0:T(8,128)(2,1)S(1)}, u32[]{:S(2)}, u32[]{:S(2)}) async-start(bf16[8,32,768]{2,1,0:T(8,128)(2,1)} %bitcast.47), calls=%async_computation.5 | async-start | bytes 786432 | tf_op jit(solution)/shard_map/all_to_all | solution.py:969
  350.2 17.4 %collective-permute-start.51 = (bf16[48,768]{1,0:T(8,128)(2,1)S(1)}, bf16[48,768]{1,0:T(8,128)(2,1)S(1)}, u32[]{:S(2)}, u32[]{:S(2)}) collective-permute-start(bf16[48,768]{1,0:T(8,128)(2,1)S(1)} %get-tuple-element.262), channel_id=1, source_target_pairs={{0,4},{1,5},{2,6},{3,7},{4,0},{5,1},{6,2},{7,3},{8,12},{9,13},{10,... | collective-permute-start | bytes 221192 | tf_op jit(solution)/shard_map/ppermute | solution.py:857
  353.2 23.2 %collective-permute-start.56 = (bf16[384,768]{1,0:T(8,128)(2,1)S(1)}, bf16[384,768]{1,0:T(8,128)(2,1)S(1)}, u32[]{:S(2)}, u32[]{:S(2)}) collective-permute-start(bf16[384,768]{1,0:T(8,128)(2,1)S(1)} %pad_maximum_fusion.2), channel_id=1, source_target_pairs={{0,1},{1,0},{2,3},{3,2},{4,5},{5,4},{6,7},{7,6},{8,9},{9,8},{10,11... | collective-permute-start | bytes 1769480 | tf_op jit(solution)/shard_map/ppermute | solution.py:857
  367.6 6.8 %collective-permute-start.52 = (bf16[48,768]{1,0:T(8,128)(2,1)S(1)}, bf16[48,768]{1,0:T(8,128)(2,1)S(1)}, u32[]{:S(2)}, u32[]{:S(2)}) collective-permute-start(bf16[48,768]{1,0:T(8,128)(2,1)S(1)} %add_convert_fusion.16), channel_id=1, source_target_pairs={{0,4},{1,5},{2,6},{3,7},{4,0},{5,1},{6,2},{7,3},{8,12},{9,13},{10,... | collective-permute-start | bytes 221192 | tf_op jit(solution)/shard_map/ppermute | solution.py:857
  367.6 22.6 %collective-permute-start.55 = (bf16[480,768]{1,0:T(8,128)(2,1)S(1)}, bf16[480,768]{1,0:T(8,128)(2,1)S(1)}, u32[]{:S(2)}, u32[]{:S(2)}) collective-permute-start(bf16[480,768]{1,0:T(8,128)(2,1)S(1)} %pad_maximum_fusion.1), channel_id=1, source_target_pairs={{0,1},{1,0},{2,3},{3,2},{4,5},{5,4},{6,7},{7,6},{8,9},{9,8},{10,11... | collective-permute-start | bytes 2211848 | tf_op jit(solution)/shard_map/ppermute | solution.py:857
  369.0 28.8 %all-to-all-start.6 = ((bf16[8,32,768]{2,1,0:T(8,128)(2,1)}), bf16[8,32,768]{2,1,0:T(8,128)(2,1)S(1)}, u32[]{:S(2)}, u32[]{:S(2)}) async-start(bf16[8,32,768]{2,1,0:T(8,128)(2,1)} %broadcast_in_dim.108), calls=%async_computation.6 | async-start | bytes 786432 | tf_op jit(solution)/shard_map/all_to_all | solution.py:976
  374.4 11.2 %collective-permute-start.53 = (bf16[96,768]{1,0:T(8,128)(2,1)S(1)}, bf16[96,768]{1,0:T(8,128)(2,1)S(1)}, u32[]{:S(2)}, u32[]{:S(2)}) collective-permute-start(bf16[96,768]{1,0:T(8,128)(2,1)S(1)} %pad_maximum_fusion.7), channel_id=1, source_target_pairs={{0,2},{1,3},{2,0},{3,1},{4,6},{5,7},{6,4},{7,5},{8,10},{9,11},{10,... | collective-permute-start | bytes 442376 | tf_op jit(solution)/shard_map/ppermute | solution.py:857
  385.7 10.9 %collective-permute-start.54 = (bf16[192,768]{1,0:T(8,128)(2,1)S(1)}, bf16[192,768]{1,0:T(8,128)(2,1)S(1)}, u32[]{:S(2)}, u32[]{:S(2)}) collective-permute-start(bf16[192,768]{1,0:T(8,128)(2,1)S(1)} %pad_maximum_fusion.6), channel_id=1, source_target_pairs={{0,1},{1,0},{2,3},{3,2},{4,5},{5,4},{6,7},{7,6},{8,9},{9,8},{10,11... | collective-permute-start | bytes 884744 | tf_op jit(solution)/shard_map/ppermute | solution.py:857
  (51 other events, 368.4 us)

commit v3 on v2

--- a/solution.py
+++ b/solution.py
@@ -1155,13 +1155,13 @@
     query_grad, value_grad = query_value[:shard], query_value[shard:]
     norms = jnp.concatenate([key_rows[shard : shard + 2], key_rows[shard + 8 : shard + 10]])
     norms = lax.dynamic_slice_in_dim(norms, place * shard, shard, 1)
-    owned = jnp.concatenate([norms.reshape(-1), key_rows[shard + 10 :].reshape(-1)])
-    shapes = [ln1_gain.shape, ln1_bias.shape, ln2_gain.shape, ln2_bias.shape, shift_taps.shape]
-    shapes += [ssm_rate.shape, ssm_freq.shape, ssm_coef.shape, ssm_skip.shape]
-    little, at = [], 0
-    for shape in shapes:
+    taps_rows = shift_taps.size // width
+    modes = key_rows[shard + 10 + taps_rows]
+    little, at = [norms[row] for row in range(4)], 0
+    little.append(key_rows[shard + 10 : shard + 10 + taps_rows].reshape(shift_taps.shape))
+    for shape in (ssm_rate.shape, ssm_freq.shape, ssm_coef.shape, ssm_skip.shape):
         count = int(np.prod(shape))
-        little.append(owned[at : at + count].reshape(shape))
+        little.append(modes[at : at + count].reshape(shape))
         at += count
     return (
         output.reshape(seqs, rows, width),

time: 407 us -> 408 us (level)
  starting transfers between devices: 84.2 us -> 90.4 us
  waiting for transfers between devices: 115 us -> 110 us
    ppermute x57, starting transfers between devices: 52.5 us -> 57.8 us  [xor_permute(): lax.ppermute(value, axis, [(source, source ^ mask) for source in range(co...]
    ppermute x57, waiting for transfers between devices: 90.9 us -> 86.5 us  [xor_permute(): lax.ppermute(value, axis, [(source, source ^ mask) for source in range(co...]
  transfers between devices with their start and end apart: 64 -> 64, of which waited for: 25 -> 25; matrix products, arithmetic and copies ran while one was open for 13% -> 13% of each run, Pallas kernels for 30% -> 29%
where the time goes in v3:
time: 408 us; the launch traced here: 403 us
  Pallas kernels  138 us (34%)
  waiting for transfers between devices  110 us (27%)
  starting transfers between devices  90.4 us (22%)
  local copies, waits for them, and re-layouts  35.5 us (9%)
  other arithmetic  27.3 us (7%)
    ppermute x57, waiting for transfers between devices, xor_permute(): lax.ppermute(value, axis, [(source, source ^ mask) for source in range(co...  86.5 us
    ppermute x57, starting transfers between devices, xor_permute(): lax.ppermute(value, axis, [(source, source ^ mask) for source in range(co...  57.8 us
    pallas_call x1, Pallas kernels, mix_bwd(): pl.pallas_call(functools.partial(mix_bwd_merged if v_base else mix_bwd_ke...  32 us
    all_to_all x5, starting transfers between devices, exchange(): return lax.all_to_all(value, 'dp', 0, 0, axis_index_groups=groups)  23.2 us
    all_to_all x5, waiting for transfers between devices, exchange(): return lax.all_to_all(value, 'dp', 0, 0, axis_index_groups=groups)  21 us
    pallas_call x1, Pallas kernels, shift_bwd(): pl.pallas_call(shift_bwd_kernel, out_shape=(jax.ShapeDtypeStruct((SHIFT,...  20.1 us
    pallas_call x1, Pallas kernels, middle_call(): pl.pallas_call(middle_kernel, out_shape=(jax.ShapeDtypeStruct((tokens, wi...  19.8 us
    pallas_call x1, Pallas kernels, ffn_grads_call(): pl.pallas_call(ffn_grads_kernel, out_shape=(jax.ShapeDtypeStruct((tokens,...  15 us
  transfers between devices with their start and end apart: 64, of which 25 were waited for; matrix products, arithmetic and copies ran while one was open for 13% of the time, Pallas kernels for 29%

profile of v3, /device:TPU:0, one launch (start us, length us, event | category | flops | bytes accessed | tf_op | source)
XLA Modules:
  0.0 403.0 jit_solution(3869581066788222899)
XLA Ops:
  2.1 3.0 collective-permute-start.1
  9.0 2.1 concatenate.51
  11.1 3.6 collective-permute-done.4.w2.k2
  15.0 3.6 collective-permute-done.13
  24.3 1.8 collective-permute-start.7
  27.4 4.2 %key_call.1 = (bf16[512,768]{1,0:T(8,128)(2,1)}, bf16[8,192,256]{2,1,0:T(8,128)(2,1)}, f32[2,768]{1,0:T(2,128)}) custom-call(s32[2]{0:T(128)} %pad_add_fusion.1.me_ref, bf16[512,768]{1,0:T(8,128)(2,1)} %bitcast.133, bf16[2,192]{1,0:T(2,128)(2,1)} %copy-done.33, bf16[2,192]{1,0:T(2,128)(2,1)} %copy-done.43, bf16[2,192]{1,0:T(2,128)(2,1)} %copy-done.42, ...), custom_call_target="tpu_custom_call" | custom-call | flops 100000000 | bytes 8192 | tf_op jit(solution)/shard_map/key_call/pallas_call | solution.py:550
  31.6 6.4 %all-to-all-start = ((bf16[8,192,256]{2,1,0:T(8,128)(2,1)}), bf16[8,192,256]{2,1,0:T(8,128)(2,1)S(1)}, u32[]{:S(2)}, u32[]{:S(2)}) async-start(bf16[8,192,256]{2,1,0:T(8,128)(2,1)} %get-tuple-element.99), calls=%async_computation | async-start | bytes 1572864 | tf_op jit(solution)/shard_map/all_to_all | solution.py:1017
  39.1 4.2 %fusion.13 = f32[3,2560]{1,0:T(4,128)S(1)} fusion(f32[3,32]{1,0:T(4,128)S(1)} %mul.141, f32[3,32]{1,0:T(4,128)S(1)} %reshape.368, f32[3,32]{1,0:T(4,128)S(1)} %mul.136, f32[2560]{0:T(1024)S(1)} %convert_select_fusion, f32[3,32]{1,0:T(4,128)S(1)} %neg.27), kind=kLoop, calls=%fused_computation.31 | loop fusion | flops 1712640 | bytes 42496 | tf_op jit(solution)/shard_map/jvp()/reduce_sum | solution.py:992
  46.1 5.7 %query_value_call.1 = (bf16[384,256]{1,0:T(8,128)(2,1)}, bf16[384,256]{1,0:T(8,128)(2,1)}, bf16[384,256]{1,0:T(8,128)(2,1)}, bf16[384,256]{1,0:T(8,128)(2,1)}, b...) custom-call(s32[2]{0:T(128)} %pad_add_fusion.1.me_ref, ...), custom_call_target="tpu_custom_call" | custom-call | flops 100000000 | bytes 8192 | tf_op jit(solution)/shard_map/query_value_call/pallas_call | solution.py:586
  51.8 2.1 collective-permute-start.16
  56.2 2.8 collective-permute-start.19
  59.7 3.2 collective-permute-start.20
  62.9 6.0 %collective-permute-done.17.refs_2_ = bf16[384,256]{1,0:T(8,128)(2,1)S(1)} collective-permute-done((bf16[384,256]{1,0:T(8,128)(2,1)}, bf16[384,256]{1,0:T(8,128)(2,1)S(1)}, u32[]{:S(2)}, u32[]{:S(2)}) %collective-permute-start.17) | collective-permute-done | bytes 196640 | tf_op jit(solution)/shard_map/ppermute | solution.py:857
  68.9 1.7 collective-permute-start.21
  70.6 2.6 collective-permute-start.22
  74.0 12.2 %shift_fwd.1.k_ref.refs_1_ = bf16[2048,192]{1,0:T(8,128)(2,1)} custom-call(s32[2176]{0:T(1024)} %copy-done.27, bf16[8,192,256]{2,1,0:T(8,128)(2,1)} %copy-done.4, bf16[64,192]{1,0:T(8,128)(2,1)} %broadcast_in_dim.91.halo_ref, f32[2,64,128]{2,1,0:T(8,128)} %pad_maximum_fusion.10.taps_ref, s32[2176,1]{1,0:T(8,128)} %broadcast_in_dim.109.segcol_ref), custom_call_target="tpu_custom_call" | custom-call | flops 10000000000 | bytes 262144 | tf_op jit(solution)/shard_map/shift_fwd/pallas_call | solution.py:185
  89.1 2.7 collect_qv.1.q_ref.v_ref.refs_0_.refs_2_
  91.9 12.6 %mix_fwd.1 = bf16[8,192,256]{2,1,0:T(8,128)(2,1)} custom-call(bf16[8,384,256]{2,1,0:T(8,128)(2,1)} %collect_qv.1.q_ref.v_ref.refs_0_.refs_2_, bf16[2048,192]{1,0:T(8,128)(2,1)} %shift_fwd.1.k_ref.refs_1_, bf16[8,384,256]{2,1,0:T(8,128)(2,1)} %collect_qv.1.q_ref.v_ref.refs_0_.refs_2_, f32[3,1,2560]{2,1,0:T(1,128)} %broadcast_select_fusion.18.row_ref.refs_4_, ...), custom_call_target="tpu_custom_call" | custom-call | flops 20000000000 | bytes 524288 | tf_op jit(solution)/shard_map/mix_fwd/pallas_call | solution.py:356
  104.5 8.9 %collective-permute-done.23.d2 = bf16[768,768]{1,0:T(8,128)(2,1)} collective-permute-done((bf16[768,768]{1,0:T(8,128)(2,1)S(1)}, bf16[768,768]{1,0:T(8,128)(2,1)}, u32[]{:S(2)}, u32[]{:S(2)}) %collective-permute-start.23) | collective-permute-done | bytes 1179680 | tf_op jit(solution)/shard_map/ppermute | solution.py:857
  113.4 3.7 all-to-all-start.1
  119.2 8.0 %collective-permute-done.25.o2 = bf16[192,768]{1,0:T(8,128)(2,1)S(1)} collective-permute-done((bf16[192,768]{1,0:T(8,128)(2,1)S(1)}, bf16[192,768]{1,0:T(8,128)(2,1)S(1)}, u32[]{:S(2)}, u32[]{:S(2)}) %collective-permute-start.25) | collective-permute-done | bytes 294944 | tf_op jit(solution)/shard_map/ppermute | solution.py:857
  127.2 1.6 collective-permute-done.24.o1
  130.4 5.4 %all-to-all-done.1.y_ref = bf16[8,192,256]{2,1,0:T(8,128)(2,1)S(1)} async-done(((bf16[8,192,256]{2,1,0:T(8,128)(2,1)}), bf16[8,192,256]{2,1,0:T(8,128)(2,1)S(1)}, u32[]{:S(2)}, u32[]{:S(2)}) %all-to-all-start.1) | async-done | bytes 786464 | tf_op jit(solution)/shard_map/all_to_all | solution.py:1017
  136.7 19.8 %middle_call.1 = (f32[512,768]{1,0:T(8,128)}, bf16[512,768]{1,0:T(8,128)(2,1)}, bf16[512,3072]{1,0:T(8,128)(2,1)}, bf16[512,3072]{1,0:T(8,128)(2,1)}, f32[512,76...) custom-call(s32[2]{0:T(128)} %pad_add_fusion.1.me_ref, bf16[8,192,256]{2,1,0:T(8,128)(2,1)} %copy-done.7, ...), custom_call_target="tpu_custom_call" | custom-call | flops 15000000512 | bytes 3145728 | tf_op jit(solution)/shard_map/middle_call/pallas_call | solution.py:656
  156.6 3.6 all-to-all-start.2
  160.1 15.0 %ffn_grads_call.1 = (bf16[512,768]{1,0:T(8,128)(2,1)}, bf16[2,768,768]{2,1,0:T(8,128)(2,1)}, bf16[2,768,768]{2,1,0:T(8,128)(2,1)}, bf16[2,960,768]{2,1,0:T(8,128)(2,1)}, bf16[2,960,768]{2,1,0:T(8,128)(2,1)}) custom-call(s32[2]{0:T(128)} %pad_add_fusion.1.me_ref, bf16[8,192,256]{2,1,0:T(8,128)(2,1)} %copy-done.7, f32[512,768]{1,0:T(8,128)} %get-tuple-element.113.resid_ref, ...), custom_call_target="tpu_custom_call" | custom-call | flops 19000000512 | bytes 3145728 | tf_op jit(solution)/shard_map/ffn_grads_call/pallas_call | solution.py:726
  175.1 4.8 %all-to-all-done.2.refs_3_ = bf16[8,192,256]{2,1,0:T(8,128)(2,1)S(1)} async-done(((bf16[8,192,256]{2,1,0:T(8,128)(2,1)}), bf16[8,192,256]{2,1,0:T(8,128)(2,1)S(1)}, u32[]{:S(2)}, u32[]{:S(2)}) %all-to-all-start.2) | async-done | bytes 786464 | tf_op jit(solution)/shard_map/all_to_all | solution.py:1017
  180.4 8.1 %collective-permute-done.31 = bf16[2,768,768]{2,1,0:T(8,128)(2,1)S(1)} collective-permute-done((bf16[2,768,768]{2,1,0:T(8,128)(2,1)}, bf16[2,768,768]{2,1,0:T(8,128)(2,1)S(1)}, u32[]{:S(2)}, u32[]{:S(2)}) %collective-permute-start.31) | collective-permute-done | bytes 2359328 | tf_op jit(solution)/shard_map/ppermute | solution.py:857
  188.5 2.2 add_convert_fusion.1
  193.3 2.6 add_convert_fusion
  197.7 32.0 %mix_bwd.1 = (bf16[8,384,256]{2,1,0:T(8,128)(2,1)}, f32[2048,192]{1,0:T(8,128)}, f32[3,1,2560]{2,1,0:T(1,128)}) custom-call(bf16[8,384,256]{2,1,0:T(8,128)(2,1)} %collect_qv.1.q_ref.v_ref.refs_0_.refs_2_, bf16[2048,192]{1,0:T(8,128)(2,1)} %shift_fwd.1.k_ref.refs_1_, bf16[8,384,256]{2,1,0:T(8,128)(2,1)} %collect_qv.1.q_ref.v_ref.refs_0_.refs_2_, ...), custom_call_target="tpu_custom_call" | custom-call | flops 40000000000 | bytes 1048576 | tf_op jit(solution)/shard_map/mix_bwd/pallas_call | solution.py:456
  229.6 4.7 %all-to-all-start.3 = ((bf16[8,384,256]{2,1,0:T(8,128)(2,1)}), bf16[8,384,256]{2,1,0:T(8,128)(2,1)}, u32[]{:S(2)}, u32[]{:S(2)}) async-start(bf16[8,384,256]{2,1,0:T(8,128)(2,1)} %get-tuple-element.135), calls=%async_computation.3 | async-start | bytes 3145728 | tf_op jit(solution)/shard_map/all_to_all | solution.py:1017
  234.3 1.5 add_convert_fusion.4
  236.0 1.6 collective-permute-start.35
  237.6 1.7 add_convert_fusion.2
  240.9 20.1 %shift_bwd.1 = (f32[64,192]{1,0:T(8,128)}, bf16[8,192,256]{2,1,0:T(8,128)(2,1)}) custom-call(s32[2176]{0:T(1024)} %copy-done.27, bf16[8,192,256]{2,1,0:T(8,128)(2,1)} %copy-done.4, bf16[64,192]{1,0:T(8,128)(2,1)} %broadcast_in_dim.91.halo_ref, f32[2048,192]{1,0:T(8,128)} %get-tuple-element.133.g_ref, f32[64,192]{1,0:T(8,128)} %broadcast_in_dim.97.ghalo_ref, ...), custom_call_target="tpu_custom_call" | custom-call | flops 20000000000 | bytes 524288 | tf_op jit(solution)/shard_map/shift_bwd/pallas_call | solution.py:259
  263.2 5.2 %fusion.19 = (f32[3,32]{1,0:T(4,128)S(1)}, bf16[3,32]{1,0:T(4,128)(2,1)S(1)}, f32[3,32]{1,0:T(4,128)S(1)}, f32[3,32]{1,0:T(4,128)S(1)}) fusion(f32[3,2560]{1,0:T(4,128)S(1)} %get-tuple-element.268, f32[3,32]{1,0:T(4,128)S(1)} %copy-done.41, f32[3,32]{1,0:T(4,128)S(1)} %copy-done.37, f32[3,32]{1,0:T(4,128)S(1)} %copy-done.39, f32[2560]{0:T(1024)S(1)} %copy-done.31, ...), kind=kLoop, calls=%fused_computation.38 | loop fusion | flops 5652096 | bytes 43840 | tf_op jit(solution)/shard_map/transpose(jvp())/reduce_sum | solution.py:988
  269.6 1.9 all-to-all-done.3.gqv_ref
  271.5 4.8 %all-to-all-start.4 = ((bf16[8,192,256]{2,1,0:T(8,128)(2,1)}), bf16[8,192,256]{2,1,0:T(8,128)(2,1)S(1)}, u32[]{:S(2)}, u32[]{:S(2)}) async-start(bf16[8,192,256]{2,1,0:T(8,128)(2,1)} %get-tuple-element.141), calls=%async_computation.4 | async-start | bytes 1572864 | tf_op jit(solution)/shard_map/all_to_all | solution.py:1017
  276.4 6.9 %qv_grads_call.1 = (bf16[2,384,768]{2,1,0:T(8,128)(2,1)}, bf16[2,384,768]{2,1,0:T(8,128)(2,1)}, f32[512,768]{1,0:T(8,128)}) custom-call(s32[2]{0:T(128)} %pad_add_fusion.1.me_ref, bf16[8,384,256]{2,1,0:T(8,128)(2,1)} %all-to-all-done.3.gqv_ref, bf16[512,768]{1,0:T(8,128)(2,1)} %get-tuple-element.95.act_ref, bf16[192,768]{1,0:T(8,128)(2,1)} %q0.1, ...), custom_call_target="tpu_custom_call" | custom-call | flops 8000000000 | bytes 1572864 | tf_op jit(solution)/shard_map/qv_grads_call/pallas_call | solution.py:785
  283.3 2.1 collective-permute-start.36
  286.9 8.9 %all-to-all-done.4.gk_ref = bf16[8,192,256]{2,1,0:T(8,128)(2,1)S(1)} async-done(((bf16[8,192,256]{2,1,0:T(8,128)(2,1)}), bf16[8,192,256]{2,1,0:T(8,128)(2,1)S(1)}, u32[]{:S(2)}, u32[]{:S(2)}) %all-to-all-start.4) | async-done | bytes 786464 | tf_op jit(solution)/shard_map/all_to_all | solution.py:1017
  296.7 6.9 %last_call.1 = (bf16[2,256,768]{2,1,0:T(8,128)(2,1)}, bf16[2,256,768]{2,1,0:T(8,128)(2,1)}, bf16[512,768]{1,0:T(8,128)(2,1)}) custom-call(s32[2]{0:T(128)} %pad_add_fusion.1.me_ref, bf16[8,192,256]{2,1,0:T(8,128)(2,1)} %copy-done.6, bf16[512,768]{1,0:T(8,128)(2,1)} %get-tuple-element.95.act_ref, f32[512,768]{1,0:T(8,128)} %get-tuple-element.145.ga_ref, ...), custom_call_target="tpu_custom_call" | custom-call | flops 6000000000 | bytes 1048576 | tf_op jit(solution)/shard_map/last_call/pallas_call | solution.py:834
  306.2 2.3 collective-permute-start.39
  311.5 8.6 %collective-permute-done.39 = bf16[240,768]{1,0:T(8,128)(2,1)S(1)} collective-permute-done((bf16[240,768]{1,0:T(8,128)(2,1)S(1)}, bf16[240,768]{1,0:T(8,128)(2,1)S(1)}, u32[]{:S(2)}, u32[]{:S(2)}) %collective-permute-start.39) | collective-permute-done | bytes 368672 | tf_op jit(solution)/shard_map/ppermute | solution.py:857
  322.1 1.5 collective-permute-done.42
  324.1 2.5 collective-permute-start.45
  327.7 7.0 %collective-permute-done.43 = bf16[120,768]{1,0:T(8,128)(2,1)S(1)} collective-permute-done((bf16[120,768]{1,0:T(8,128)(2,1)S(1)}, bf16[120,768]{1,0:T(8,128)(2,1)S(1)}, u32[]{:S(2)}, u32[]{:S(2)}) %collective-permute-start.43) | collective-permute-done | bytes 184352 | tf_op jit(solution)/shard_map/ppermute | solution.py:857
  335.0 2.2 collective-permute-start.48
  337.3 3.2 collective-permute-start.49
  340.5 4.6 %collective-permute-done.46 = bf16[120,768]{1,0:T(8,128)(2,1)S(1)} collective-permute-done((bf16[120,768]{1,0:T(8,128)(2,1)S(1)}, bf16[120,768]{1,0:T(8,128)(2,1)S(1)}, u32[]{:S(2)}, u32[]{:S(2)}) %collective-permute-start.46) | collective-permute-done | bytes 184352 | tf_op jit(solution)/shard_map/ppermute | solution.py:857
  346.1 4.0 all-to-all-start.5
  350.2 3.0 collective-permute-start.51
  353.3 1.5 collective-permute-start.56
  354.8 10.4 %collective-permute-done.50 = bf16[240,768]{1,0:T(8,128)(2,1)S(1)} collective-permute-done((bf16[240,768]{1,0:T(8,128)(2,1)S(1)}, bf16[240,768]{1,0:T(8,128)(2,1)S(1)}, u32[]{:S(2)}, u32[]{:S(2)}) %collective-permute-start.50) | collective-permute-done | bytes 368672 | tf_op jit(solution)/shard_map/ppermute | solution.py:857
  365.3 2.2 all-to-all-done.5
  368.8 5.4 %all-to-all-start.6 = ((bf16[8,32,768]{2,1,0:T(8,128)(2,1)}), bf16[8,32,768]{2,1,0:T(8,128)(2,1)S(1)}, u32[]{:S(2)}, u32[]{:S(2)}) async-start(bf16[8,32,768]{2,1,0:T(8,128)(2,1)} %broadcast_in_dim.108), calls=%async_computation.6 | async-start | bytes 786432 | tf_op jit(solution)/shard_map/all_to_all | solution.py:976
  374.3 2.1 collective-permute-start.53
  376.5 1.6 maximum_convert_fusion
  378.1 7.5 %collective-permute-done.53 = bf16[96,768]{1,0:T(8,128)(2,1)S(1)} collective-permute-done((bf16[96,768]{1,0:T(8,128)(2,1)S(1)}, bf16[96,768]{1,0:T(8,128)(2,1)S(1)}, u32[]{:S(2)}, u32[]{:S(2)}) %collective-permute-start.53) | collective-permute-done | bytes 147488 | tf_op jit(solution)/shard_map/ppermute | solution.py:857
  385.6 1.6 collective-permute-start.54
  387.2 3.4 collective-permute-done.55
  392.0 1.5 copy.48
  393.5 1.8 copy.55
  (313 shorter events, 60.7 us)
Async XLA Ops:
  2.1 20.0 %collective-permute-start.1 = (bf16[2,192]{1,0:T(2,128)(2,1)S(1)}, bf16[2,192]{1,0:T(2,128)(2,1)S(1)}, u32[]{:S(2)}, u32[]{:S(2)}) collective-permute-start(bf16[2,192]{1,0:T(2,128)(2,1)S(1)} %pad_maximum_fusion.11.n0), channel_id=1, source_target_pairs={{0,16},{8,24},{16,0},{24,8},{1,17},{9,25},{17,1},{25,9},{2,18},{10... | collective-permute-start | bytes 2312 | tf_op jit(solution)/shard_map/ppermute | solution.py:857
  5.1 19.2 %collective-permute-start = (bf16[2,192]{1,0:T(2,128)(2,1)S(1)}, bf16[2,192]{1,0:T(2,128)(2,1)S(1)}, u32[]{:S(2)}, u32[]{:S(2)}) collective-permute-start(bf16[2,192]{1,0:T(2,128)(2,1)S(1)} %pad_maximum_fusion.11.n0), channel_id=1, source_target_pairs={{0,8},{8,0},{16,24},{24,16},{1,9},{9,1},{17,25},{25,17},{2,10},{10... | collective-permute-start | bytes 2312 | tf_op jit(solution)/shard_map/ppermute | solution.py:857
  5.1 9.6 %collective-permute-start.4 = (bf16[192,768]{1,0:T(8,128)(2,1)}, bf16[192,768]{1,0:T(8,128)(2,1)S(1)}, u32[]{:S(2)}, u32[]{:S(2)}) collective-permute-start(bf16[192,768]{1,0:T(8,128)(2,1)} %k0.1), channel_id=1, source_target_pairs={{0,16},{8,24},{16,0},{24,8},{1,17},{9,25},{17,1},{25,9},{2,18},{10... | collective-permute-start | bytes 884744 | tf_op jit(solution)/shard_map/ppermute | solution.py:857
  5.3 21.1 %collective-permute-start.3 = (bf16[192,768]{1,0:T(8,128)(2,1)}, bf16[192,768]{1,0:T(8,128)(2,1)S(1)}, u32[]{:S(2)}, u32[]{:S(2)}) collective-permute-start(bf16[192,768]{1,0:T(8,128)(2,1)} %k0.1), channel_id=1, source_target_pairs={{0,8},{8,0},{16,24},{24,16},{1,9},{9,1},{17,25},{25,17},{2,10},{10... | collective-permute-start | bytes 884744 | tf_op jit(solution)/shard_map/ppermute | solution.py:857
  14.7 3.8 collective-permute-start.13
  15.0 7.6 %collective-permute-start.12 = (bf16[104,128]{1,0:T(8,128)(2,1)S(1)}, bf16[104,128]{1,0:T(8,128)(2,1)S(1)}, u32[]{:S(2)}, u32[]{:S(2)}) collective-permute-start(bf16[104,128]{1,0:T(8,128)(2,1)S(1)} %pad_bitcast_fusion), channel_id=1, source_target_pairs={{0,8},{8,0},{16,24},{24,16},{1,9},{9,1},{17,25},{25,17},{2,10},{10... | collective-permute-start | bytes 79880 | tf_op jit(solution)/shard_map/ppermute | solution.py:857
  18.6 4.5 %collective-permute-start.14 = (bf16[104,128]{1,0:T(8,128)(2,1)S(1)}, bf16[104,128]{1,0:T(8,128)(2,1)S(1)}, u32[]{:S(2)}, u32[]{:S(2)}) collective-permute-start(bf16[104,128]{1,0:T(8,128)(2,1)S(1)} %collective-permute-done.13), channel_id=1, source_target_pairs={{0,8},{8,0},{16,24},{24,16},{1,9},{9,1},{17,25},{25,17},{2,10},{10... | collective-permute-start | bytes 79880 | tf_op jit(solution)/shard_map/ppermute | solution.py:857
  22.0 4.1 %collective-permute-start.2 = (bf16[2,192]{1,0:T(2,128)(2,1)S(1)}, bf16[2,192]{1,0:T(2,128)(2,1)S(1)}, u32[]{:S(2)}, u32[]{:S(2)}) collective-permute-start(bf16[2,192]{1,0:T(2,128)(2,1)S(1)} %collective-permute-done.1.n2), channel_id=1, source_target_pairs={{0,8},{8,0},{16,24},{24,16},{1,9},{9,1},{17,25},{25,17},{2,10},{10... | collective-permute-start | bytes 2312 | tf_op jit(solution)/shard_map/ppermute | solution.py:857
  22.6 15.8 %collective-permute-start.10 = (bf16[192,768]{1,0:T(8,128)(2,1)S(1)}, bf16[192,768]{1,0:T(8,128)(2,1)S(1)}, u32[]{:S(2)}, u32[]{:S(2)}) collective-permute-start(bf16[192,768]{1,0:T(8,128)(2,1)S(1)} %copy-done.10), channel_id=1, source_target_pairs={{0,16},{8,24},{16,0},{24,8},{1,17},{9,25},{17,1},{25,9},{2,18},{10... | collective-permute-start | bytes 884744 | tf_op jit(solution)/shard_map/ppermute | solution.py:857
  23.1 3.6 collective-permute-start.5
  24.3 19.0 %collective-permute-start.7 = (bf16[192,768]{1,0:T(8,128)(2,1)S(1)}, bf16[192,768]{1,0:T(8,128)(2,1)S(1)}, u32[]{:S(2)}, u32[]{:S(2)}) collective-permute-start(bf16[192,768]{1,0:T(8,128)(2,1)S(1)} %copy-done.9), channel_id=1, source_target_pairs={{0,16},{8,24},{16,0},{24,8},{1,17},{9,25},{17,1},{25,9},{2,18},{10... | collective-permute-start | bytes 884744 | tf_op jit(solution)/shard_map/ppermute | solution.py:857
  26.1 18.7 %collective-permute-start.6 = (bf16[192,768]{1,0:T(8,128)(2,1)S(1)}, bf16[192,768]{1,0:T(8,128)(2,1)S(1)}, u32[]{:S(2)}, u32[]{:S(2)}) collective-permute-start(bf16[192,768]{1,0:T(8,128)(2,1)S(1)} %copy-done.9), channel_id=1, source_target_pairs={{0,8},{8,0},{16,24},{24,16},{1,9},{9,1},{17,25},{25,17},{2,10},{10... | collective-permute-start | bytes 884744 | tf_op jit(solution)/shard_map/ppermute | solution.py:857
  26.3 18.5 %collective-permute-start.9 = (bf16[192,768]{1,0:T(8,128)(2,1)S(1)}, bf16[192,768]{1,0:T(8,128)(2,1)S(1)}, u32[]{:S(2)}, u32[]{:S(2)}) collective-permute-start(bf16[192,768]{1,0:T(8,128)(2,1)S(1)} %copy-done.10), channel_id=1, source_target_pairs={{0,8},{8,0},{16,24},{24,16},{1,9},{9,1},{17,25},{25,17},{2,10},{10... | collective-permute-start | bytes 884744 | tf_op jit(solution)/shard_map/ppermute | solution.py:857
  31.6 41.6 %all-to-all-start = ((bf16[8,192,256]{2,1,0:T(8,128)(2,1)}), bf16[8,192,256]{2,1,0:T(8,128)(2,1)S(1)}, u32[]{:S(2)}, u32[]{:S(2)}) async-start(bf16[8,192,256]{2,1,0:T(8,128)(2,1)} %get-tuple-element.99), calls=%async_computation | async-start | bytes 1572864 | tf_op jit(solution)/shard_map/all_to_all | solution.py:1017
  38.5 32.1 %collective-permute-start.15 = (bf16[192,3072]{1,0:T(8,128)(2,1)}, bf16[192,3072]{1,0:T(8,128)(2,1)}, u32[]{:S(2)}, u32[]{:S(2)}) collective-permute-start(bf16[192,3072]{1,0:T(8,128)(2,1)} %u0), channel_id=1, source_target_pairs={{0,16},{8,24},{16,0},{24,8},{1,17},{9,25},{17,1},{25,9},{2,18},{10... | collective-permute-start | bytes 3538952 | tf_op jit(solution)/shard_map/ppermute | solution.py:857
  43.3 1.6 collective-permute-start.11
  43.4 2.0 collective-permute-start.8
  51.8 7.9 %collective-permute-start.16 = (bf16[384,256]{1,0:T(8,128)(2,1)}, bf16[384,256]{1,0:T(8,128)(2,1)S(1)}, u32[]{:S(2)}, u32[]{:S(2)}) collective-permute-start(bf16[384,256]{1,0:T(8,128)(2,1)} %get-tuple-element.103), channel_id=1, source_target_pairs={{0,1},{1,0},{2,3},{3,2},{4,5},{5,4},{6,7},{7,6},{8,9},{9,8},{10,11... | collective-permute-start | bytes 589832 | tf_op jit(solution)/shard_map/ppermute | solution.py:857
  53.9 15.0 %collective-permute-start.17 = (bf16[384,256]{1,0:T(8,128)(2,1)}, bf16[384,256]{1,0:T(8,128)(2,1)S(1)}, u32[]{:S(2)}, u32[]{:S(2)}) collective-permute-start(bf16[384,256]{1,0:T(8,128)(2,1)} %get-tuple-element.104), channel_id=1, source_target_pairs={{0,2},{1,3},{2,0},{3,1},{4,6},{5,7},{6,4},{7,5},{8,10},{9,11},{10,... | collective-permute-start | bytes 589832 | tf_op jit(solution)/shard_map/ppermute | solution.py:857
  56.1 30.2 %collective-permute-start.18 = (bf16[384,256]{1,0:T(8,128)(2,1)}, bf16[384,256]{1,0:T(8,128)(2,1)S(1)}, u32[]{:S(2)}, u32[]{:S(2)}) collective-permute-start(bf16[384,256]{1,0:T(8,128)(2,1)} %get-tuple-element.105), channel_id=1, source_target_pairs={{0,3},{1,2},{2,1},{3,0},{4,7},{5,6},{6,5},{7,4},{8,11},{9,10},{10,... | collective-permute-start | bytes 589832 | tf_op jit(solution)/shard_map/ppermute | solution.py:857
  56.2 31.5 %collective-permute-start.19 = (bf16[384,256]{1,0:T(8,128)(2,1)}, bf16[384,256]{1,0:T(8,128)(2,1)S(1)}, u32[]{:S(2)}, u32[]{:S(2)}) collective-permute-start(bf16[384,256]{1,0:T(8,128)(2,1)} %get-tuple-element.106), channel_id=1, source_target_pairs={{0,4},{1,5},{2,6},{3,7},{4,0},{5,1},{6,2},{7,3},{8,12},{9,13},{10,... | collective-permute-start | bytes 589832 | tf_op jit(solution)/shard_map/ppermute | solution.py:857
  59.7 28.0 %collective-permute-start.20 = (bf16[384,256]{1,0:T(8,128)(2,1)}, bf16[384,256]{1,0:T(8,128)(2,1)S(1)}, u32[]{:S(2)}, u32[]{:S(2)}) collective-permute-start(bf16[384,256]{1,0:T(8,128)(2,1)} %get-tuple-element.107), channel_id=1, source_target_pairs={{0,5},{1,4},{2,7},{3,6},{4,1},{5,0},{6,3},{7,2},{8,13},{9,12},{10,... | collective-permute-start | bytes 589832 | tf_op jit(solution)/shard_map/ppermute | solution.py:857
  68.9 18.8 %collective-permute-start.21 = (bf16[384,256]{1,0:T(8,128)(2,1)}, bf16[384,256]{1,0:T(8,128)(2,1)S(1)}, u32[]{:S(2)}, u32[]{:S(2)}) collective-permute-start(bf16[384,256]{1,0:T(8,128)(2,1)} %get-tuple-element.108), channel_id=1, source_target_pairs={{0,6},{1,7},{2,4},{3,5},{4,2},{5,3},{6,0},{7,1},{8,14},{9,15},{10,... | collective-permute-start | bytes 589832 | tf_op jit(solution)/shard_map/ppermute | solution.py:857
  70.6 17.1 %collective-permute-start.22 = (bf16[384,256]{1,0:T(8,128)(2,1)}, bf16[384,256]{1,0:T(8,128)(2,1)S(1)}, u32[]{:S(2)}, u32[]{:S(2)}) collective-permute-start(bf16[384,256]{1,0:T(8,128)(2,1)} %get-tuple-element.109), channel_id=1, source_target_pairs={{0,7},{1,6},{2,5},{3,4},{4,3},{5,2},{6,1},{7,0},{8,15},{9,14},{10,... | collective-permute-start | bytes 589832 | tf_op jit(solution)/shard_map/ppermute | solution.py:857
  86.3 27.1 %collective-permute-start.23 = (bf16[768,768]{1,0:T(8,128)(2,1)S(1)}, bf16[768,768]{1,0:T(8,128)(2,1)}, u32[]{:S(2)}, u32[]{:S(2)}) collective-permute-start(bf16[768,768]{1,0:T(8,128)(2,1)S(1)} %copy-done.46), channel_id=1, source_target_pairs={{0,16},{8,24},{16,0},{24,8},{1,17},{9,25},{17,1},{25,9},{2,18},{10... | collective-permute-start | bytes 3538952 | tf_op jit(solution)/shard_map/ppermute | solution.py:857
  113.4 22.4 %all-to-all-start.1 = ((bf16[8,192,256]{2,1,0:T(8,128)(2,1)}), bf16[8,192,256]{2,1,0:T(8,128)(2,1)S(1)}, u32[]{:S(2)}, u32[]{:S(2)}) async-start(bf16[8,192,256]{2,1,0:T(8,128)(2,1)} %mix_fwd.1), calls=%async_computation.1 | async-start | bytes 1572864 | tf_op jit(solution)/shard_map/all_to_all | solution.py:1017
  117.1 13.3 %collective-permute-start.29 = (bf16[768,768]{1,0:T(8,128)(2,1)}, bf16[768,768]{1,0:T(8,128)(2,1)}, u32[]{:S(2)}, u32[]{:S(2)}) collective-permute-start(bf16[768,768]{1,0:T(8,128)(2,1)} %d0.1), channel_id=1, source_target_pairs={{0,8},{8,0},{16,24},{24,16},{1,9},{9,1},{17,25},{25,17},{2,10},{10... | collective-permute-start | bytes 3538952 | tf_op jit(solution)/shard_map/ppermute | solution.py:857
  117.2 13.2 %collective-permute-start.27 = (bf16[192,3072]{1,0:T(8,128)(2,1)S(1)}, bf16[192,3072]{1,0:T(8,128)(2,1)}, u32[]{:S(2)}, u32[]{:S(2)}) collective-permute-start(bf16[192,3072]{1,0:T(8,128)(2,1)S(1)} %copy-done.45), channel_id=1, source_target_pairs={{0,8},{8,0},{16,24},{24,16},{1,9},{9,1},{17,25},{25,17},{2,10},{10... | collective-permute-start | bytes 3538952 | tf_op jit(solution)/shard_map/ppermute | solution.py:857
  117.7 12.7 %collective-permute-start.30 = (bf16[768,768]{1,0:T(8,128)(2,1)}, bf16[768,768]{1,0:T(8,128)(2,1)}, u32[]{:S(2)}, u32[]{:S(2)}) collective-permute-start(bf16[768,768]{1,0:T(8,128)(2,1)} %collective-permute-done.23.d2), channel_id=1, source_target_pairs={{0,8},{8,0},{16,24},{24,16},{1,9},{9,1},{17,25},{25,17},{2,10},{10... | collective-permute-start | bytes 3538952 | tf_op jit(solution)/shard_map/ppermute | solution.py:857
  117.8 12.6 %collective-permute-start.28 = (bf16[192,3072]{1,0:T(8,128)(2,1)}, bf16[192,3072]{1,0:T(8,128)(2,1)}, u32[]{:S(2)}, u32[]{:S(2)}) collective-permute-start(bf16[192,3072]{1,0:T(8,128)(2,1)} %collective-permute-done.15.u2), channel_id=1, source_target_pairs={{0,8},{8,0},{16,24},{24,16},{1,9},{9,1},{17,25},{25,17},{2,10},{10... | collective-permute-start | bytes 3538952 | tf_op jit(solution)/shard_map/ppermute | solution.py:857
  118.2 9.0 %collective-permute-start.25 = (bf16[192,768]{1,0:T(8,128)(2,1)S(1)}, bf16[192,768]{1,0:T(8,128)(2,1)S(1)}, u32[]{:S(2)}, u32[]{:S(2)}) collective-permute-start(bf16[192,768]{1,0:T(8,128)(2,1)S(1)} %copy-done.47), channel_id=1, source_target_pairs={{0,16},{8,24},{16,0},{24,8},{1,17},{9,25},{17,1},{25,9},{2,18},{10... | collective-permute-start | bytes 884744 | tf_op jit(solution)/shard_map/ppermute | solution.py:857
  127.2 1.6 collective-permute-start.24
  128.8 1.6 collective-permute-start.26
  156.6 23.3 %all-to-all-start.2 = ((bf16[8,192,256]{2,1,0:T(8,128)(2,1)}), bf16[8,192,256]{2,1,0:T(8,128)(2,1)S(1)}, u32[]{:S(2)}, u32[]{:S(2)}) async-start(bf16[8,192,256]{2,1,0:T(8,128)(2,1)} %get-tuple-element.121), calls=%async_computation.2 | async-start | bytes 1572864 | tf_op jit(solution)/shard_map/all_to_all | solution.py:1017
  179.9 13.4 %collective-permute-start.32 = (bf16[2,960,768]{2,1,0:T(8,128)(2,1)}, bf16[2,960,768]{2,1,0:T(8,128)(2,1)}, u32[]{:S(2)}, u32[]{:S(2)}) collective-permute-start(bf16[2,960,768]{2,1,0:T(8,128)(2,1)} %get-tuple-element.127), channel_id=1, source_target_pairs={{0,8},{8,0},{16,24},{24,16},{1,9},{9,1},{17,25},{25,17},{2,10},{10... | collective-permute-start | bytes 8847368 | tf_op jit(solution)/shard_map/ppermute | solution.py:857
  179.9 8.6 %collective-permute-start.31 = (bf16[2,768,768]{2,1,0:T(8,128)(2,1)}, bf16[2,768,768]{2,1,0:T(8,128)(2,1)S(1)}, u32[]{:S(2)}, u32[]{:S(2)}) collective-permute-start(bf16[2,768,768]{2,1,0:T(8,128)(2,1)} %get-tuple-element.125), channel_id=1, source_target_pairs={{0,8},{8,0},{16,24},{24,16},{1,9},{9,1},{17,25},{25,17},{2,10},{10... | collective-permute-start | bytes 7077896 | tf_op jit(solution)/shard_map/ppermute | solution.py:857
  191.9 42.4 %collective-permute-start.33 = (bf16[2,384,768]{2,1,0:T(8,128)(2,1)}, bf16[2,384,768]{2,1,0:T(8,128)(2,1)}, u32[]{:S(2)}, u32[]{:S(2)}) collective-permute-start(bf16[2,384,768]{2,1,0:T(8,128)(2,1)} %get-tuple-element.218), channel_id=1, source_target_pairs={{0,1},{1,0},{2,3},{3,2},{4,5},{5,4},{6,7},{7,6},{8,9},{9,8},{10,11... | collective-permute-start | bytes 3538952 | tf_op jit(solution)/shard_map/ppermute | solution.py:857
  197.2 40.4 %collective-permute-start.34 = (bf16[960,768]{1,0:T(8,128)(2,1)}, bf16[960,768]{1,0:T(8,128)(2,1)}, u32[]{:S(2)}, u32[]{:S(2)}) collective-permute-start(bf16[960,768]{1,0:T(8,128)(2,1)} %get-tuple-element.216), channel_id=1, source_target_pairs={{0,16},{8,24},{16,0},{24,8},{1,17},{9,25},{17,1},{25,9},{2,18},{10... | collective-permute-start | bytes 4423688 | tf_op jit(solution)/shard_map/ppermute | solution.py:857
  229.6 41.9 %all-to-all-start.3 = ((bf16[8,384,256]{2,1,0:T(8,128)(2,1)}), bf16[8,384,256]{2,1,0:T(8,128)(2,1)}, u32[]{:S(2)}, u32[]{:S(2)}) async-start(bf16[8,384,256]{2,1,0:T(8,128)(2,1)} %get-tuple-element.135), calls=%async_computation.3 | async-start | bytes 3145728 | tf_op jit(solution)/shard_map/all_to_all | solution.py:1017
  236.0 26.1 %collective-permute-start.35 = (bf16[384,768]{1,0:T(8,128)(2,1)S(1)}, bf16[384,768]{1,0:T(8,128)(2,1)S(1)}, u32[]{:S(2)}, u32[]{:S(2)}) collective-permute-start(bf16[384,768]{1,0:T(8,128)(2,1)S(1)} %get-tuple-element.230), channel_id=1, source_target_pairs={{0,16},{8,24},{16,0},{24,8},{1,17},{9,25},{17,1},{25,9},{2,18},{10... | collective-permute-start | bytes 1769480 | tf_op jit(solution)/shard_map/ppermute | solution.py:857
  271.5 24.3 %all-to-all-start.4 = ((bf16[8,192,256]{2,1,0:T(8,128)(2,1)}), bf16[8,192,256]{2,1,0:T(8,128)(2,1)S(1)}, u32[]{:S(2)}, u32[]{:S(2)}) async-start(bf16[8,192,256]{2,1,0:T(8,128)(2,1)} %get-tuple-element.141), calls=%async_computation.4 | async-start | bytes 1572864 | tf_op jit(solution)/shard_map/all_to_all | solution.py:1017
  283.2 25.3 %collective-permute-start.37 = (bf16[2,384,768]{2,1,0:T(8,128)(2,1)}, bf16[2,384,768]{2,1,0:T(8,128)(2,1)S(1)}, u32[]{:S(2)}, u32[]{:S(2)}) collective-permute-start(bf16[2,384,768]{2,1,0:T(8,128)(2,1)} %get-tuple-element.143), channel_id=1, source_target_pairs={{0,8},{8,0},{16,24},{24,16},{1,9},{9,1},{17,25},{25,17},{2,10},{10... | collective-permute-start | bytes 3538952 | tf_op jit(solution)/shard_map/ppermute | solution.py:857
  283.3 21.6 %collective-permute-start.36 = (bf16[480,768]{1,0:T(8,128)(2,1)}, bf16[480,768]{1,0:T(8,128)(2,1)}, u32[]{:S(2)}, u32[]{:S(2)}) collective-permute-start(bf16[480,768]{1,0:T(8,128)(2,1)} %get-tuple-element.222), channel_id=1, source_target_pairs={{0,1},{1,0},{2,3},{3,2},{4,5},{5,4},{6,7},{7,6},{8,9},{9,8},{10,11... | collective-permute-start | bytes 2211848 | tf_op jit(solution)/shard_map/ppermute | solution.py:857
  285.4 25.0 %collective-permute-start.38 = (bf16[192,768]{1,0:T(8,128)(2,1)}, bf16[192,768]{1,0:T(8,128)(2,1)S(1)}, u32[]{:S(2)}, u32[]{:S(2)}) collective-permute-start(bf16[192,768]{1,0:T(8,128)(2,1)} %get-tuple-element.246), channel_id=1, source_target_pairs={{0,2},{1,3},{2,0},{3,1},{4,6},{5,7},{6,4},{7,5},{8,10},{9,11},{10,... | collective-permute-start | bytes 884744 | tf_op jit(solution)/shard_map/ppermute | solution.py:857
  303.6 18.1 %collective-permute-start.40 = (bf16[2,256,768]{2,1,0:T(8,128)(2,1)}, bf16[2,256,768]{2,1,0:T(8,128)(2,1)S(1)}, u32[]{:S(2)}, u32[]{:S(2)}) collective-permute-start(bf16[2,256,768]{2,1,0:T(8,128)(2,1)} %get-tuple-element.149), channel_id=1, source_target_pairs={{0,8},{8,0},{16,24},{24,16},{1,9},{9,1},{17,25},{25,17},{2,10},{10... | collective-permute-start | bytes 2359304 | tf_op jit(solution)/shard_map/ppermute | solution.py:857
  306.2 13.8 %collective-permute-start.39 = (bf16[240,768]{1,0:T(8,128)(2,1)S(1)}, bf16[240,768]{1,0:T(8,128)(2,1)S(1)}, u32[]{:S(2)}, u32[]{:S(2)}) collective-permute-start(bf16[240,768]{1,0:T(8,128)(2,1)S(1)} %get-tuple-element.238), channel_id=1, source_target_pairs={{0,2},{1,3},{2,0},{3,1},{4,6},{5,7},{6,4},{7,5},{8,10},{9,11},{10,... | collective-permute-start | bytes 1105928 | tf_op jit(solution)/shard_map/ppermute | solution.py:857
  308.9 14.7 %collective-permute-start.42 = (bf16[384,768]{1,0:T(8,128)(2,1)S(1)}, bf16[384,768]{1,0:T(8,128)(2,1)S(1)}, u32[]{:S(2)}, u32[]{:S(2)}) collective-permute-start(bf16[384,768]{1,0:T(8,128)(2,1)S(1)} %get-tuple-element.228), channel_id=1, source_target_pairs={{0,16},{8,24},{16,0},{24,8},{1,17},{9,25},{17,1},{25,9},{2,18},{10... | collective-permute-start | bytes 1769480 | tf_op jit(solution)/shard_map/ppermute | solution.py:857
  310.5 11.5 %collective-permute-start.41 = (bf16[96,768]{1,0:T(8,128)(2,1)S(1)}, bf16[96,768]{1,0:T(8,128)(2,1)S(1)}, u32[]{:S(2)}, u32[]{:S(2)}) collective-permute-start(bf16[96,768]{1,0:T(8,128)(2,1)S(1)} %get-tuple-element.258), channel_id=1, source_target_pairs={{0,4},{1,5},{2,6},{3,7},{4,0},{5,1},{6,2},{7,3},{8,12},{9,13},{10,... | collective-permute-start | bytes 442376 | tf_op jit(solution)/shard_map/ppermute | solution.py:857
  320.2 14.5 %collective-permute-start.43 = (bf16[120,768]{1,0:T(8,128)(2,1)S(1)}, bf16[120,768]{1,0:T(8,128)(2,1)S(1)}, u32[]{:S(2)}, u32[]{:S(2)}) collective-permute-start(bf16[120,768]{1,0:T(8,128)(2,1)S(1)} %get-tuple-element.250), channel_id=1, source_target_pairs={{0,4},{1,5},{2,6},{3,7},{4,0},{5,1},{6,2},{7,3},{8,12},{9,13},{10,... | collective-permute-start | bytes 552968 | tf_op jit(solution)/shard_map/ppermute | solution.py:857
  323.8 11.1 %collective-permute-start.44 = (bf16[192,768]{1,0:T(8,128)(2,1)S(1)}, bf16[192,768]{1,0:T(8,128)(2,1)S(1)}, u32[]{:S(2)}, u32[]{:S(2)}) collective-permute-start(bf16[192,768]{1,0:T(8,128)(2,1)S(1)} %get-tuple-element.244), channel_id=1, source_target_pairs={{0,1},{1,0},{2,3},{3,2},{4,5},{5,4},{6,7},{7,6},{8,9},{9,8},{10,11... | collective-permute-start | bytes 884744 | tf_op jit(solution)/shard_map/ppermute | solution.py:857
  324.1 13.2 %collective-permute-start.45 = (bf16[96,768]{1,0:T(8,128)(2,1)S(1)}, bf16[96,768]{1,0:T(8,128)(2,1)S(1)}, u32[]{:S(2)}, u32[]{:S(2)}) collective-permute-start(bf16[96,768]{1,0:T(8,128)(2,1)S(1)} %add_convert_fusion.15), channel_id=1, source_target_pairs={{0,4},{1,5},{2,6},{3,7},{4,0},{5,1},{6,2},{7,3},{8,12},{9,13},{10,... | collective-permute-start | bytes 442376 | tf_op jit(solution)/shard_map/ppermute | solution.py:857
  326.6 18.7 %collective-permute-start.47 = (bf16[256,768]{1,0:T(8,128)(2,1)S(1)}, bf16[256,768]{1,0:T(8,128)(2,1)S(1)}, u32[]{:S(2)}, u32[]{:S(2)}) collective-permute-start(bf16[256,768]{1,0:T(8,128)(2,1)S(1)} %get-tuple-element.234), channel_id=1, source_target_pairs={{0,16},{8,24},{16,0},{24,8},{1,17},{9,25},{17,1},{25,9},{2,18},{10... | collective-permute-start | bytes 1179656 | tf_op jit(solution)/shard_map/ppermute | solution.py:857
  334.8 10.4 %collective-permute-start.46 = (bf16[120,768]{1,0:T(8,128)(2,1)S(1)}, bf16[120,768]{1,0:T(8,128)(2,1)S(1)}, u32[]{:S(2)}, u32[]{:S(2)}) collective-permute-start(bf16[120,768]{1,0:T(8,128)(2,1)S(1)} %add_convert_fusion.13), channel_id=1, source_target_pairs={{0,4},{1,5},{2,6},{3,7},{4,0},{5,1},{6,2},{7,3},{8,12},{9,13},{10,... | collective-permute-start | bytes 552968 | tf_op jit(solution)/shard_map/ppermute | solution.py:857
  335.0 15.1 %collective-permute-start.48 = (bf16[96,768]{1,0:T(8,128)(2,1)S(1)}, bf16[96,768]{1,0:T(8,128)(2,1)S(1)}, u32[]{:S(2)}, u32[]{:S(2)}) collective-permute-start(bf16[96,768]{1,0:T(8,128)(2,1)S(1)} %get-tuple-element.254), channel_id=1, source_target_pairs={{0,2},{1,3},{2,0},{3,1},{4,6},{5,7},{6,4},{7,5},{8,10},{9,11},{10,... | collective-permute-start | bytes 442376 | tf_op jit(solution)/shard_map/ppermute | solution.py:857
  337.3 15.9 %collective-permute-start.49 = (bf16[192,768]{1,0:T(8,128)(2,1)S(1)}, bf16[192,768]{1,0:T(8,128)(2,1)S(1)}, u32[]{:S(2)}, u32[]{:S(2)}) collective-permute-start(bf16[192,768]{1,0:T(8,128)(2,1)S(1)} %pad_maximum_fusion.5), channel_id=1, source_target_pairs={{0,2},{1,3},{2,0},{3,1},{4,6},{5,7},{6,4},{7,5},{8,10},{9,11},{10,... | collective-permute-start | bytes 884744 | tf_op jit(solution)/shard_map/ppermute | solution.py:857
  345.2 20.0 %collective-permute-start.50 = (bf16[240,768]{1,0:T(8,128)(2,1)S(1)}, bf16[240,768]{1,0:T(8,128)(2,1)S(1)}, u32[]{:S(2)}, u32[]{:S(2)}) collective-permute-start(bf16[240,768]{1,0:T(8,128)(2,1)S(1)} %pad_maximum_fusion.4), channel_id=1, source_target_pairs={{0,2},{1,3},{2,0},{3,1},{4,6},{5,7},{6,4},{7,5},{8,10},{9,11},{10,... | collective-permute-start | bytes 1105928 | tf_op jit(solution)/shard_map/ppermute | solution.py:857
  346.1 21.3 %all-to-all-start.5 = ((bf16[8,32,768]{2,1,0:T(8,128)(2,1)}), bf16[8,32,768]{2,1,0:T(8,128)(2,1)S(1)}, u32[]{:S(2)}, u32[]{:S(2)}) async-start(bf16[8,32,768]{2,1,0:T(8,128)(2,1)} %bitcast.47), calls=%async_computation.5 | async-start | bytes 786432 | tf_op jit(solution)/shard_map/all_to_all | solution.py:969
  350.2 17.3 %collective-permute-start.51 = (bf16[48,768]{1,0:T(8,128)(2,1)S(1)}, bf16[48,768]{1,0:T(8,128)(2,1)S(1)}, u32[]{:S(2)}, u32[]{:S(2)}) collective-permute-start(bf16[48,768]{1,0:T(8,128)(2,1)S(1)} %get-tuple-element.262), channel_id=1, source_target_pairs={{0,4},{1,5},{2,6},{3,7},{4,0},{5,1},{6,2},{7,3},{8,12},{9,13},{10,... | collective-permute-start | bytes 221192 | tf_op jit(solution)/shard_map/ppermute | solution.py:857
  353.3 23.2 %collective-permute-start.56 = (bf16[384,768]{1,0:T(8,128)(2,1)S(1)}, bf16[384,768]{1,0:T(8,128)(2,1)S(1)}, u32[]{:S(2)}, u32[]{:S(2)}) collective-permute-start(bf16[384,768]{1,0:T(8,128)(2,1)S(1)} %pad_maximum_fusion.2), channel_id=1, source_target_pairs={{0,1},{1,0},{2,3},{3,2},{4,5},{5,4},{6,7},{7,6},{8,9},{9,8},{10,11... | collective-permute-start | bytes 1769480 | tf_op jit(solution)/shard_map/ppermute | solution.py:857
  367.5 6.8 %collective-permute-start.52 = (bf16[48,768]{1,0:T(8,128)(2,1)S(1)}, bf16[48,768]{1,0:T(8,128)(2,1)S(1)}, u32[]{:S(2)}, u32[]{:S(2)}) collective-permute-start(bf16[48,768]{1,0:T(8,128)(2,1)S(1)} %add_convert_fusion.16), channel_id=1, source_target_pairs={{0,4},{1,5},{2,6},{3,7},{4,0},{5,1},{6,2},{7,3},{8,12},{9,13},{10,... | collective-permute-start | bytes 221192 | tf_op jit(solution)/shard_map/ppermute | solution.py:857
  368.0 22.6 %collective-permute-start.55 = (bf16[480,768]{1,0:T(8,128)(2,1)S(1)}, bf16[480,768]{1,0:T(8,128)(2,1)S(1)}, u32[]{:S(2)}, u32[]{:S(2)}) collective-permute-start(bf16[480,768]{1,0:T(8,128)(2,1)S(1)} %pad_maximum_fusion.1), channel_id=1, source_target_pairs={{0,1},{1,0},{2,3},{3,2},{4,5},{5,4},{6,7},{7,6},{8,9},{9,8},{10,11... | collective-permute-start | bytes 2211848 | tf_op jit(solution)/shard_map/ppermute | solution.py:857
  368.8 29.0 %all-to-all-start.6 = ((bf16[8,32,768]{2,1,0:T(8,128)(2,1)}), bf16[8,32,768]{2,1,0:T(8,128)(2,1)S(1)}, u32[]{:S(2)}, u32[]{:S(2)}) async-start(bf16[8,32,768]{2,1,0:T(8,128)(2,1)} %broadcast_in_dim.108), calls=%async_computation.6 | async-start | bytes 786432 | tf_op jit(solution)/shard_map/all_to_all | solution.py:976
  374.3 11.2 %collective-permute-start.53 = (bf16[96,768]{1,0:T(8,128)(2,1)S(1)}, bf16[96,768]{1,0:T(8,128)(2,1)S(1)}, u32[]{:S(2)}, u32[]{:S(2)}) collective-permute-start(bf16[96,768]{1,0:T(8,128)(2,1)S(1)} %pad_maximum_fusion.7), channel_id=1, source_target_pairs={{0,2},{1,3},{2,0},{3,1},{4,6},{5,7},{6,4},{7,5},{8,10},{9,11},{10,... | collective-permute-start | bytes 442376 | tf_op jit(solution)/shard_map/ppermute | solution.py:857
  385.6 10.9 %collective-permute-start.54 = (bf16[192,768]{1,0:T(8,128)(2,1)S(1)}, bf16[192,768]{1,0:T(8,128)(2,1)S(1)}, u32[]{:S(2)}, u32[]{:S(2)}) collective-permute-start(bf16[192,768]{1,0:T(8,128)(2,1)S(1)} %pad_maximum_fusion.6), channel_id=1, source_target_pairs={{0,1},{1,0},{2,3},{3,2},{4,5},{5,4},{6,7},{7,6},{8,9},{9,8},{10,11... | collective-permute-start | bytes 884744 | tf_op jit(solution)/shard_map/ppermute | solution.py:857
  (51 other events, 371.8 us)
